TPU v7x, 32 devices: a whole 2x2x4 slice. The times are simulated.
32 devices in a mesh: groups: 2 (over y), vocab: 8 (over z, x), mp: 2 (over core).
Axes of the slice: x: 2, y: 2, z: 4, core: 2. Of those that a mesh axis runs over, the one named last changes fastest.
Arguments:
- gate_pre: bfloat16 [32, 14336], P(('groups', 'vocab'), 'mp'), parts along dimension 0, may hold values from -6 to 6
- up_pre: bfloat16 [32, 14336], P(('groups', 'vocab'), 'mp'), parts along dimension 0, may hold values from -6 to 6
- down_weight: bfloat16 [8192, 14336], P('vocab', 'mp'), may hold values from -0.046875 to 0.046875
- residual: bfloat16 [32, 8192], P(('groups', 'vocab', 'mp')), parts along dimension 0, may hold values from -36 to 36
- norm_gain: bfloat16 [8192], replicated, may hold values from 0.5 to 1.5
- head_weight: bfloat16 [8192, 4032], P('mp', 'vocab')
- targets: int32 [32], P(('groups', 'mp')), parts along dimension 0, may hold values from 0 to 4031
Outputs:
- log_likelihood: float32 [32], P(('groups', 'mp')), parts along dimension 0
There are 2 independent parts, one for each index of `groups`. A program takes and returns all parts, laid end to end along the dimension named above; an argument that names none is the same for every part. Nothing has to cross between parts.
All inputs are finite; a program needn't handle non-finite values.
Results may differ from a plain program's by a relative error of at most 0.0003.
The roundings to bfloat16 on the way count: a program that leaves them out, or rounds other values in their place, can miss the bound.
Values may be sent and summed in bfloat16 or wider, within the bound.
No kernel may reach another device: no remote copies, remote signals or barrier semaphores. Data moves between devices by JAX's collectives and lax.ppermute only.
A program may use at most 64 MiB of HBM per device.

v0:
```python
import jax
import jax.numpy as jnp
from jax import lax
from jax.sharding import PartitionSpec as P

EPSILON = 1e-05


def merged_2(value, axis, combine):
    everything = jax.tree.map(lambda part: lax.all_gather(part, axis), value)
    first = jax.tree.map(lambda part: part[0], everything)

    def turn(k, so_far):
        return combine(so_far, jax.tree.map(lambda part: part[k], everything))

    return lax.fori_loop(1, lax.axis_size(axis), turn, first)


def merge_stats(earlier, follows):
    joint_max = jnp.maximum(earlier[0], follows[0])
    joint_sum = earlier[1] * jnp.exp(earlier[0] - joint_max) + follows[1] * jnp.exp(
        follows[0] - joint_max
    )
    return (joint_max, joint_sum, earlier[2] + follows[2])


def body(gate_pre, up_pre, down_weight, residual, norm_gain, head_weight, targets):
    vocab_count = lax.axis_size("vocab")
    model_count = lax.axis_size("mp")
    model_index = lax.axis_index("mp")
    vocab_index = lax.axis_index("vocab")
    gated_units = (jax.nn.silu(gate_pre.astype(jnp.float32)) * up_pre.astype(jnp.float32)).astype(
        jnp.bfloat16
    )
    down_terms = lax.dot_general(
        lax.all_gather(gated_units, "vocab", axis=0, tiled=True),
        down_weight,
        (((1,), (1,)), ((), ())),
        preferred_element_type=jnp.float32,
    )
    own_rows = residual.shape[0]
    block_cols = down_weight.shape[0]
    grouped = down_terms.reshape(vocab_count, model_count, own_rows, block_cols)
    arrived = lax.all_to_all(
        lax.all_to_all(grouped, "vocab", split_axis=0, concat_axis=3, tiled=True),
        "mp",
        split_axis=1,
        concat_axis=0,
        tiled=True,
    )
    update = jnp.sum(arrived, axis=(0, 1))
    stream = (residual.astype(jnp.float32) + update).astype(jnp.bfloat16)
    stream = lax.optimization_barrier(stream)
    widened = stream.astype(jnp.float32)
    mean_square = jnp.mean(widened * widened, axis=1, keepdims=True)
    normed = (
        widened * lax.rsqrt(mean_square + EPSILON) * norm_gain.astype(jnp.float32)[None, :]
    ).astype(jnp.bfloat16)
    half_width = head_weight.shape[0]
    halves = lax.dynamic_slice_in_dim(
        lax.all_gather(normed, ("vocab", "mp"), axis=0, tiled=True),
        model_index * half_width,
        half_width,
        1,
    )
    logit_terms = jnp.dot(halves, head_weight, preferred_element_type=jnp.float32)
    logits = lax.psum_scatter(logit_terms, "mp", scatter_dimension=0, tiled=True)
    local_ids = targets - vocab_index * logits.shape[1]
    columns = lax.broadcasted_iota(jnp.int32, logits.shape, 1)
    chosen = jnp.sum(jnp.where(columns == local_ids[:, None], logits, 0.0), axis=1)
    row_top = jnp.max(logits, axis=1)
    exp_total = jnp.sum(jnp.exp(logits - row_top[:, None]), axis=1)
    merged = merged_2((row_top, exp_total, chosen), "vocab", merge_stats)
    return merged[2] - merged[0] - jnp.log(merged[1])


def solution(mesh):
    return jax.shard_map(
        body,
        mesh=mesh,
        in_specs=(
            P(("groups", "vocab"), "mp"),
            P(("groups", "vocab"), "mp"),
            P("vocab", "mp"),
            P(("groups", "vocab", "mp"), None),
            P(),
            P("mp", "vocab"),
            P(("groups", "mp")),
        ),
        out_specs=P(("groups", "mp")),
        check_vma=False,
    )
```

profile of v0, /device:TPU:0, one launch (start us, length us, event | category | flops | bytes accessed | tf_op | source)
XLA Modules:
  0.0 128.8 jit_solution(11626139243467973319)
XLA Ops:
  6.5 0.9 fusion.12
  7.4 32.5 %all-gather.3 = bf16[8,2,7168]{2,1,0:T(2,128)(2,1)S(1)} all-gather(bf16[1,2,7168]{2,1,0:T(2,128)(2,1)S(1)} %fusion.12), channel_id=1, replica_groups=mesh['groups'=2,'vocab'=8,'mp'=2] {'vocab'}, dimensions={0}, use_global_device_ids=true | all-gather | bytes 258048 | tf_op jit(solution)/shard_map/all_gather | solution.py:36
  39.9 0.1 reshape.39
  40.0 9.1 %fusion.14 = f32[16,1024]{1,0:T(8,128)S(1)} fusion(bf16[16,7168]{1,0:T(8,128)(2,1)S(1)} %reshape.39, bf16[1024,7168]{1,0:T(8,128)(2,1)} %param.11), kind=kOutput, calls=%fused_computation.28 | convolution fusion | flops 234881024 | bytes 14974976 | tf_op jit(solution)/shard_map/dot_general | solution.py:35
  49.1 0.7 reshape.18
  49.7 5.5 %all-to-all-start = ((f32[8,2,1,1024]{3,1,2,0:T(2,128)}), f32[8,2,1,1024]{3,1,2,0:T(2,128)S(1)}, u32[]{:S(2)}, u32[]{:S(2)}) async-start(f32[8,2,1,1024]{3,1,2,0:T(2,128)} %bitcast.4), calls=%async_computation | async-start | bytes 131072 | tf_op jit(solution)/shard_map/all_to_all | solution.py:45
  55.3 6.8 %all-to-all-done = f32[8,2,1,1024]{3,1,2,0:T(2,128)S(1)} async-done(((f32[8,2,1,1024]{3,1,2,0:T(2,128)}), f32[8,2,1,1024]{3,1,2,0:T(2,128)S(1)}, u32[]{:S(2)}, u32[]{:S(2)}) %all-to-all-start) | async-done | bytes 65568 | tf_op jit(solution)/shard_map/all_to_all | solution.py:45
  62.2 3.8 %all_to_all.27 = f32[1,2,1,8192]{3,2,0,1:T(1,128)S(1)} all-to-all(f32[1,2,1,8192]{3,2,0,1:T(1,128)S(1)} %copy.10), channel_id=1, replica_groups=mesh['groups'=2,'vocab'=8,'mp'=2] {'mp'}, dimensions={1} | all-to-all | bytes 131072 | tf_op jit(solution)/shard_map/all_to_all | solution.py:44
  66.0 0.1 reduce_sum.38
  66.2 0.7 multiply_reduce_fusion
  67.6 19.5 %all-gather.4 = bf16[16,1,8192]{2,1,0:T(2,128)(2,1)S(1)} all-gather(bf16[1,1,8192]{2,1,0:T(2,128)(2,1)S(1)} %convert_bitcast_fusion), channel_id=1, replica_groups=mesh['groups'=2,'vocab'=8,'mp'=2] {'vocab','mp'}, dimensions={0}, use_global_device_ids=true | all-gather | bytes 278528 | tf_op jit(solution)/shard_map/all_gather | solution.py:61
  87.0 0.3 constant_dynamic-slice_fusion.3
  87.3 4.0 %fusion.7 = f32[16,504]{1,0:T(8,128)} fusion(bf16[4096,504]{0,1:T(8,128)(2,1)} %param.14, bf16[16,1,4096]{2,1,0:T(2,128)(2,1)S(1)} %constant_dynamic-slice_fusion.3), kind=kOutput, calls=%fused_computation.11 | convolution fusion | flops 66060288 | bytes 4292096 | tf_op jit(solution)/shard_map/dot_general | solution.py:66
  91.4 0.6 dynamic-slice
  92.7 4.2 %reduce-scatter.2.cloned.1.call-done = f32[8,504]{1,0:T(8,128)} async-done(((f32[16,504]{1,0:T(8,128)}), f32[8,504]{1,0:T(8,128)}) %reduce-scatter.2.cloned.1.call-update) | async-done | bytes 16144 | tf_op jit(solution)/shard_map/reduce_scatter | solution.py:67
  96.8 0.8 reduce_max.9
  97.7 0.2 dynamic-update-slice
  97.9 0.9 select_reduce_fusion
  98.9 0.2 dynamic-update-slice.2
  99.1 0.2 dynamic-update-slice.1
  99.3 21.5 %all-reduce.3 = (f32[64]{0:T(128)S(1)}, f32[64]{0:T(128)S(1)}, f32[64]{0:T(128)S(1)}) all-reduce(f32[64]{0:T(128)S(1)} %dynamic-update-slice, f32[64]{0:T(128)S(1)} %dynamic-update-slice.1, f32[64]{0:T(128)S(1)} %dynamic-update-slice.2), channel_id=2, replica_groups=mesh['groups'=2,'vocab'=8,'mp'=2] {'vocab'}, use_global_device_ids=true, to_apply=%add | all-reduce | flops 192 | bytes 1536
  120.9 0.1 reshape.20
  121.1 0.3 while.19
  121.4 0.5 log_subtract_fusion
  (27 shorter events, 0.6 us)
Async XLA Ops:
  6.5 84.8 %copy-start.3 = (u32[32]{0:T(128)S(1)}, u32[32]{0:T(128)}, u32[]{:S(2)}) copy-start(u32[32]{0:T(128)} %constant.71) | copy-start | bytes 388
  6.5 48.8 %copy-start.1 = (bf16[8192]{0:T(1024)(128)(2,1)S(1)}, bf16[8192]{0:T(1024)(128)(2,1)}, u32[]{:S(2)}) copy-start(bf16[8192]{0:T(1024)(128)(2,1)} %param.13) | copy-start | bytes 49156
  6.5 59.6 %copy-start = (bf16[1,8192]{1,0:T(2,128)(2,1)S(1)}, bf16[1,8192]{1,0:T(2,128)(2,1)}, u32[]{:S(2)}) copy-start(bf16[1,8192]{1,0:T(2,128)(2,1)} %param.12) | copy-start | bytes 49156
  6.5 84.8 %copy-start.2 = (s32[8]{0:T(128)S(1)}, s32[8]{0:T(128)}, u32[]{:S(2)}) copy-start(s32[8]{0:T(128)} %param.15) | copy-start | bytes 100
  49.7 12.4 %all-to-all-start = ((f32[8,2,1,1024]{3,1,2,0:T(2,128)}), f32[8,2,1,1024]{3,1,2,0:T(2,128)S(1)}, u32[]{:S(2)}, u32[]{:S(2)}) async-start(f32[8,2,1,1024]{3,1,2,0:T(2,128)} %bitcast.4), calls=%async_computation | async-start | bytes 131072 | tf_op jit(solution)/shard_map/all_to_all | solution.py:45
  55.2 41.6 %reduce-scatter.2.cloned.1.call-start = ((), (), s32[]{:S(2)}) async-start(), calls=%async_computation.3 | async-start | bytes 49152 | tf_op jit(solution)/shard_map/reduce_scatter | solution.py:67
Sparse Core Ops, SparseCore 0:
  91.4 5.3 reduce-scatter.1
where the time goes:
time: 129 us
  blocking collectives  77.3 us (60%)
  between operations  14.9 us (12%)
  matrix products  13 us (10%)
  waiting for transfers between devices  11 us (9%)
  starting transfers between devices  5.54 us (4%)
  other arithmetic  4.22 us (3%)
  local copies, waits for them, and re-layouts  2.68 us (2%)
    all_gather x1, blocking collectives, body(): lax.all_gather(gated_units, 'vocab', axis=0, tiled=True)  32.5 us
    unnamed x1, blocking collectives  21.5 us
    all_gather x1, blocking collectives, body(): lax.all_gather(normed, ('vocab', 'mp'), axis=0, tiled=True)  19.5 us
    dot_general x1, matrix products, body(): lax.dot_general(lax.all_gather(gated_units, 'vocab', axis=0, tiled=True),...  9.05 us
    all_to_all x1, waiting for transfers between devices, body(): lax.all_to_all(grouped, 'vocab', split_axis=0, concat_axis=3, tiled=True)  6.83 us
    all_to_all x1, starting transfers between devices, body(): lax.all_to_all(grouped, 'vocab', split_axis=0, concat_axis=3, tiled=True)  5.51 us
    reduce_scatter x1, waiting for transfers between devices, body(): lax.psum_scatter(logit_terms, 'mp', scatter_dimension=0, tiled=True)  4.19 us
    dot_general x1, matrix products, body(): jnp.dot(halves, head_weight, preferred_element_type=jnp.float32)  3.98 us
  transfers between devices with their start and end apart: 2, of which 2 were waited for; matrix products, arithmetic and copies ran while one was open for 1% of the time, Pallas kernels for 0%

commit v1 on v0

v1 whole, which is shorter than its diff:
```python
import jax
import jax.numpy as jnp
from jax import lax
from jax.sharding import PartitionSpec as P

EPSILON = 1e-05


def spread(value, axis):
    count = lax.axis_size(axis)
    copies = jnp.broadcast_to(value[None], (count,) + value.shape)
    return lax.all_to_all(copies, axis, 0, 0, tiled=True)


def partner(value):
    return lax.ppermute(value, "mp", [(0, 1), (1, 0)])


def body(gate_pre, up_pre, down_weight, residual, norm_gain, head_weight, targets):
    vocab_count = lax.axis_size("vocab")
    model_index = lax.axis_index("mp")
    vocab_index = lax.axis_index("vocab")
    rows, half_units = gate_pre.shape
    block = down_weight.shape[0]
    own_rows = residual.shape[0]
    tokens = rows * vocab_count
    gated_units = (jax.nn.silu(gate_pre.astype(jnp.float32)) * up_pre.astype(jnp.float32)).astype(
        jnp.bfloat16
    )
    extra = own_rows * block // rows
    blocks = residual.reshape(own_rows, vocab_count, block).transpose(1, 0, 2)
    sent = jnp.concatenate(
        [
            jnp.broadcast_to(gated_units[None], (vocab_count, rows, half_units)),
            blocks.reshape(vocab_count, rows, extra),
        ],
        axis=2,
    )
    arrived = lax.all_to_all(sent, "vocab", 0, 0, tiled=True)
    units = arrived[:, :, :half_units].reshape(tokens, half_units)
    own_residual = arrived[:, :, half_units:].reshape(vocab_count, 1, own_rows, block)
    down_terms = lax.dot_general(
        units, down_weight, (((1,), (1,)), ((), ())), preferred_element_type=jnp.float32
    )
    mine = lax.broadcasted_iota(jnp.int32, (1, rows // own_rows, 1, 1), 1) == model_index
    terms = down_terms.reshape(vocab_count, rows // own_rows, own_rows, block) + jnp.where(
        mine, own_residual.astype(jnp.float32), 0.0
    )
    terms = terms.reshape(tokens, block)
    stream = (terms + partner(terms)).astype(jnp.bfloat16)
    stream = lax.optimization_barrier(stream)
    whole = spread(stream, "vocab")
    widened = whole.astype(jnp.float32)
    width = vocab_count * block
    mean_square = jnp.sum(widened * widened, axis=(0, 2)) / width
    half_width = head_weight.shape[0]
    half_blocks = vocab_count // lax.axis_size("mp")
    here = lax.dynamic_slice_in_dim(whole, model_index * half_blocks, half_blocks, 0)
    gain = lax.dynamic_slice_in_dim(norm_gain, model_index * half_width, half_width, 0)
    normed = (
        here.astype(jnp.float32)
        * lax.rsqrt(mean_square + EPSILON)[None, :, None]
        * gain.astype(jnp.float32).reshape(half_blocks, 1, block)
    ).astype(jnp.bfloat16)
    normed = normed.transpose(1, 0, 2).reshape(tokens, half_width)
    logit_terms = jnp.dot(normed, head_weight, preferred_element_type=jnp.float32)
    half_tokens = targets.shape[0]
    kept = lax.dynamic_slice_in_dim(logit_terms, model_index * half_tokens, half_tokens, 0)
    given = lax.dynamic_slice_in_dim(logit_terms, (1 - model_index) * half_tokens, half_tokens, 0)
    logits = kept + partner(given)
    local_ids = targets - vocab_index * logits.shape[1]
    columns = lax.broadcasted_iota(jnp.int32, logits.shape, 1)
    chosen = jnp.sum(jnp.where(columns == local_ids[:, None], logits, 0.0), axis=1)
    row_top = jnp.max(logits, axis=1)
    exp_total = jnp.sum(jnp.exp(logits - row_top[:, None]), axis=1)
    stats = spread(jnp.stack([row_top, exp_total, chosen]), "vocab")
    top = jnp.max(stats[:, 0], axis=0)
    total = jnp.sum(stats[:, 1] * jnp.exp(stats[:, 0] - top[None]), axis=0)
    return jnp.sum(stats[:, 2], axis=0) - top - jnp.log(total)


def solution(mesh):
    return jax.shard_map(
        body,
        mesh=mesh,
        in_specs=(
            P(("groups", "vocab"), "mp"),
            P(("groups", "vocab"), "mp"),
            P("vocab", "mp"),
            P(("groups", "vocab", "mp"), None),
            P(),
            P("mp", "vocab"),
            P(("groups", "mp")),
        ),
        out_specs=P(("groups", "mp")),
        check_vma=False,
    )
```

time: 129 us -> 59.4 us (0.46)
  blocking collectives: 77.3 us -> 9.92 us
  between operations: 14.9 us -> 0.16 us
  waiting for transfers between devices: 11 us -> 20.4 us
  starting transfers between devices: 5.54 us -> 10.9 us
  local copies, waits for them, and re-layouts: 2.68 us -> 1.18 us
    all_gather x2 -> x0, blocking collectives: 52 us -> none  [the longest x1 32.5 us: body(): lax.all_gather(gated_units, 'vocab', axis=0, tiled=True)]
    unnamed x1 -> x0, blocking collectives: 21.5 us -> none
    all_to_all x1 -> x2, waiting for transfers between devices: 6.83 us -> 18 us  [the longest x1 9.35 us: spread(): return lax.all_to_all(copies, axis, 0, 0, tiled=True)]
    all_to_all x1, blocking collectives: 3.79 us -> 9.92 us  [spread(): return lax.all_to_all(copies, axis, 0, 0, tiled=True)]
    all_to_all x1 -> x2, starting transfers between devices: 5.51 us -> 10.8 us  [the longest x1 7.28 us: body(): arrived = lax.all_to_all(sent, 'vocab', 0, 0, tiled=True)]
    reduce_scatter x1 -> x0, waiting for transfers between devices: 4.19 us -> none  [body(): lax.psum_scatter(logit_terms, 'mp', scatter_dimension=0, tiled=True)]
    ppermute x0 -> x2, waiting for transfers between devices: none -> 2.39 us  [partner(): return lax.ppermute(value, 'mp', [(0, 1), (1, 0)])]
    unnamed x16 -> x5, local copies, waits for them, and re-layouts: 1.44 us -> 0.02 us
  transfers between devices with their start and end apart: 2 -> 4, of which waited for: 2 -> 4; matrix products, arithmetic and copies ran while one was open for 1% -> 0% of each run, Pallas kernels for 0% -> 0%
where the time goes in v1:
time: 59.4 us; the launch traced here: 58.8 us
  waiting for transfers between devices  20.4 us (34%)
  matrix products  12.4 us (21%)
  starting transfers between devices  10.9 us (18%)
  blocking collectives  9.92 us (17%)
  other arithmetic  3.9 us (7%)
  local copies, waits for them, and re-layouts  1.18 us (2%)
    all_to_all x1, blocking collectives, spread(): return lax.all_to_all(copies, axis, 0, 0, tiled=True)  9.92 us
    all_to_all x1, waiting for transfers between devices, spread(): return lax.all_to_all(copies, axis, 0, 0, tiled=True)  9.35 us
    dot_general x1, matrix products, body(): lax.dot_general(units, down_weight, (((1,), (1,)), ((), ())), preferred_e...  9.05 us
    all_to_all x1, waiting for transfers between devices, body(): arrived = lax.all_to_all(sent, 'vocab', 0, 0, tiled=True)  8.67 us
    all_to_all x1, starting transfers between devices, body(): arrived = lax.all_to_all(sent, 'vocab', 0, 0, tiled=True)  7.28 us
    all_to_all x1, starting transfers between devices, spread(): return lax.all_to_all(copies, axis, 0, 0, tiled=True)  3.48 us
    dot_general x1, matrix products, body(): jnp.dot(normed, head_weight, preferred_element_type=jnp.float32)  3.33 us
    ppermute x2, waiting for transfers between devices, partner(): return lax.ppermute(value, 'mp', [(0, 1), (1, 0)])  2.39 us
  transfers between devices with their start and end apart: 4, of which 4 were waited for; matrix products, arithmetic and copies ran while one was open for 0% of the time, Pallas kernels for 0%

profile of v1, /device:TPU:0, one launch (start us, length us, event | category | flops | bytes accessed | tf_op | source)
XLA Modules:
  0.0 58.8 jit_solution(9855059927982875965)
XLA Ops:
  0.0 0.9 %reduce.2 = bf16[8192]{0:T(1024)(128)(2,1)S(1)} reduce(bf16[1,8192]{1,0:T(2,128)(2,1)} %param.10, bf16[]{:T(256)} %constant.39), dimensions={0}, to_apply=%param.10.reduce_sub_computation | reduce | bytes 32770 | tf_op args[3]
  0.9 0.8 %fusion.10 = bf16[2,7168]{1,0:T(2,128)(2,1)S(1)} fusion(bf16[2,7168]{1,0:T(2,128)(2,1)} %param.8, bf16[2,7168]{1,0:T(2,128)(2,1)} %param.7), kind=kLoop, calls=%fused_computation.14 | loop fusion | flops 114688 | bytes 86016 | tf_op jit(solution)/shard_map/convert_element_type | solution.py:27
  1.7 0.1 broadcast_in_dim.30
  1.9 0.0 copy-start.1
  1.9 0.9 %pad_maximum_fusion = bf16[8,2,7680]{2,1,0:T(2,128)(2,1)} fusion(bf16[8,2,512]{2,1,0:T(2,128)(2,1)S(1)} %reshape_transpose_reshape.3, bf16[8,2,7168]{2,1,0:T(2,128)(2,1)S(1)} %broadcast_in_dim.30), kind=kLoop, calls=%fused_computation.5 | loop fusion | flops 491520 | bytes 491520 | tf_op jit(solution)/shard_map/concatenate | solution.py:32
  2.8 7.3 %all-to-all-start = ((bf16[8,2,7680]{2,1,0:T(2,128)(2,1)}), bf16[8,2,7680]{2,1,0:T(2,128)(2,1)S(1)}, u32[]{:S(2)}, u32[]{:S(2)}) async-start(bf16[8,2,7680]{2,1,0:T(2,128)(2,1)} %pad_maximum_fusion), calls=%async_computation | async-start | bytes 491520 | tf_op jit(solution)/shard_map/all_to_all | solution.py:39
  10.1 8.7 %all-to-all-done = bf16[8,2,7680]{2,1,0:T(2,128)(2,1)S(1)} async-done(((bf16[8,2,7680]{2,1,0:T(2,128)(2,1)}), bf16[8,2,7680]{2,1,0:T(2,128)(2,1)S(1)}, u32[]{:S(2)}, u32[]{:S(2)}) %all-to-all-start) | async-done | bytes 245792 | tf_op jit(solution)/shard_map/all_to_all | solution.py:39
  18.8 0.2 slice.21
  18.9 9.1 %fusion.2 = f32[8,2,1024]{2,0,1:T(8,128)S(1)} fusion(bf16[1024,7168]{1,0:T(8,128)(2,1)} %param.9, bf16[8,2,7168]{2,1,0:T(2,128)(2,1)S(1)} %slice.21, f32[8,1024]{1,0:T(8,128)S(1)} %bitcast.24, pred[2]{0:T(512)(128)(4,1)S(1)} %iota_compare_fusion.1), kind=kOutput, calls=%fused_computation.2 | convolution fusion | flops 234913792 | bytes 15007746 | tf_op jit(solution)/shard_map/dot_general | solution.py:42
  28.0 0.1 copy.11
  28.1 0.1 collective-permute-start
  28.2 1.2 %collective-permute-done = f32[16,1024]{1,0:T(8,128)S(1)} collective-permute-done((f32[16,1024]{1,0:T(8,128)S(1)}, f32[16,1024]{1,0:T(8,128)S(1)}, u32[]{:S(2)}, u32[]{:S(2)}) %collective-permute-start) | collective-permute-done | bytes 65568 | tf_op jit(solution)/shard_map/ppermute | solution.py:16
  29.4 0.7 %broadcast_in_dim.50 = bf16[8,16,1024]{2,1,0:T(8,128)(2,1)} broadcast(bf16[16,1024]{1,0:T(8,128)(2,1)S(1)} %add_convert_fusion), dimensions={1,2} | broadcast | bytes 294912 | tf_op jit(solution)/shard_map/broadcast_in_dim | solution.py:11
  30.2 3.5 %all-to-all-start.1 = ((bf16[8,16,1024]{2,1,0:T(8,128)(2,1)}), bf16[8,16,1024]{2,1,0:T(8,128)(2,1)S(1)}, u32[]{:S(2)}, u32[]{:S(2)}) async-start(bf16[8,16,1024]{2,1,0:T(8,128)(2,1)} %broadcast_in_dim.50), calls=%async_computation.1 | async-start | bytes 524288 | tf_op jit(solution)/shard_map/all_to_all | solution.py:12
  33.7 9.3 %all-to-all-done.1 = bf16[8,16,1024]{2,1,0:T(8,128)(2,1)S(1)} async-done(((bf16[8,16,1024]{2,1,0:T(8,128)(2,1)}), bf16[8,16,1024]{2,1,0:T(8,128)(2,1)S(1)}, u32[]{:S(2)}, u32[]{:S(2)}) %all-to-all-start.1) | async-done | bytes 262176 | tf_op jit(solution)/shard_map/all_to_all | solution.py:12
  43.0 0.2 multiply_reduce_fusion
  43.2 0.1 fusion.6
  43.4 3.3 %fusion.12 = f32[16,504]{1,0:T(8,128)S(1)} fusion(bf16[16,4096]{1,0:T(8,128)(2,1)S(1)} %bitcast.23, bf16[4096,504]{0,1:T(8,128)(2,1)} %param.12), kind=kOutput, calls=%fused_computation.30 | convolution fusion | flops 66060288 | bytes 4292096 | tf_op jit(solution)/shard_map/dot_general | solution.py:66
  46.7 0.0 collective-permute-start.1
  46.8 1.1 %collective-permute-done.1 = f32[8,504]{1,0:T(8,128)S(1)} collective-permute-done((f32[8,504]{1,0:T(8,128)S(1)}, f32[8,504]{1,0:T(8,128)S(1)}, u32[]{:S(2)}, u32[]{:S(2)}) %collective-permute-start.1) | collective-permute-done | bytes 16160 | tf_op jit(solution)/shard_map/ppermute | solution.py:16
  47.9 0.1 fusion.11
  48.0 0.2 exponential_reduce_fusion
  48.3 9.9 %all_to_all.15 = f32[8,3,8]{2,1,0:T(4,128)S(1)} all-to-all(f32[8,3,8]{2,1,0:T(4,128)S(1)} %broadcast_in_dim.52), channel_id=1, replica_groups=mesh['groups'=2,'vocab'=8,'mp'=2] {'vocab'}, dimensions={0} | all-to-all | bytes 1536 | tf_op jit(solution)/shard_map/all_to_all | solution.py:12
  58.3 0.5 log_subtract_fusion
  (20 shorter events, 0.2 us)
Async XLA Ops:
  0.0 33.6 %copy-start = (bf16[8192]{0:T(1024)(128)(2,1)S(1)}, bf16[8192]{0:T(1024)(128)(2,1)}, u32[]{:S(2)}) copy-start(bf16[8192]{0:T(1024)(128)(2,1)} %param.11) | copy-start | bytes 49156
  1.9 44.9 %copy-start.1 = (s32[8]{0:T(128)S(1)}, s32[8]{0:T(128)}, u32[]{:S(2)}) copy-start(s32[8]{0:T(128)} %param.13) | copy-start | bytes 100
  2.8 16.0 %all-to-all-start = ((bf16[8,2,7680]{2,1,0:T(2,128)(2,1)}), bf16[8,2,7680]{2,1,0:T(2,128)(2,1)S(1)}, u32[]{:S(2)}, u32[]{:S(2)}) async-start(bf16[8,2,7680]{2,1,0:T(2,128)(2,1)} %pad_maximum_fusion), calls=%async_computation | async-start | bytes 491520 | tf_op jit(solution)/shard_map/all_to_all | solution.py:39
  28.1 1.3 %collective-permute-start = (f32[16,1024]{1,0:T(8,128)S(1)}, f32[16,1024]{1,0:T(8,128)S(1)}, u32[]{:S(2)}, u32[]{:S(2)}) collective-permute-start(f32[16,1024]{1,0:T(8,128)S(1)} %reshape.46), channel_id=1, source_target_pairs={{0,1},{1,0},{2,3},{3,2},{4,5},{5,4},{6,7},{7,6},{8,9},{9,8},{10,11... | collective-permute-start | bytes 196616 | tf_op jit(solution)/shard_map/ppermute | solution.py:16
  30.2 12.9 %all-to-all-start.1 = ((bf16[8,16,1024]{2,1,0:T(8,128)(2,1)}), bf16[8,16,1024]{2,1,0:T(8,128)(2,1)S(1)}, u32[]{:S(2)}, u32[]{:S(2)}) async-start(bf16[8,16,1024]{2,1,0:T(8,128)(2,1)} %broadcast_in_dim.50), calls=%async_computation.1 | async-start | bytes 524288 | tf_op jit(solution)/shard_map/all_to_all | solution.py:12
  46.7 1.2 %collective-permute-start.1 = (f32[8,504]{1,0:T(8,128)S(1)}, f32[8,504]{1,0:T(8,128)S(1)}, u32[]{:S(2)}, u32[]{:S(2)}) collective-permute-start(f32[8,504]{1,0:T(8,128)S(1)} %constant_dynamic-slice_fusion), channel_id=1, source_target_pairs={{0,1},{1,0},{2,3},{3,2},{4,5},{5,4},{6,7},{7,6},{8,9},{9,8},{10,11... | collective-permute-start | bytes 48392 | tf_op jit(solution)/shard_map/ppermute | solution.py:16

commit v2 on v1

v2 whole, which is shorter than its diff:
```python
import jax
import jax.numpy as jnp
from jax import lax
from jax.experimental import pallas as pl
from jax.experimental.pallas import tpu as pltpu
from jax.sharding import PartitionSpec as P

EPSILON = 1e-05
ROWS_BY_ROWS = (((1,), (1,)), ((), ()))
SMALL = 2 << 20
fence = lax.optimization_barrier
NEAR = pl.BlockSpec(memory_space=pltpu.VMEM)
FAR = pl.BlockSpec(memory_space=pltpu.HBM)
VECTOR = pltpu.VMEM
DMA = pltpu.SemaphoreType.DMA


def partner(value):
    return lax.ppermute(value, "mp", [(0, 1), (1, 0)])


def swapped(value):
    return fence(lax.all_to_all(fence(value), "vocab", 0, 0, tiled=True))


def call(kernel, out_shape, operands, places, scratch=(), grant=SMALL):
    operands = tuple(
        pltpu.with_memory_space_constraint(one, pltpu.HBM) if place is FAR else one
        for one, place in zip(operands, places)
    )
    return pl.pallas_call(
        kernel,
        out_shape=out_shape,
        in_specs=places,
        out_specs=jax.tree.map(lambda _: NEAR, out_shape),
        scratch_shapes=list(scratch),
        compiler_params=pltpu.CompilerParams(vmem_limit_bytes=grant),
    )(*operands)


def pieces(length, most, step):
    for count in range(pl.cdiv(length, most), length + 1):
        if length % count == 0 and (length // count) % step == 0:
            return count
    return 1


def gated_kernel(gate_hbm, up_hbm, residual_hbm, out_ref, gate_ref, up_ref, residual_ref, done):
    loads = (
        pltpu.make_async_copy(gate_hbm, gate_ref, done.at[0]),
        pltpu.make_async_copy(up_hbm, up_ref, done.at[1]),
        pltpu.make_async_copy(residual_hbm, residual_ref, done.at[2]),
    )
    for load in loads:
        load.start()
    for load in loads:
        load.wait()
    count, rows, width = out_ref.shape
    units = gate_ref.shape[1]
    block = width - units
    gate = gate_ref[...].astype(jnp.float32)
    up = up_ref[...].astype(jnp.float32)
    gated = (gate / (1.0 + jnp.exp(-gate)) * up).astype(jnp.bfloat16)
    token = lax.broadcasted_iota(jnp.int32, (rows, block), 0)
    first = lax.axis_index("mp") * residual_ref.shape[0]
    for peer in range(count):
        out_ref[peer, :, :units] = gated
        tail = jnp.zeros((rows, block), jnp.float32)
        for row in range(residual_ref.shape[0]):
            here = residual_ref[row : row + 1, peer * block : (peer + 1) * block]
            here = jnp.broadcast_to(here.astype(jnp.float32), (rows, block))
            tail = jnp.where(token == first + row, here, tail)
        out_ref[peer, :, units:] = tail.astype(jnp.bfloat16)


def weight_loads(weight_hbm, weight_ref, done, row_parts, unit_parts):
    rows, units = weight_ref.shape[0] // row_parts, weight_ref.shape[1] // unit_parts
    loads = {}
    for i in range(row_parts):
        for j in range(unit_parts):
            here = (pl.ds(i * rows, rows), pl.ds(j * units, units))
            loads[i, j] = pltpu.make_async_copy(
                weight_hbm.at[here], weight_ref.at[here], done.at[i, j]
            )
            loads[i, j].start()
    return loads, rows, units


def down_kernel(parts, chunks_ref, weight_hbm, kept_ref, given_ref, weight_ref, units_ref, done):
    loads, block, depth = weight_loads(weight_hbm, weight_ref, done, *parts)
    count, rows, width = chunks_ref.shape
    units = weight_ref.shape[1]
    half = kept_ref.shape[0]
    for peer in range(count):
        units_ref[peer * rows : (peer + 1) * rows, :] = chunks_ref[peer]
    is_low = lax.axis_index("mp") == 0
    for i in range(parts[0]):
        here = slice(i * block, (i + 1) * block)
        terms = units_ref[:, units + i * block : units + (i + 1) * block].astype(jnp.float32)
        for j in range(parts[1]):
            loads[i, j].wait()
            deep = slice(j * depth, (j + 1) * depth)
            terms += lax.dot_general(
                units_ref[:, deep],
                weight_ref[here, deep],
                ROWS_BY_ROWS,
                preferred_element_type=jnp.float32,
            )
        low, high = terms[:half], terms[half:]
        kept_ref[:, here] = jnp.where(is_low, low, high)
        given_ref[:, here] = jnp.where(is_low, high, low)


def stream_kernel(kept_ref, arrived_ref, out_ref):
    stream = (kept_ref[...] + arrived_ref[...]).astype(jnp.bfloat16)
    for peer in range(out_ref.shape[0]):
        out_ref[peer] = stream


def norm_kernel(stream_ref, gain_ref, own_ref, other_ref):
    count, tokens, block = stream_ref.shape
    half = count // 2
    squares = jnp.zeros((tokens, block), jnp.float32)
    for part in range(count):
        values = stream_ref[part].astype(jnp.float32)
        squares += values * values
    mean_square = jnp.sum(squares, axis=1, keepdims=True) / (count * block)
    scale = lax.rsqrt(mean_square + EPSILON)
    index = lax.axis_index("mp")
    for out_ref, side in ((own_ref, index), (other_ref, 1 - index)):
        for part in range(half):
            at = side * half + part
            gain = gain_ref[pl.ds(at, 1), :]
            values = stream_ref[at].astype(jnp.float32) * scale * gain
            out_ref[:, part * block : (part + 1) * block] = values.astype(jnp.bfloat16)


def head_kernel(parts, own_ref, other_ref, weight_hbm, kept_ref, given_ref, weight_ref, done):
    loads, block, depth = weight_loads(weight_hbm, weight_ref, done, *parts)
    tokens = own_ref.shape[0]
    terms = jnp.zeros((2 * tokens, block), jnp.float32)
    for j in range(parts[1]):
        loads[0, j].wait()
        deep = slice(j * depth, (j + 1) * depth)
        terms += lax.dot_general(
            jnp.concatenate([own_ref[:, deep], other_ref[:, deep]], axis=0),
            weight_ref[:, deep],
            ROWS_BY_ROWS,
            preferred_element_type=jnp.float32,
        )
    kept_ref[...] = terms[:tokens]
    given_ref[...] = terms[tokens:]


def body(gate_pre, up_pre, down_weight, residual, norm_gain, head_weight, targets):
    vocab_count = lax.axis_size("vocab")
    vocab_index = lax.axis_index("vocab")
    rows, half_units = gate_pre.shape
    block = down_weight.shape[0]
    tokens = rows * vocab_count
    half_tokens = targets.shape[0]
    half_width, columns_here = head_weight.shape
    shaped = jax.ShapeDtypeStruct
    chunk = shaped((vocab_count, rows, half_units + block), jnp.bfloat16)
    operands = (gate_pre, up_pre, residual)
    places = [VECTOR(one.shape, one.dtype) for one in operands]
    chunks = swapped(call(gated_kernel, chunk, operands, [FAR] * 3, places + [DMA((3,))]))
    part = shaped((half_tokens, block), jnp.float32)
    parts = (pieces(block, 256, 8), pieces(half_units, 1792, 128))
    kept, given = call(
        lambda *refs: down_kernel(parts, *refs),
        (part, part),
        (chunks, down_weight),
        [NEAR, FAR],
        [
            VECTOR(down_weight.shape, jnp.bfloat16),
            VECTOR((tokens, half_units + block), jnp.bfloat16),
            DMA(parts),
        ],
        24 << 20,
    )
    chunk = shaped((vocab_count, half_tokens, block), jnp.bfloat16)
    gain = norm_gain.astype(jnp.float32).reshape(vocab_count, block)
    arrived, gain = fence((partner(given), gain))
    stream = swapped(call(stream_kernel, chunk, (kept, arrived), [NEAR] * 2))
    part = shaped((half_tokens, half_width), jnp.bfloat16)
    own, other = call(norm_kernel, (part, part), (stream, gain), [NEAR] * 2)
    part = shaped((half_tokens, columns_here), jnp.float32)
    parts_head = (1, pieces(half_width, 1024, 128))
    kept, given = call(
        lambda *refs: head_kernel(parts_head, *refs),
        (part, part),
        (own, partner(other), head_weight.T),
        [NEAR, NEAR, FAR],
        [VECTOR((columns_here, half_width), jnp.bfloat16), DMA(parts_head)],
        12 << 20,
    )
    logits = kept + partner(given)
    local_ids = targets - vocab_index * columns_here
    columns = lax.broadcasted_iota(jnp.int32, logits.shape, 1)
    chosen = jnp.sum(jnp.where(columns == local_ids[:, None], logits, 0.0), axis=1)
    row_top = jnp.max(logits, axis=1)
    exp_total = jnp.sum(jnp.exp(logits - row_top[:, None]), axis=1)
    stats = jnp.stack([row_top, exp_total, chosen])
    stats = swapped(jnp.broadcast_to(stats[None], (vocab_count,) + stats.shape))
    top = jnp.max(stats[:, 0], axis=0)
    total = jnp.sum(stats[:, 1] * jnp.exp(stats[:, 0] - top[None]), axis=0)
    return jnp.sum(stats[:, 2], axis=0) - top - jnp.log(total)


def solution(mesh):
    return jax.shard_map(
        body,
        mesh=mesh,
        in_specs=(
            P(("groups", "vocab"), "mp"),
            P(("groups", "vocab"), "mp"),
            P("vocab", "mp"),
            P(("groups", "vocab", "mp"), None),
            P(),
            P("mp", "vocab"),
            P(("groups", "mp")),
        ),
        out_specs=P(("groups", "mp")),
        check_vma=False,
    )
```

time: 59.4 us -> 54.2 us (0.912)
  blocking collectives: 9.92 us -> 35.8 us
  waiting for transfers between devices: 20.4 us -> 3.42 us
  Pallas kernels: 0 us -> 13.2 us
  matrix products: 12.4 us -> 0 us
  starting transfers between devices: 10.9 us -> 0.36 us
  other arithmetic: 3.9 us -> 0.95 us
  local copies, waits for them, and re-layouts: 1.18 us -> 0.03 us
    all_to_all x1 -> x3, blocking collectives: 9.92 us -> 35.8 us  [swapped(): return fence(lax.all_to_all(fence(value), 'vocab', 0, 0, tiled=True))]
    all_to_all x2 -> x0, waiting for transfers between devices: 18 us -> none  [the longest x1 9.35 us: spread(): return lax.all_to_all(copies, axis, 0, 0, tiled=True)]
    pallas_call x0 -> x5, Pallas kernels: none -> 13.2 us  [call(): pl.pallas_call(kernel, out_shape=out_shape, in_specs=places, out_specs=ja...]
    dot_general x2 -> x0, matrix products: 12.4 us -> none  [the longest x1 9.05 us: body(): lax.dot_general(units, down_weight, (((1,), (1,)), ((), ())), preferred_e...]
    all_to_all x2 -> x0, starting transfers between devices: 10.8 us -> none  [the longest x1 7.28 us: body(): arrived = lax.all_to_all(sent, 'vocab', 0, 0, tiled=True)]
    ppermute x2 -> x3, waiting for transfers between devices: 2.39 us -> 3.42 us  [partner(): return lax.ppermute(value, 'mp', [(0, 1), (1, 0)])]
    unnamed x3 -> x0, other arithmetic: 0.97 us -> none
    concatenate x1 -> x0, other arithmetic: 0.9 us -> none  [body(): jnp.concatenate([jnp.broadcast_to(gated_units[None], (vocab_count, rows,...]
  transfers between devices with their start and end apart: 4 -> 3, of which waited for: 4 -> 3; matrix products, arithmetic and copies ran while one was open for 0% -> 0% of each run, Pallas kernels for 0% -> 0%
where the time goes in v2:
time: 54.2 us; the launch traced here: 53.9 us
  blocking collectives  35.8 us (66%)
  Pallas kernels  13.2 us (24%)
  waiting for transfers between devices  3.42 us (6%)
  other arithmetic  0.95 us (2%)
    all_to_all x3, blocking collectives, swapped(): return fence(lax.all_to_all(fence(value), 'vocab', 0, 0, tiled=True))  35.8 us
    pallas_call x5, Pallas kernels, call(): pl.pallas_call(kernel, out_shape=out_shape, in_specs=places, out_specs=ja...  13.2 us
    ppermute x3, waiting for transfers between devices, partner(): return lax.ppermute(value, 'mp', [(0, 1), (1, 0)])  3.42 us
  transfers between devices with their start and end apart: 3, of which 3 were waited for; matrix products, arithmetic and copies ran while one was open for 0% of the time, Pallas kernels for 0%

profile of v2, /device:TPU:0, one launch (start us, length us, event | category | flops | bytes accessed | tf_op | source)
XLA Modules:
  0.0 53.9 jit_solution(12443050968670162549)
XLA Ops:
  0.0 0.0 copy-start
  0.0 0.0 copy-start.1
  0.0 0.9 %shard_map.73 = bf16[8,2,8192]{2,1,0:T(2,128)(2,1)S(1)} custom-call(bf16[2,7168]{1,0:T(2,128)(2,1)} %gate_hbm.1, bf16[2,7168]{1,0:T(2,128)(2,1)} %up_hbm.1, bf16[1,8192]{1,0:T(2,128)(2,1)} %residual_hbm.1), custom_call_target="tpu_custom_call" | custom-call | tf_op jit(solution)/shard_map/pallas_call | solution.py:31
  0.9 16.0 %all_to_all.15.refs_0_ = bf16[8,2,8192]{2,1,0:T(2,128)(2,1)S(1)} all-to-all(bf16[8,2,8192]{2,1,0:T(2,128)(2,1)S(1)} %shard_map.73), channel_id=1, replica_groups=mesh['groups'=2,'vocab'=8,'mp'=2] {'vocab'}, dimensions={0} | all-to-all | bytes 524288 | tf_op jit(solution)/shard_map/all_to_all | solution.py:23
  16.9 9.4 %shard_map.74 = (f32[8,1024]{1,0:T(8,128)S(1)}, f32[8,1024]{1,0:T(8,128)S(1)}) custom-call(bf16[8,2,8192]{2,1,0:T(2,128)(2,1)S(1)} %all_to_all.15.refs_0_, bf16[1024,7168]{1,0:T(8,128)(2,1)} %refs_1_.1), custom_call_target="tpu_custom_call" | custom-call | tf_op jit(solution)/shard_map/pallas_call | solution.py:31
  26.3 0.1 collective-permute-start
  26.4 0.0 copy-done
  26.4 1.2 %collective-permute-done.arrived_ref = f32[8,1024]{1,0:T(8,128)S(1)} collective-permute-done((f32[8,1024]{1,0:T(8,128)S(1)}, f32[8,1024]{1,0:T(8,128)S(1)}, u32[]{:S(2)}, u32[]{:S(2)}) %collective-permute-start) | collective-permute-done | bytes 32800 | tf_op jit(solution)/shard_map/ppermute | solution.py:19
  27.6 10.7 %all_to_all.16.stream_ref = bf16[8,8,1024]{2,1,0:T(8,128)(2,1)S(1)} all-to-all(bf16[8,8,1024]{2,1,0:T(8,128)(2,1)S(1)} %shard_map.75), channel_id=1, replica_groups=mesh['groups'=2,'vocab'=8,'mp'=2] {'vocab'}, dimensions={0} | all-to-all | bytes 262144 | tf_op jit(solution)/shard_map/all_to_all | solution.py:23
  38.4 0.1 shard_map.76
  38.5 0.1 collective-permute-start.1
  38.6 1.2 %collective-permute-done.1.refs_1_ = bf16[8,4096]{1,0:T(8,128)(2,1)S(1)} collective-permute-done((bf16[8,4096]{1,0:T(8,128)(2,1)S(1)}, bf16[8,4096]{1,0:T(8,128)(2,1)S(1)}, u32[]{:S(2)}, u32[]{:S(2)}) %collective-permute-start.1) | collective-permute-done | bytes 65568 | tf_op jit(solution)/shard_map/ppermute | solution.py:19
  39.8 2.8 %shard_map.77 = (f32[8,504]{1,0:T(8,128)S(1)}, f32[8,504]{1,0:T(8,128)S(1)}) custom-call(bf16[8,4096]{1,0:T(8,128)(2,1)S(1)} %get-tuple-element.17.refs_0_, bf16[8,4096]{1,0:T(8,128)(2,1)S(1)} %collective-permute-done.1.refs_1_, bf16[504,4096]{1,0:T(8,128)(2,1)} %bitcast.10), custom_call_target="tpu_custom_call" | custom-call | tf_op jit(solution)/shard_map/pallas_call | solution.py:31
  42.6 0.2 collective-permute-start.2
  42.8 0.0 copy-done.1
  42.8 1.0 %collective-permute-done.2 = f32[8,504]{1,0:T(8,128)S(1)} collective-permute-done((f32[8,504]{1,0:T(8,128)S(1)}, f32[8,504]{1,0:T(8,128)S(1)}, u32[]{:S(2)}, u32[]{:S(2)}) %collective-permute-start.2) | collective-permute-done | bytes 16160 | tf_op jit(solution)/shard_map/ppermute | solution.py:19
  43.8 0.1 fusion
  44.0 0.2 exponential_reduce_fusion
  44.2 9.1 %all_to_all.17 = f32[8,3,8]{2,1,0:T(4,128)S(1)} all-to-all(f32[8,3,8]{2,1,0:T(4,128)S(1)} %broadcast_in_dim.7), channel_id=1, replica_groups=mesh['groups'=2,'vocab'=8,'mp'=2] {'vocab'}, dimensions={0} | all-to-all | bytes 1536 | tf_op jit(solution)/shard_map/all_to_all | solution.py:23
  53.3 0.5 log_subtract_fusion
  (8 shorter events, 0.1 us)
Async XLA Ops:
  0.0 26.4 %copy-start = (bf16[8192]{0:T(1024)(128)(2,1)S(1)}, bf16[8192]{0:T(1024)(128)(2,1)}, u32[]{:S(2)}) copy-start(bf16[8192]{0:T(1024)(128)(2,1)} %param.11) | copy-start | bytes 49156
  0.0 42.8 %copy-start.1 = (s32[8]{0:T(128)S(1)}, s32[8]{0:T(128)}, u32[]{:S(2)}) copy-start(s32[8]{0:T(128)} %param.13) | copy-start | bytes 100
  26.3 1.3 %collective-permute-start = (f32[8,1024]{1,0:T(8,128)S(1)}, f32[8,1024]{1,0:T(8,128)S(1)}, u32[]{:S(2)}, u32[]{:S(2)}) collective-permute-start(f32[8,1024]{1,0:T(8,128)S(1)} %get-tuple-element.14), channel_id=1, source_target_pairs={{0,1},{1,0},{2,3},{3,2},{4,5},{5,4},{6,7},{7,6},{8,9},{9,8},{10,11... | collective-permute-start | bytes 98312 | tf_op jit(solution)/shard_map/ppermute | solution.py:19
  38.5 1.3 %collective-permute-start.1 = (bf16[8,4096]{1,0:T(8,128)(2,1)S(1)}, bf16[8,4096]{1,0:T(8,128)(2,1)S(1)}, u32[]{:S(2)}, u32[]{:S(2)}) collective-permute-start(bf16[8,4096]{1,0:T(8,128)(2,1)S(1)} %get-tuple-element.18), channel_id=1, source_target_pairs={{0,1},{1,0},{2,3},{3,2},{4,5},{5,4},{6,7},{7,6},{8,9},{9,8},{10,11... | collective-permute-start | bytes 196616 | tf_op jit(solution)/shard_map/ppermute | solution.py:19
  42.6 1.2 %collective-permute-start.2 = (f32[8,504]{1,0:T(8,128)S(1)}, f32[8,504]{1,0:T(8,128)S(1)}, u32[]{:S(2)}, u32[]{:S(2)}) collective-permute-start(f32[8,504]{1,0:T(8,128)S(1)} %get-tuple-element.20), channel_id=1, source_target_pairs={{0,1},{1,0},{2,3},{3,2},{4,5},{5,4},{6,7},{7,6},{8,9},{9,8},{10,11... | collective-permute-start | bytes 48392 | tf_op jit(solution)/shard_map/ppermute | solution.py:19

commit v3 on v2

--- a/solution.py
+++ b/solution.py
@@ -8,11 +8,17 @@
 EPSILON = 1e-05
 ROWS_BY_ROWS = (((1,), (1,)), ((), ()))
 SMALL = 2 << 20
+GRANT = 8 << 20
 fence = lax.optimization_barrier
 NEAR = pl.BlockSpec(memory_space=pltpu.VMEM)
 FAR = pl.BlockSpec(memory_space=pltpu.HBM)
 VECTOR = pltpu.VMEM
 DMA = pltpu.SemaphoreType.DMA
+
+
+def brought(weight):
+    own = [(k, k) for k in range(lax.axis_size("mp"))]
+    return pltpu.with_memory_space_constraint(lax.ppermute(weight, "mp", own), pltpu.VMEM)
 
 
 def partner(value):
@@ -73,42 +79,19 @@
         out_ref[peer, :, units:] = tail.astype(jnp.bfloat16)
 
 
-def weight_loads(weight_hbm, weight_ref, done, row_parts, unit_parts):
-    rows, units = weight_ref.shape[0] // row_parts, weight_ref.shape[1] // unit_parts
-    loads = {}
-    for i in range(row_parts):
-        for j in range(unit_parts):
-            here = (pl.ds(i * rows, rows), pl.ds(j * units, units))
-            loads[i, j] = pltpu.make_async_copy(
-                weight_hbm.at[here], weight_ref.at[here], done.at[i, j]
-            )
-            loads[i, j].start()
-    return loads, rows, units
-
-
-def down_kernel(parts, chunks_ref, weight_hbm, kept_ref, given_ref, weight_ref, units_ref, done):
-    loads, block, depth = weight_loads(weight_hbm, weight_ref, done, *parts)
+def down_kernel(chunks_ref, weight_ref, kept_ref, given_ref, units_ref):
     count, rows, width = chunks_ref.shape
     units = weight_ref.shape[1]
     half = kept_ref.shape[0]
     for peer in range(count):
         units_ref[peer * rows : (peer + 1) * rows, :] = chunks_ref[peer]
+    terms = lax.dot_general(
+        units_ref[:, :units], weight_ref[...], ROWS_BY_ROWS, preferred_element_type=jnp.float32
+    ) + units_ref[:, units:].astype(jnp.float32)
+    low, high = terms[:half], terms[half:]
     is_low = lax.axis_index("mp") == 0
-    for i in range(parts[0]):
-        here = slice(i * block, (i + 1) * block)
-        terms = units_ref[:, units + i * block : units + (i + 1) * block].astype(jnp.float32)
-        for j in range(parts[1]):
-            loads[i, j].wait()
-            deep = slice(j * depth, (j + 1) * depth)
-            terms += lax.dot_general(
-                units_ref[:, deep],
-                weight_ref[here, deep],
-                ROWS_BY_ROWS,
-                preferred_element_type=jnp.float32,
-            )
-        low, high = terms[:half], terms[half:]
-        kept_ref[:, here] = jnp.where(is_low, low, high)
-        given_ref[:, here] = jnp.where(is_low, high, low)
+    kept_ref[...] = jnp.where(is_low, low, high)
+    given_ref[...] = jnp.where(is_low, high, low)
 
 
 def stream_kernel(kept_ref, arrived_ref, out_ref):
@@ -135,6 +118,19 @@
             out_ref[:, part * block : (part + 1) * block] = values.astype(jnp.bfloat16)
 
 
+def weight_loads(weight_hbm, weight_ref, done, row_parts, unit_parts):
+    rows, units = weight_ref.shape[0] // row_parts, weight_ref.shape[1] // unit_parts
+    loads = {}
+    for i in range(row_parts):
+        for j in range(unit_parts):
+            here = (pl.ds(i * rows, rows), pl.ds(j * units, units))
+            loads[i, j] = pltpu.make_async_copy(
+                weight_hbm.at[here], weight_ref.at[here], done.at[i, j]
+            )
+            loads[i, j].start()
+    return loads, rows, units
+
+
 def head_kernel(parts, own_ref, other_ref, weight_hbm, kept_ref, given_ref, weight_ref, done):
     loads, block, depth = weight_loads(weight_hbm, weight_ref, done, *parts)
     tokens = own_ref.shape[0]
@@ -161,23 +157,19 @@
     half_tokens = targets.shape[0]
     half_width, columns_here = head_weight.shape
     shaped = jax.ShapeDtypeStruct
+    down_rows = brought(down_weight)
     chunk = shaped((vocab_count, rows, half_units + block), jnp.bfloat16)
     operands = (gate_pre, up_pre, residual)
     places = [VECTOR(one.shape, one.dtype) for one in operands]
     chunks = swapped(call(gated_kernel, chunk, operands, [FAR] * 3, places + [DMA((3,))]))
     part = shaped((half_tokens, block), jnp.float32)
-    parts = (pieces(block, 256, 8), pieces(half_units, 1792, 128))
     kept, given = call(
-        lambda *refs: down_kernel(parts, *refs),
+        down_kernel,
         (part, part),
-        (chunks, down_weight),
-        [NEAR, FAR],
-        [
-            VECTOR(down_weight.shape, jnp.bfloat16),
-            VECTOR((tokens, half_units + block), jnp.bfloat16),
-            DMA(parts),
-        ],
-        24 << 20,
+        (chunks, down_rows),
+        [NEAR, NEAR],
+        [VECTOR((tokens, half_units + block), jnp.bfloat16)],
+        GRANT,
     )
     chunk = shaped((vocab_count, half_tokens, block), jnp.bfloat16)
     gain = norm_gain.astype(jnp.float32).reshape(vocab_count, block)
@@ -186,7 +178,7 @@
     part = shaped((half_tokens, half_width), jnp.bfloat16)
     own, other = call(norm_kernel, (part, part), (stream, gain), [NEAR] * 2)
     part = shaped((half_tokens, columns_here), jnp.float32)
-    parts_head = (1, pieces(half_width, 1024, 128))
+    parts_head = (1, pieces(half_width, 512, 128))
     kept, given = call(
         lambda *refs: head_kernel(parts_head, *refs),
         (part, part),

time: 54.2 us -> 53.6 us (0.989)
  Pallas kernels: 13.2 us -> 7.46 us
  starting transfers between devices: 0.36 us -> 5.5 us
    pallas_call x5, Pallas kernels: 13.2 us -> 7.46 us  [call(): pl.pallas_call(kernel, out_shape=out_shape, in_specs=places, out_specs=ja...]
    ppermute x0 -> x1, starting transfers between devices: none -> 5.2 us  [brought(): lax.ppermute(weight, 'mp', own)]
  transfers between devices with their start and end apart: 3 -> 4, of which waited for: 3 -> 3; matrix products, arithmetic and copies ran while one was open for 0% -> 0% of each run, Pallas kernels for 0% -> 2%
where the time goes in v3:
time: 53.6 us; the launch traced here: 53.2 us
  blocking collectives  35.8 us (67%)
  Pallas kernels  7.46 us (14%)
  starting transfers between devices  5.5 us (10%)
  waiting for transfers between devices  3.44 us (6%)
  other arithmetic  0.95 us (2%)
    all_to_all x3, blocking collectives, swapped(): return fence(lax.all_to_all(fence(value), 'vocab', 0, 0, tiled=True))  35.8 us
    pallas_call x5, Pallas kernels, call(): pl.pallas_call(kernel, out_shape=out_shape, in_specs=places, out_specs=ja...  7.46 us
    ppermute x1, starting transfers between devices, brought(): lax.ppermute(weight, 'mp', own)  5.2 us
    ppermute x3, waiting for transfers between devices, partner(): return lax.ppermute(value, 'mp', [(0, 1), (1, 0)])  3.44 us
  transfers between devices with their start and end apart: 4, of which 3 were waited for; matrix products, arithmetic and copies ran while one was open for 0% of the time, Pallas kernels for 2%

profile of v3, /device:TPU:0, one launch (start us, length us, event | category | flops | bytes accessed | tf_op | source)
XLA Modules:
  0.0 53.2 jit_solution(16671289462797473895)
XLA Ops:
  0.0 0.0 copy-start
  0.0 0.0 copy-start.1
  0.0 5.2 %collective-permute-start = (bf16[1024,7168]{1,0:T(8,128)(2,1)}, bf16[1024,7168]{1,0:T(8,128)(2,1)S(1)}, u32[]{:S(2)}, u32[]{:S(2)}) collective-permute-start(bf16[1024,7168]{1,0:T(8,128)(2,1)} %param.9), channel_id=1, source_target_pairs={{0,0},{1,1},{2,2},{3,3},{4,4},{5,5},{6,6},{7,7},{8,8},{9,9},{10,10... | collective-permute-start | bytes 44040200 | tf_op jit(solution)/shard_map/ppermute | solution.py:21
  5.2 0.9 %shard_map.73 = bf16[8,2,8192]{2,1,0:T(2,128)(2,1)S(1)} custom-call(bf16[2,7168]{1,0:T(2,128)(2,1)} %gate_hbm.1, bf16[2,7168]{1,0:T(2,128)(2,1)} %up_hbm.1, bf16[1,8192]{1,0:T(2,128)(2,1)} %residual_hbm.1), custom_call_target="tpu_custom_call" | custom-call | tf_op jit(solution)/shard_map/pallas_call | solution.py:37
  6.1 16.0 %all_to_all.15.chunks_ref = bf16[8,2,8192]{2,1,0:T(2,128)(2,1)S(1)} all-to-all(bf16[8,2,8192]{2,1,0:T(2,128)(2,1)S(1)} %shard_map.73), channel_id=1, replica_groups=mesh['groups'=2,'vocab'=8,'mp'=2] {'vocab'}, dimensions={0} | all-to-all | bytes 524288 | tf_op jit(solution)/shard_map/all_to_all | solution.py:29
  22.1 0.0 collective-permute-done.weight_ref
  22.1 3.9 %shard_map.74 = (f32[8,1024]{1,0:T(8,128)S(1)}, f32[8,1024]{1,0:T(8,128)S(1)}) custom-call(bf16[8,2,8192]{2,1,0:T(2,128)(2,1)S(1)} %all_to_all.15.chunks_ref, bf16[1024,7168]{1,0:T(8,128)(2,1)S(1)} %collective-permute-done.weight_ref), custom_call_target="tpu_custom_call" | custom-call | tf_op jit(solution)/shard_map/pallas_call | solution.py:37
  26.0 0.0 collective-permute-start.1
  26.0 0.0 copy-done
  26.1 1.2 %collective-permute-done.1.arrived_ref = f32[8,1024]{1,0:T(8,128)S(1)} collective-permute-done((f32[8,1024]{1,0:T(8,128)S(1)}, f32[8,1024]{1,0:T(8,128)S(1)}, u32[]{:S(2)}, u32[]{:S(2)}) %collective-permute-start.1) | collective-permute-done | bytes 32800 | tf_op jit(solution)/shard_map/ppermute | solution.py:25
  27.3 10.7 %all_to_all.16.stream_ref = bf16[8,8,1024]{2,1,0:T(8,128)(2,1)S(1)} all-to-all(bf16[8,8,1024]{2,1,0:T(8,128)(2,1)S(1)} %shard_map.75), channel_id=1, replica_groups=mesh['groups'=2,'vocab'=8,'mp'=2] {'vocab'}, dimensions={0} | all-to-all | bytes 262144 | tf_op jit(solution)/shard_map/all_to_all | solution.py:29
  38.0 0.1 shard_map.76
  38.1 0.1 collective-permute-start.2
  38.2 1.2 %collective-permute-done.2.refs_1_ = bf16[8,4096]{1,0:T(8,128)(2,1)S(1)} collective-permute-done((bf16[8,4096]{1,0:T(8,128)(2,1)S(1)}, bf16[8,4096]{1,0:T(8,128)(2,1)S(1)}, u32[]{:S(2)}, u32[]{:S(2)}) %collective-permute-start.2) | collective-permute-done | bytes 65568 | tf_op jit(solution)/shard_map/ppermute | solution.py:25
  39.5 2.5 %shard_map.77 = (f32[8,504]{1,0:T(8,128)S(1)}, f32[8,504]{1,0:T(8,128)S(1)}) custom-call(bf16[8,4096]{1,0:T(8,128)(2,1)S(1)} %get-tuple-element.17.refs_0_, bf16[8,4096]{1,0:T(8,128)(2,1)S(1)} %collective-permute-done.2.refs_1_, bf16[504,4096]{1,0:T(8,128)(2,1)} %bitcast.10), custom_call_target="tpu_custom_call" | custom-call | tf_op jit(solution)/shard_map/pallas_call | solution.py:37
  42.0 0.2 collective-permute-start.3
  42.2 0.0 copy-done.1
  42.2 1.0 %collective-permute-done.3 = f32[8,504]{1,0:T(8,128)S(1)} collective-permute-done((f32[8,504]{1,0:T(8,128)S(1)}, f32[8,504]{1,0:T(8,128)S(1)}, u32[]{:S(2)}, u32[]{:S(2)}) %collective-permute-start.3) | collective-permute-done | bytes 16160 | tf_op jit(solution)/shard_map/ppermute | solution.py:25
  43.2 0.1 fusion
  43.3 0.2 exponential_reduce_fusion
  43.6 9.1 %all_to_all.17 = f32[8,3,8]{2,1,0:T(4,128)S(1)} all-to-all(f32[8,3,8]{2,1,0:T(4,128)S(1)} %broadcast_in_dim.7), channel_id=1, replica_groups=mesh['groups'=2,'vocab'=8,'mp'=2] {'vocab'}, dimensions={0} | all-to-all | bytes 1536 | tf_op jit(solution)/shard_map/all_to_all | solution.py:29
  52.7 0.5 log_subtract_fusion
  (8 shorter events, 0.1 us)
Async XLA Ops:
  0.0 26.1 %copy-start = (bf16[8192]{0:T(1024)(128)(2,1)S(1)}, bf16[8192]{0:T(1024)(128)(2,1)}, u32[]{:S(2)}) copy-start(bf16[8192]{0:T(1024)(128)(2,1)} %param.11) | copy-start | bytes 49156
  0.0 42.2 %copy-start.1 = (s32[8]{0:T(128)S(1)}, s32[8]{0:T(128)}, u32[]{:S(2)}) copy-start(s32[8]{0:T(128)} %param.13) | copy-start | bytes 100
  0.0 22.1 %collective-permute-start = (bf16[1024,7168]{1,0:T(8,128)(2,1)}, bf16[1024,7168]{1,0:T(8,128)(2,1)S(1)}, u32[]{:S(2)}, u32[]{:S(2)}) collective-permute-start(bf16[1024,7168]{1,0:T(8,128)(2,1)} %param.9), channel_id=1, source_target_pairs={{0,0},{1,1},{2,2},{3,3},{4,4},{5,5},{6,6},{7,7},{8,8},{9,9},{10,10... | collective-permute-start | bytes 44040200 | tf_op jit(solution)/shard_map/ppermute | solution.py:21
  26.0 1.2 %collective-permute-start.1 = (f32[8,1024]{1,0:T(8,128)S(1)}, f32[8,1024]{1,0:T(8,128)S(1)}, u32[]{:S(2)}, u32[]{:S(2)}) collective-permute-start(f32[8,1024]{1,0:T(8,128)S(1)} %get-tuple-element.14), channel_id=1, source_target_pairs={{0,1},{1,0},{2,3},{3,2},{4,5},{5,4},{6,7},{7,6},{8,9},{9,8},{10,11... | collective-permute-start | bytes 98312 | tf_op jit(solution)/shard_map/ppermute | solution.py:25
  38.1 1.3 %collective-permute-start.2 = (bf16[8,4096]{1,0:T(8,128)(2,1)S(1)}, bf16[8,4096]{1,0:T(8,128)(2,1)S(1)}, u32[]{:S(2)}, u32[]{:S(2)}) collective-permute-start(bf16[8,4096]{1,0:T(8,128)(2,1)S(1)} %get-tuple-element.18), channel_id=1, source_target_pairs={{0,1},{1,0},{2,3},{3,2},{4,5},{5,4},{6,7},{7,6},{8,9},{9,8},{10,11... | collective-permute-start | bytes 196616 | tf_op jit(solution)/shard_map/ppermute | solution.py:25
  42.0 1.2 %collective-permute-start.3 = (f32[8,504]{1,0:T(8,128)S(1)}, f32[8,504]{1,0:T(8,128)S(1)}, u32[]{:S(2)}, u32[]{:S(2)}) collective-permute-start(f32[8,504]{1,0:T(8,128)S(1)} %get-tuple-element.20), channel_id=1, source_target_pairs={{0,1},{1,0},{2,3},{3,2},{4,5},{5,4},{6,7},{7,6},{8,9},{9,8},{10,11... | collective-permute-start | bytes 48392 | tf_op jit(solution)/shard_map/ppermute | solution.py:25

commit v4 on v2

--- a/solution.py
+++ b/solution.py
@@ -152,9 +152,42 @@
     given_ref[...] = terms[tokens:]
 
 
+def stats_kernel(kept_ref, arrived_ref, targets_ref, out_ref):
+    logits = kept_ref[...] + arrived_ref[...]
+    tokens, columns = logits.shape
+    square = (tokens, tokens)
+    diagonal = lax.broadcasted_iota(jnp.int32, square, 0) == lax.broadcasted_iota(
+        jnp.int32, square, 1
+    )
+    wanted = jnp.broadcast_to(targets_ref[...].reshape(1, tokens), square).astype(jnp.float32)
+    wanted = jnp.sum(jnp.where(diagonal, wanted, 0.0), axis=1, keepdims=True).astype(jnp.int32)
+    wanted -= lax.axis_index("vocab") * columns
+    here = lax.broadcasted_iota(jnp.int32, logits.shape, 1) == wanted
+    chosen = jnp.sum(jnp.where(here, logits, 0.0), axis=1, keepdims=True)
+    top = jnp.max(logits, axis=1, keepdims=True)
+    total = jnp.sum(jnp.exp(logits - top), axis=1, keepdims=True)
+    lane = lax.broadcasted_iota(jnp.int32, (tokens, 3 * tokens), 1)
+    token = lax.broadcasted_iota(jnp.int32, (tokens, 3 * tokens), 0)
+    row = jnp.zeros((tokens, 3 * tokens), jnp.float32)
+    for place, value in enumerate((top, total, chosen)):
+        row = jnp.where(lane == token + place * tokens, value, row)
+    row = jnp.sum(row, axis=0, keepdims=True)
+    for peer in range(out_ref.shape[0]):
+        out_ref[peer] = row
+
+
+def merge_kernel(stats_ref, out_ref):
+    tokens = out_ref.shape[1]
+    tops = stats_ref[:, 0, :tokens]
+    totals = stats_ref[:, 0, tokens : 2 * tokens]
+    chosen = jnp.sum(stats_ref[:, 0, 2 * tokens :], axis=0, keepdims=True)
+    top = jnp.max(tops, axis=0, keepdims=True)
+    total = jnp.sum(totals * jnp.exp(tops - top), axis=0, keepdims=True)
+    out_ref[...] = chosen - top - jnp.log(total)
+
+
 def body(gate_pre, up_pre, down_weight, residual, norm_gain, head_weight, targets):
     vocab_count = lax.axis_size("vocab")
-    vocab_index = lax.axis_index("vocab")
     rows, half_units = gate_pre.shape
     block = down_weight.shape[0]
     tokens = rows * vocab_count
@@ -166,7 +199,7 @@
     places = [VECTOR(one.shape, one.dtype) for one in operands]
     chunks = swapped(call(gated_kernel, chunk, operands, [FAR] * 3, places + [DMA((3,))]))
     part = shaped((half_tokens, block), jnp.float32)
-    parts = (pieces(block, 256, 8), pieces(half_units, 1792, 128))
+    parts = (1, pieces(half_units, 512, 128))
     kept, given = call(
         lambda *refs: down_kernel(parts, *refs),
         (part, part),
@@ -186,7 +219,7 @@
     part = shaped((half_tokens, half_width), jnp.bfloat16)
     own, other = call(norm_kernel, (part, part), (stream, gain), [NEAR] * 2)
     part = shaped((half_tokens, columns_here), jnp.float32)
-    parts_head = (1, pieces(half_width, 1024, 128))
+    parts_head = (1, pieces(half_width, 512, 128))
     kept, given = call(
         lambda *refs: head_kernel(parts_head, *refs),
         (part, part),
@@ -195,17 +228,11 @@
         [VECTOR((columns_here, half_width), jnp.bfloat16), DMA(parts_head)],
         12 << 20,
     )
-    logits = kept + partner(given)
-    local_ids = targets - vocab_index * columns_here
-    columns = lax.broadcasted_iota(jnp.int32, logits.shape, 1)
-    chosen = jnp.sum(jnp.where(columns == local_ids[:, None], logits, 0.0), axis=1)
-    row_top = jnp.max(logits, axis=1)
-    exp_total = jnp.sum(jnp.exp(logits - row_top[:, None]), axis=1)
-    stats = jnp.stack([row_top, exp_total, chosen])
-    stats = swapped(jnp.broadcast_to(stats[None], (vocab_count,) + stats.shape))
-    top = jnp.max(stats[:, 0], axis=0)
-    total = jnp.sum(stats[:, 1] * jnp.exp(stats[:, 0] - top[None]), axis=0)
-    return jnp.sum(stats[:, 2], axis=0) - top - jnp.log(total)
+    row = shaped((vocab_count, 1, 3 * half_tokens), jnp.float32)
+    operands = (kept, partner(given), targets)
+    stats = swapped(call(stats_kernel, row, operands, [NEAR] * 3))
+    row = shaped((1, half_tokens), jnp.float32)
+    return call(merge_kernel, row, (stats,), [NEAR]).reshape(half_tokens)
 
 
 def solution(mesh):

time: 54.2 us -> 50.2 us (0.926)
  Pallas kernels: 13.2 us -> 10.3 us
  other arithmetic: 0.95 us -> 0 us
    pallas_call x5 -> x7, Pallas kernels: 13.2 us -> 10.3 us  [call(): pl.pallas_call(kernel, out_shape=out_shape, in_specs=places, out_specs=ja...]
where the time goes in v4:
time: 50.2 us; the launch traced here: 49.9 us
  blocking collectives  35.7 us (71%)
  Pallas kernels  10.3 us (21%)
  waiting for transfers between devices  3.43 us (7%)
    all_to_all x3, blocking collectives, swapped(): return fence(lax.all_to_all(fence(value), 'vocab', 0, 0, tiled=True))  35.7 us
    pallas_call x7, Pallas kernels, call(): pl.pallas_call(kernel, out_shape=out_shape, in_specs=places, out_specs=ja...  10.3 us
    ppermute x3, waiting for transfers between devices, partner(): return lax.ppermute(value, 'mp', [(0, 1), (1, 0)])  3.43 us
  transfers between devices with their start and end apart: 3, of which 3 were waited for; matrix products, arithmetic and copies ran while one was open for 0% of the time, Pallas kernels for 0%

profile of v4, /device:TPU:0, one launch (start us, length us, event | category | flops | bytes accessed | tf_op | source)
XLA Modules:
  0.0 49.9 jit_solution(12187403757612888571)
XLA Ops:
  0.0 0.0 copy-start.1
  0.0 0.0 copy-start
  0.0 0.9 %shard_map.73 = bf16[8,2,8192]{2,1,0:T(2,128)(2,1)S(1)} custom-call(bf16[2,7168]{1,0:T(2,128)(2,1)} %gate_hbm.1, bf16[2,7168]{1,0:T(2,128)(2,1)} %up_hbm.1, bf16[1,8192]{1,0:T(2,128)(2,1)} %residual_hbm.1), custom_call_target="tpu_custom_call" | custom-call | tf_op jit(solution)/shard_map/pallas_call | solution.py:31
  0.9 16.0 %all_to_all.15.refs_0_ = bf16[8,2,8192]{2,1,0:T(2,128)(2,1)S(1)} all-to-all(bf16[8,2,8192]{2,1,0:T(2,128)(2,1)S(1)} %shard_map.73), channel_id=1, replica_groups=mesh['groups'=2,'vocab'=8,'mp'=2] {'vocab'}, dimensions={0} | all-to-all | bytes 524288 | tf_op jit(solution)/shard_map/all_to_all | solution.py:23
  16.9 5.8 %shard_map.74 = (f32[8,1024]{1,0:T(8,128)S(1)}, f32[8,1024]{1,0:T(8,128)S(1)}) custom-call(bf16[8,2,8192]{2,1,0:T(2,128)(2,1)S(1)} %all_to_all.15.refs_0_, bf16[1024,7168]{1,0:T(8,128)(2,1)} %refs_1_.1), custom_call_target="tpu_custom_call" | custom-call | tf_op jit(solution)/shard_map/pallas_call | solution.py:31
  22.8 0.1 collective-permute-start
  22.8 0.0 copy-done.1
  22.9 1.2 %collective-permute-done.arrived_ref = f32[8,1024]{1,0:T(8,128)S(1)} collective-permute-done((f32[8,1024]{1,0:T(8,128)S(1)}, f32[8,1024]{1,0:T(8,128)S(1)}, u32[]{:S(2)}, u32[]{:S(2)}) %collective-permute-start) | collective-permute-done | bytes 32800 | tf_op jit(solution)/shard_map/ppermute | solution.py:19
  24.1 10.7 %all_to_all.16.stream_ref = bf16[8,8,1024]{2,1,0:T(8,128)(2,1)S(1)} all-to-all(bf16[8,8,1024]{2,1,0:T(8,128)(2,1)S(1)} %shard_map.75), channel_id=1, replica_groups=mesh['groups'=2,'vocab'=8,'mp'=2] {'vocab'}, dimensions={0} | all-to-all | bytes 262144 | tf_op jit(solution)/shard_map/all_to_all | solution.py:23
  34.8 0.1 shard_map.76
  34.9 0.1 collective-permute-start.1
  35.0 1.2 %collective-permute-done.1.refs_1_ = bf16[8,4096]{1,0:T(8,128)(2,1)S(1)} collective-permute-done((bf16[8,4096]{1,0:T(8,128)(2,1)S(1)}, bf16[8,4096]{1,0:T(8,128)(2,1)S(1)}, u32[]{:S(2)}, u32[]{:S(2)}) %collective-permute-start.1) | collective-permute-done | bytes 65568 | tf_op jit(solution)/shard_map/ppermute | solution.py:19
  36.2 2.5 %shard_map.77 = (f32[8,504]{1,0:T(8,128)S(1)}, f32[8,504]{1,0:T(8,128)S(1)}) custom-call(bf16[8,4096]{1,0:T(8,128)(2,1)S(1)} %get-tuple-element.17.refs_0_, bf16[8,4096]{1,0:T(8,128)(2,1)S(1)} %collective-permute-done.1.refs_1_, bf16[504,4096]{1,0:T(8,128)(2,1)} %bitcast.2), custom_call_target="tpu_custom_call" | custom-call | tf_op jit(solution)/shard_map/pallas_call | solution.py:31
  38.7 0.2 collective-permute-start.2
  39.0 1.0 %collective-permute-done.2.arrived_ref = f32[8,504]{1,0:T(8,128)S(1)} collective-permute-done((f32[8,504]{1,0:T(8,128)S(1)}, f32[8,504]{1,0:T(8,128)S(1)}, u32[]{:S(2)}, u32[]{:S(2)}) %collective-permute-start.2) | collective-permute-done | bytes 16160 | tf_op jit(solution)/shard_map/ppermute | solution.py:19
  40.0 0.0 copy-done
  40.0 0.2 shard_map.78
  40.2 9.0 %all_to_all.17.stats_ref = f32[8,1,24]{2,1,0:T(1,128)S(1)} all-to-all(f32[8,1,24]{2,1,0:T(1,128)S(1)} %shard_map.78), channel_id=1, replica_groups=mesh['groups'=2,'vocab'=8,'mp'=2] {'vocab'}, dimensions={0} | all-to-all | bytes 1536 | tf_op jit(solution)/shard_map/all_to_all | solution.py:23
  49.1 0.7 %shard_map.79 = f32[1,8]{1,0:T(1,128)} custom-call(f32[8,1,24]{2,1,0:T(1,128)S(1)} %all_to_all.17.stats_ref), custom_call_target="tpu_custom_call" | custom-call | tf_op jit(solution)/shard_map/pallas_call | solution.py:31
  (2 shorter events, 0.0 us)
Async XLA Ops:
  0.0 22.8 %copy-start.1 = (bf16[8192]{0:T(1024)(128)(2,1)S(1)}, bf16[8192]{0:T(1024)(128)(2,1)}, u32[]{:S(2)}) copy-start(bf16[8192]{0:T(1024)(128)(2,1)} %param.11) | copy-start | bytes 49156
  0.0 40.0 %copy-start = (s32[8]{0:T(128)S(1)}, s32[8]{0:T(128)}, u32[]{:S(2)}) copy-start(s32[8]{0:T(128)} %targets_ref.1) | copy-start | bytes 100
  22.8 1.3 %collective-permute-start = (f32[8,1024]{1,0:T(8,128)S(1)}, f32[8,1024]{1,0:T(8,128)S(1)}, u32[]{:S(2)}, u32[]{:S(2)}) collective-permute-start(f32[8,1024]{1,0:T(8,128)S(1)} %get-tuple-element.14), channel_id=1, source_target_pairs={{0,1},{1,0},{2,3},{3,2},{4,5},{5,4},{6,7},{7,6},{8,9},{9,8},{10,11... | collective-permute-start | bytes 98312 | tf_op jit(solution)/shard_map/ppermute | solution.py:19
  34.9 1.3 %collective-permute-start.1 = (bf16[8,4096]{1,0:T(8,128)(2,1)S(1)}, bf16[8,4096]{1,0:T(8,128)(2,1)S(1)}, u32[]{:S(2)}, u32[]{:S(2)}) collective-permute-start(bf16[8,4096]{1,0:T(8,128)(2,1)S(1)} %get-tuple-element.18), channel_id=1, source_target_pairs={{0,1},{1,0},{2,3},{3,2},{4,5},{5,4},{6,7},{7,6},{8,9},{9,8},{10,11... | collective-permute-start | bytes 196616 | tf_op jit(solution)/shard_map/ppermute | solution.py:19
  38.7 1.2 %collective-permute-start.2 = (f32[8,504]{1,0:T(8,128)S(1)}, f32[8,504]{1,0:T(8,128)S(1)}, u32[]{:S(2)}, u32[]{:S(2)}) collective-permute-start(f32[8,504]{1,0:T(8,128)S(1)} %get-tuple-element.20), channel_id=1, source_target_pairs={{0,1},{1,0},{2,3},{3,2},{4,5},{5,4},{6,7},{7,6},{8,9},{9,8},{10,11... | collective-permute-start | bytes 48392 | tf_op jit(solution)/shard_map/ppermute | solution.py:19

commit v5 on v4

v5 whole, which is shorter than its diff:
```python
import jax
import jax.numpy as jnp
from jax import lax
from jax.experimental import pallas as pl
from jax.experimental.pallas import tpu as pltpu
from jax.sharding import PartitionSpec as P

EPSILON = 1e-05
ROWS_BY_ROWS = (((1,), (1,)), ((), ()))
SMALL = 2 << 20
fence = lax.optimization_barrier
NEAR = pl.BlockSpec(memory_space=pltpu.VMEM)
FAR = pl.BlockSpec(memory_space=pltpu.HBM)
FREE = pl.BlockSpec(memory_space=pl.ANY)
VECTOR = pltpu.VMEM
DMA = pltpu.SemaphoreType.DMA


def partner(value):
    return lax.ppermute(value, "mp", [(0, 1), (1, 0)])


def swapped(value):
    return fence(lax.all_to_all(fence(value), "vocab", 0, 0, tiled=True))


def call(
    kernel, out_shape, operands, places, scratch=(), results=None, grant=SMALL, cost=0
):
    operands = tuple(
        pltpu.with_memory_space_constraint(one, pltpu.HBM) if place is FAR else one
        for one, place in zip(operands, places)
    )
    return pl.pallas_call(
        kernel,
        out_shape=out_shape,
        in_specs=places,
        out_specs=results or jax.tree.map(lambda _: NEAR, out_shape),
        scratch_shapes=list(scratch),
        cost_estimate=pl.CostEstimate(flops=0, bytes_accessed=cost, transcendentals=0) if cost else None,
        compiler_params=pltpu.CompilerParams(vmem_limit_bytes=grant),
    )(*operands)


def block_of(length, most):
    return max(size for size in range(1, most + 1) if length % size == 0)


def gated_kernel(
    gate_hbm, up_hbm, residual_hbm, weight_hbm, out_ref, early_ref, gate_ref, up_ref, residual_ref, done
):
    loads = (
        pltpu.make_async_copy(gate_hbm, gate_ref, done.at[0]),
        pltpu.make_async_copy(up_hbm, up_ref, done.at[1]),
        pltpu.make_async_copy(residual_hbm, residual_ref, done.at[2]),
        pltpu.make_async_copy(
            weight_hbm.at[:, pl.ds(0, early_ref.shape[1])], early_ref, done.at[3]
        ),
    )
    for load in loads:
        load.start()
    for load in loads[:3]:
        load.wait()
    count, rows, width = out_ref.shape
    units = gate_ref.shape[1]
    extra = width - units
    gate = gate_ref[...].astype(jnp.float32)
    up = up_ref[...].astype(jnp.float32)
    gated = (gate / (1.0 + jnp.exp(-gate)) * up).astype(jnp.bfloat16)
    for peer in range(count):
        out_ref[peer, :, :units] = gated
        for row in range(rows):
            first = (peer * rows + row) * extra
            out_ref[peer, row : row + 1, units:] = residual_ref[:, first : first + extra]
    loads[3].wait()


def weight_loads(weight_hbm, weight_ref, done, skip):
    depth = weight_ref.shape[1] // done.shape[0]
    loads = []
    for part in range(done.shape[0]):
        loads.append(
            pltpu.make_async_copy(
                weight_hbm.at[:, pl.ds(skip + part * depth, depth)],
                weight_ref.at[:, pl.ds(part * depth, depth)],
                done.at[part],
            )
        )
        loads[-1].start()
    return loads, depth


def product(left, early_ref, weight_ref, loads, depth):
    skip = early_ref.shape[1]
    terms = lax.dot_general(
        left(0, skip), early_ref[...], ROWS_BY_ROWS, preferred_element_type=jnp.float32
    )
    for part, load in enumerate(loads):
        load.wait()
        terms += lax.dot_general(
            left(skip + part * depth, depth),
            weight_ref[:, part * depth : (part + 1) * depth],
            ROWS_BY_ROWS,
            preferred_element_type=jnp.float32,
        )
    return terms


def down_kernel(chunks_ref, early_ref, weight_hbm, kept_ref, given_ref, weight_ref, units_ref, done):
    units = weight_hbm.shape[1]
    loads, depth = weight_loads(weight_hbm, weight_ref, done, early_ref.shape[1])
    count, rows, width = chunks_ref.shape
    half, block = kept_ref.shape
    for peer in range(count):
        units_ref[peer * rows : (peer + 1) * rows, :] = chunks_ref[peer]
    terms = product(
        lambda first, size: units_ref[:, first : first + size], early_ref, weight_ref, loads, depth
    )
    index = lax.axis_index("mp")
    token = lax.broadcasted_iota(jnp.int32, (count * rows, block), 0)
    pieces = [
        jnp.concatenate(
            [chunks_ref[peer, row : row + 1, units:].astype(jnp.float32) for row in range(rows)],
            axis=1,
        )
        for peer in range(count)
    ]
    own = jnp.concatenate([jnp.broadcast_to(piece, (rows, block)) for piece in pieces], axis=0)
    terms += jnp.where(lax.rem(token, rows) == index, own, 0.0)
    low, high = terms[:half], terms[half:]
    is_low = index == 0
    kept_ref[...] = jnp.where(is_low, low, high)
    given_ref[...] = jnp.where(is_low, high, low)


def stream_kernel(kept_ref, arrived_ref, out_ref):
    stream = (kept_ref[...] + arrived_ref[...]).astype(jnp.bfloat16)
    for peer in range(out_ref.shape[0]):
        out_ref[peer] = stream


def norm_kernel(stream_ref, gain_ref, own_ref, other_ref):
    count, tokens, block = stream_ref.shape
    half = count // 2
    squares = jnp.zeros((tokens, block), jnp.float32)
    for part in range(count):
        values = stream_ref[part].astype(jnp.float32)
        squares += values * values
    mean_square = jnp.sum(squares, axis=1, keepdims=True) / (count * block)
    scale = lax.rsqrt(mean_square + EPSILON)
    index = lax.axis_index("mp")
    for out_ref, side in ((own_ref, index), (other_ref, 1 - index)):
        for part in range(half):
            at = side * half + part
            gain = gain_ref[pl.ds(at, 1), :]
            values = stream_ref[at].astype(jnp.float32) * scale * gain
            out_ref[:, part * block : (part + 1) * block] = values.astype(jnp.bfloat16)


def early_kernel(weight_hbm, early_ref, done):
    load = pltpu.make_async_copy(weight_hbm.at[:, pl.ds(0, early_ref.shape[1])], early_ref, done)
    load.start()
    load.wait()


def head_kernel(own_ref, other_ref, early_ref, weight_hbm, kept_ref, given_ref, weight_ref, done):
    loads, depth = weight_loads(weight_hbm, weight_ref, done, early_ref.shape[1])
    tokens = own_ref.shape[0]
    terms = product(
        lambda first, size: jnp.concatenate(
            [own_ref[:, first : first + size], other_ref[:, first : first + size]], axis=0
        ),
        early_ref,
        weight_ref,
        loads,
        depth,
    )
    kept_ref[...] = terms[:tokens]
    given_ref[...] = terms[tokens:]


def stats_kernel(kept_ref, arrived_ref, targets_ref, out_ref):
    logits = kept_ref[...] + arrived_ref[...]
    tokens, columns = logits.shape
    square = (tokens, tokens)
    diagonal = lax.broadcasted_iota(jnp.int32, square, 0) == lax.broadcasted_iota(
        jnp.int32, square, 1
    )
    wanted = jnp.broadcast_to(targets_ref[...].reshape(1, tokens), square).astype(jnp.float32)
    wanted = jnp.sum(jnp.where(diagonal, wanted, 0.0), axis=1, keepdims=True).astype(jnp.int32)
    wanted -= lax.axis_index("vocab") * columns
    here = lax.broadcasted_iota(jnp.int32, logits.shape, 1) == wanted
    chosen = jnp.sum(jnp.where(here, logits, 0.0), axis=1, keepdims=True)
    top = jnp.max(logits, axis=1, keepdims=True)
    total = jnp.sum(jnp.exp(logits - top), axis=1, keepdims=True)
    lane = lax.broadcasted_iota(jnp.int32, (tokens, 3 * tokens), 1)
    token = lax.broadcasted_iota(jnp.int32, (tokens, 3 * tokens), 0)
    row = jnp.zeros((tokens, 3 * tokens), jnp.float32)
    for place, value in enumerate((top, total, chosen)):
        row = jnp.where(lane == token + place * tokens, value, row)
    row = jnp.sum(row, axis=0, keepdims=True)
    for peer in range(out_ref.shape[0]):
        out_ref[peer] = row


def body(gate_pre, up_pre, down_weight, residual, norm_gain, head_weight, targets):
    vocab_count = lax.axis_size("vocab")
    rows, half_units = gate_pre.shape
    block = down_weight.shape[0]
    tokens = rows * vocab_count
    half_tokens = targets.shape[0]
    half_width, columns_here = head_weight.shape
    shaped = jax.ShapeDtypeStruct
    step = block_of(half_units, 512)
    extra = residual.shape[0] * block // rows
    chunk = shaped((vocab_count, rows, half_units + extra), jnp.bfloat16)
    operands = (gate_pre, up_pre, residual, down_weight)
    places = [VECTOR(one.shape, one.dtype) for one in operands[:3]]
    early = pltpu.VMEM((block, step), jnp.bfloat16)
    chunks, early = call(
        gated_kernel, (chunk, early), operands, [FAR] * 4, places + [DMA((4,))], results=(NEAR, FREE)
    )
    part = shaped((half_tokens, block), jnp.float32)
    rest = half_units - step
    kept, given = call(
        down_kernel,
        (part, part),
        (swapped(chunks), early, down_weight),
        [NEAR, NEAR, FAR],
        [
            VECTOR((block, rest), jnp.bfloat16),
            VECTOR((tokens, half_units + extra), jnp.bfloat16),
            DMA((rest // step,)),
        ],
        grant=24 << 20,
    )
    chunk = shaped((vocab_count, half_tokens, block), jnp.bfloat16)
    gain = norm_gain.astype(jnp.float32).reshape(vocab_count, block)
    arrived, gain = fence((partner(given), gain))
    stream = swapped(call(stream_kernel, chunk, (kept, arrived), [NEAR] * 2))
    part = shaped((half_tokens, half_width), jnp.bfloat16)
    own, other = call(norm_kernel, (part, part), (stream, gain), [NEAR] * 2)
    step = block_of(half_width, 512)
    first = half_width // step // 2 * step
    other, head_weight = fence((other, head_weight))
    early = call(
        early_kernel,
        pltpu.VMEM((columns_here, first), jnp.bfloat16),
        (head_weight.T,),
        [FAR],
        [DMA],
        results=FREE,
        cost=first * columns_here * 4,
    )
    part = shaped((half_tokens, columns_here), jnp.float32)
    rest = half_width - first
    kept, given = call(
        head_kernel,
        (part, part),
        (own, partner(other), early, head_weight.T),
        [NEAR, NEAR, NEAR, FAR],
        [VECTOR((columns_here, rest), jnp.bfloat16), DMA((rest // step,))],
        grant=12 << 20,
    )
    row = shaped((vocab_count, 1, 3 * half_tokens), jnp.float32)
    operands = (kept, partner(given), targets)
    stats = swapped(call(stats_kernel, row, operands, [NEAR] * 3))
    tops, totals, chosen = jnp.split(stats[:, 0], 3, axis=1)
    top = jnp.max(tops, axis=0)
    total = jnp.sum(totals * jnp.exp(tops - top[None]), axis=0)
    return jnp.sum(chosen, axis=0) - top - jnp.log(total)


def solution(mesh):
    return jax.shard_map(
        body,
        mesh=mesh,
        in_specs=(
            P(("groups", "vocab"), "mp"),
            P(("groups", "vocab"), "mp"),
            P("vocab", "mp"),
            P(("groups", "vocab", "mp"), None),
            P(),
            P("mp", "vocab"),
            P(("groups", "mp")),
        ),
        out_specs=P(("groups", "mp")),
        check_vma=False,
    )
```

time: 50.2 us -> 50.1 us (level)
  waiting for transfers between devices: 3.43 us -> 2.01 us
  Pallas kernels: 10.3 us -> 11 us
  other arithmetic: 0 us -> 0.63 us
    ppermute x3, waiting for transfers between devices: 3.43 us -> 2.01 us  [partner(): return lax.ppermute(value, 'mp', [(0, 1), (1, 0)])]
    pallas_call x7, Pallas kernels: 10.3 us -> 11 us  [call(): pl.pallas_call(kernel, out_shape=out_shape, in_specs=places, out_specs=re...]
    sub x0 -> x1, other arithmetic: none -> 0.53 us  [body(): return jnp.sum(chosen, axis=0) - top - jnp.log(total)]
  transfers between devices with their start and end apart: 3 -> 3, of which waited for: 3 -> 2; matrix products, arithmetic and copies ran while one was open for 0% -> 0% of each run, Pallas kernels for 0% -> 3%
where the time goes in v5:
time: 50.1 us; the launch traced here: 49.8 us
  blocking collectives  35.3 us (70%)
  Pallas kernels  11 us (22%)
  waiting for transfers between devices  2.01 us (4%)
  starting transfers between devices  0.7 us (1%)
  other arithmetic  0.63 us (1%)
    all_to_all x3, blocking collectives, swapped(): return fence(lax.all_to_all(fence(value), 'vocab', 0, 0, tiled=True))  35.3 us
    pallas_call x7, Pallas kernels, call(): pl.pallas_call(kernel, out_shape=out_shape, in_specs=places, out_specs=re...  11 us
    ppermute x3, waiting for transfers between devices, partner(): return lax.ppermute(value, 'mp', [(0, 1), (1, 0)])  2.01 us
  transfers between devices with their start and end apart: 3, of which 2 were waited for; matrix products, arithmetic and copies ran while one was open for 0% of the time, Pallas kernels for 3%

profile of v5, /device:TPU:0, one launch (start us, length us, event | category | flops | bytes accessed | tf_op | source)
XLA Modules:
  0.0 49.8 jit_solution(1308476712682572379)
XLA Ops:
  0.0 1.3 %shard_map.73 = (bf16[8,2,7680]{2,1,0:T(2,128)(2,1)S(1)}, bf16[1024,512]{1,0:T(8,128)(2,1)S(1)}) custom-call(bf16[2,7168]{1,0:T(2,128)(2,1)} %gate_hbm.1, bf16[2,7168]{1,0:T(2,128)(2,1)} %up_hbm.1, bf16[1,8192]{1,0:T(2,128)(2,1)} %residual_hbm.1, bf16[1024,7168]{1,0:T(8,128)(2,1)} %weight_hbm.3), custom_call_target="tpu_custom_call" | custom-call | tf_op jit(solution)/shard_map/pallas_call | solution.py:34
  1.3 15.8 %all_to_all.15.chunks_ref = bf16[8,2,7680]{2,1,0:T(2,128)(2,1)S(1)} all-to-all(bf16[8,2,7680]{2,1,0:T(2,128)(2,1)S(1)} %get-tuple-element.17), channel_id=1, replica_groups=mesh['groups'=2,'vocab'=8,'mp'=2] {'vocab'}, dimensions={0} | all-to-all | bytes 491520 | tf_op jit(solution)/shard_map/all_to_all | solution.py:24
  17.1 0.0 copy-start.1
  17.1 5.5 %shard_map.74 = (f32[8,1024]{1,0:T(8,128)S(1)}, f32[8,1024]{1,0:T(8,128)S(1)}) custom-call(bf16[8,2,7680]{2,1,0:T(2,128)(2,1)S(1)} %all_to_all.15.chunks_ref, bf16[1024,512]{1,0:T(8,128)(2,1)S(1)} %get-tuple-element.18.early_ref, bf16[1024,7168]{1,0:T(8,128)(2,1)} %weight_hbm.3), custom_call_target="tpu_custom_call" | custom-call | tf_op jit(solution)/shard_map/pallas_call | solution.py:34
  22.6 0.1 collective-permute-start
  22.7 0.0 copy-done.1
  22.7 1.2 %collective-permute-done.arrived_ref = f32[8,1024]{1,0:T(8,128)S(1)} collective-permute-done((f32[8,1024]{1,0:T(8,128)S(1)}, f32[8,1024]{1,0:T(8,128)S(1)}, u32[]{:S(2)}, u32[]{:S(2)}) %collective-permute-start) | collective-permute-done | bytes 32800 | tf_op jit(solution)/shard_map/ppermute | solution.py:20
  23.9 10.6 %all_to_all.16.stream_ref = bf16[8,8,1024]{2,1,0:T(8,128)(2,1)S(1)} all-to-all(bf16[8,8,1024]{2,1,0:T(8,128)(2,1)S(1)} %shard_map.75), channel_id=1, replica_groups=mesh['groups'=2,'vocab'=8,'mp'=2] {'vocab'}, dimensions={0} | all-to-all | bytes 262144 | tf_op jit(solution)/shard_map/all_to_all | solution.py:24
  34.5 0.1 shard_map.76
  34.6 0.1 collective-permute-start.1
  34.7 1.6 %shard_map.77.early_ref = bf16[504,2048]{1,0:T(8,128)(2,1)S(1)} custom-call(bf16[504,4096]{1,0:T(8,128)(2,1)} %bitcast.2), custom_call_target="tpu_custom_call" | custom-call | bytes 4128768 | tf_op jit(solution)/shard_map/pallas_call | solution.py:34
  36.3 0.0 copy-start
  36.3 0.0 collective-permute-done.1.other_ref
  36.3 2.3 %shard_map.78 = (f32[8,504]{1,0:T(8,128)S(1)}, f32[8,504]{1,0:T(8,128)S(1)}) custom-call(bf16[8,4096]{1,0:T(8,128)(2,1)S(1)} %get-tuple-element.23.own_ref, bf16[8,4096]{1,0:T(8,128)(2,1)S(1)} %collective-permute-done.1.other_ref, bf16[504,2048]{1,0:T(8,128)(2,1)S(1)} %shard_map.77.early_ref, bf16[504,4096]{1,0:T(8,128)(2,1)} %bitcast.3), custom_call_target="tpu_custom_call" | custom-call | tf_op jit(solution)/shard_map/pallas_call | solution.py:34
  38.6 0.6 %collective-permute-start.2 = (f32[8,504]{1,0:T(8,128)S(1)}, f32[8,504]{1,0:T(8,128)S(1)}, u32[]{:S(2)}, u32[]{:S(2)}) collective-permute-start(f32[8,504]{1,0:T(8,128)S(1)} %get-tuple-element.28), channel_id=1, source_target_pairs={{0,1},{1,0},{2,3},{3,2},{4,5},{5,4},{6,7},{7,6},{8,9},{9,8},{10,11... | collective-permute-start | bytes 48392 | tf_op jit(solution)/shard_map/ppermute | solution.py:20
  39.2 0.8 %collective-permute-done.2.arrived_ref = f32[8,504]{1,0:T(8,128)S(1)} collective-permute-done((f32[8,504]{1,0:T(8,128)S(1)}, f32[8,504]{1,0:T(8,128)S(1)}, u32[]{:S(2)}, u32[]{:S(2)}) %collective-permute-start.2) | collective-permute-done | bytes 16160 | tf_op jit(solution)/shard_map/ppermute | solution.py:20
  40.0 0.0 copy-done
  40.0 0.2 shard_map.79
  40.2 9.0 %all_to_all.17 = f32[8,1,24]{2,1,0:T(1,128)S(1)} all-to-all(f32[8,1,24]{2,1,0:T(1,128)S(1)} %shard_map.79), channel_id=1, replica_groups=mesh['groups'=2,'vocab'=8,'mp'=2] {'vocab'}, dimensions={0} | all-to-all | bytes 1536 | tf_op jit(solution)/shard_map/all_to_all | solution.py:24
  49.2 0.1 slice_reduce_fusion
  49.3 0.5 %log_subtract_fusion = f32[8]{0:T(128)} fusion(f32[8]{0:T(128)S(1)} %get-tuple-element.30, f32[8]{0:T(128)S(1)} %get-tuple-element.29, f32[8]{0:T(128)S(1)} %slice_reduce_fusion.1), kind=kLoop, calls=%fused_computation.3 | loop fusion | flops 16 | bytes 128 | tf_op jit(solution)/shard_map/sub | solution.py:271
  (3 shorter events, 0.0 us)
Async XLA Ops:
  17.1 5.6 %copy-start.1 = (bf16[8192]{0:T(1024)(128)(2,1)S(1)}, bf16[8192]{0:T(1024)(128)(2,1)}, u32[]{:S(2)}) copy-start(bf16[8192]{0:T(1024)(128)(2,1)} %param.11) | copy-start | bytes 49156
  22.6 1.3 %collective-permute-start = (f32[8,1024]{1,0:T(8,128)S(1)}, f32[8,1024]{1,0:T(8,128)S(1)}, u32[]{:S(2)}, u32[]{:S(2)}) collective-permute-start(f32[8,1024]{1,0:T(8,128)S(1)} %get-tuple-element.20), channel_id=1, source_target_pairs={{0,1},{1,0},{2,3},{3,2},{4,5},{5,4},{6,7},{7,6},{8,9},{9,8},{10,11... | collective-permute-start | bytes 98312 | tf_op jit(solution)/shard_map/ppermute | solution.py:20
  34.6 1.7 %collective-permute-start.1 = (bf16[8,4096]{1,0:T(8,128)(2,1)S(1)}, bf16[8,4096]{1,0:T(8,128)(2,1)S(1)}, u32[]{:S(2)}, u32[]{:S(2)}) collective-permute-start(bf16[8,4096]{1,0:T(8,128)(2,1)S(1)} %get-tuple-element.25), channel_id=1, source_target_pairs={{0,1},{1,0},{2,3},{3,2},{4,5},{5,4},{6,7},{7,6},{8,9},{9,8},{10,11... | collective-permute-start | bytes 196616 | tf_op jit(solution)/shard_map/ppermute | solution.py:20
  36.3 3.7 %copy-start = (s32[8]{0:T(128)S(1)}, s32[8]{0:T(128)}, u32[]{:S(2)}) copy-start(s32[8]{0:T(128)} %targets_ref.1) | copy-start | bytes 100
  38.6 1.4 %collective-permute-start.2 = (f32[8,504]{1,0:T(8,128)S(1)}, f32[8,504]{1,0:T(8,128)S(1)}, u32[]{:S(2)}, u32[]{:S(2)}) collective-permute-start(f32[8,504]{1,0:T(8,128)S(1)} %get-tuple-element.28), channel_id=1, source_target_pairs={{0,1},{1,0},{2,3},{3,2},{4,5},{5,4},{6,7},{7,6},{8,9},{9,8},{10,11... | collective-permute-start | bytes 48392 | tf_op jit(solution)/shard_map/ppermute | solution.py:20

commit v6 on v5

v6 whole, which is shorter than its diff:
```python
import jax
import jax.numpy as jnp
from jax import lax
from jax.experimental import pallas as pl
from jax.experimental.pallas import tpu as pltpu
from jax.sharding import PartitionSpec as P

EPSILON = 1e-05
ROWS_BY_ROWS = (((1,), (1,)), ((), ()))
SMALL = 2 << 20
fence = lax.optimization_barrier
NEAR = pl.BlockSpec(memory_space=pltpu.VMEM)
FAR = pl.BlockSpec(memory_space=pltpu.HBM)
VECTOR = pltpu.VMEM
DMA = pltpu.SemaphoreType.DMA


def partner(value):
    return lax.ppermute(value, "mp", [(0, 1), (1, 0)])


def swapped(value):
    return fence(lax.all_to_all(fence(value), "vocab", 0, 0, tiled=True))


def call(kernel, out_shape, operands, places, scratch=(), grant=SMALL):
    operands = tuple(
        pltpu.with_memory_space_constraint(one, pltpu.HBM) if place is FAR else one
        for one, place in zip(operands, places)
    )
    return pl.pallas_call(
        kernel,
        out_shape=out_shape,
        in_specs=places,
        out_specs=jax.tree.map(lambda _: NEAR, out_shape),
        scratch_shapes=list(scratch),
        compiler_params=pltpu.CompilerParams(vmem_limit_bytes=grant),
    )(*operands)


def block_of(length, most):
    return max(size for size in range(1, most + 1) if length % size == 0)


def gated_kernel(gate_hbm, up_hbm, residual_hbm, out_ref, gate_ref, up_ref, residual_ref, done):
    loads = (
        pltpu.make_async_copy(gate_hbm, gate_ref, done.at[0]),
        pltpu.make_async_copy(up_hbm, up_ref, done.at[1]),
        pltpu.make_async_copy(residual_hbm, residual_ref, done.at[2]),
    )
    for load in loads:
        load.start()
    for load in loads:
        load.wait()
    count, rows, width = out_ref.shape
    units = gate_ref.shape[1]
    extra = width - units
    gate = gate_ref[...].astype(jnp.float32)
    up = up_ref[...].astype(jnp.float32)
    gated = (gate / (1.0 + jnp.exp(-gate)) * up).astype(jnp.bfloat16)
    for peer in range(count):
        out_ref[peer, :, :units] = gated
        for row in range(rows):
            first = (peer * rows + row) * extra
            out_ref[peer, row : row + 1, units:] = residual_ref[:, first : first + extra]


def weight_loads(weight_hbm, weight_ref, done):
    depth = weight_ref.shape[1] // done.shape[0]
    loads = []
    for part in range(done.shape[0]):
        here = (slice(None), pl.ds(part * depth, depth))
        loads.append(
            pltpu.make_async_copy(weight_hbm.at[here], weight_ref.at[here], done.at[part])
        )
        loads[-1].start()
    return loads


def product(terms, left_ref, weight_ref, loads):
    depth = weight_ref.shape[1] // len(loads)
    for part, load in enumerate(loads):
        load.wait()
        here = slice(part * depth, (part + 1) * depth)
        terms += lax.dot_general(
            left_ref[:, here],
            weight_ref[:, here],
            ROWS_BY_ROWS,
            preferred_element_type=jnp.float32,
        )
    return terms


def down_kernel(chunks_ref, weight_hbm, kept_ref, given_ref, weight_ref, units_ref, own_ref, done):
    loads = weight_loads(weight_hbm, weight_ref, done)
    units = weight_hbm.shape[1]
    count, rows, width = chunks_ref.shape
    half, block = kept_ref.shape
    index = lax.axis_index("mp")
    token = lax.broadcasted_iota(jnp.int32, (rows, block), 0)
    for peer in range(count):
        units_ref[peer * rows : (peer + 1) * rows, :] = chunks_ref[peer, :, :units]
        pieces = [chunks_ref[peer, row : row + 1, units:].astype(jnp.float32) for row in range(rows)]
        residual = jnp.broadcast_to(jnp.concatenate(pieces, axis=1), (rows, block))
        own_ref[peer * rows : (peer + 1) * rows, :] = jnp.where(token == index, residual, 0.0)
    terms = product(own_ref[...], units_ref, weight_ref, loads)
    low, high = terms[:half], terms[half:]
    kept_ref[...] = jnp.where(index == 0, low, high)
    given_ref[...] = jnp.where(index == 0, high, low)


def stream_kernel(kept_ref, arrived_ref, out_ref):
    stream = (kept_ref[...] + arrived_ref[...]).astype(jnp.bfloat16)
    for peer in range(out_ref.shape[0]):
        out_ref[peer] = stream


def norm_kernel(stream_ref, gain_ref, own_ref, other_ref):
    count, tokens, block = stream_ref.shape
    half = count // 2
    squares = jnp.zeros((tokens, block), jnp.float32)
    for part in range(count):
        values = stream_ref[part].astype(jnp.float32)
        squares += values * values
    mean_square = jnp.sum(squares, axis=1, keepdims=True) / (count * block)
    scale = lax.rsqrt(mean_square + EPSILON)
    index = lax.axis_index("mp")
    for out_ref, side in ((own_ref, index), (other_ref, 1 - index)):
        for part in range(half):
            at = side * half + part
            gain = gain_ref[pl.ds(at, 1), :]
            values = stream_ref[at].astype(jnp.float32) * scale * gain
            out_ref[:, part * block : (part + 1) * block] = values.astype(jnp.bfloat16)


def column_of(row_ref):
    size = row_ref.shape[0]
    square = (size, size)
    diagonal = lax.broadcasted_iota(jnp.int32, square, 0) == lax.broadcasted_iota(
        jnp.int32, square, 1
    )
    spread = jnp.broadcast_to(row_ref[...].reshape(1, size), square).astype(jnp.float32)
    return jnp.sum(jnp.where(diagonal, spread, 0.0), axis=1, keepdims=True)


def head_kernel(own_ref, other_ref, targets_ref, weight_hbm, out_ref, weight_ref, halves_ref, done):
    loads = weight_loads(weight_hbm, weight_ref, done)
    tokens = own_ref.shape[0]
    columns = weight_ref.shape[0]
    halves_ref[...] = jnp.concatenate([own_ref[...], other_ref[...]], axis=0)
    out_ref[:tokens, columns:] = column_of(targets_ref)
    out_ref[tokens:, columns:] = jnp.zeros((tokens, 1), jnp.float32)
    terms = jnp.zeros((2 * tokens, columns), jnp.float32)
    out_ref[:, :columns] = product(terms, halves_ref, weight_ref, loads)


def stats_kernel(mine_ref, arrived_ref, out_ref):
    half = mine_ref.shape[0] // 2
    columns = mine_ref.shape[1] - 1
    own = mine_ref[:half, :] + arrived_ref[half:, :]
    other = mine_ref[half:, :] + arrived_ref[:half, :]
    is_low = lax.axis_index("mp") == 0
    both = jnp.concatenate(
        [jnp.where(is_low, own, other), jnp.where(is_low, other, own)], axis=0
    )
    logits, wanted = both[:, :columns], both[:, columns:].astype(jnp.int32)
    tokens = 2 * half
    wanted -= lax.axis_index("vocab") * columns
    here = lax.broadcasted_iota(jnp.int32, logits.shape, 1) == wanted
    chosen = jnp.sum(jnp.where(here, logits, 0.0), axis=1, keepdims=True)
    top = jnp.max(logits, axis=1, keepdims=True)
    total = jnp.sum(jnp.exp(logits - top), axis=1, keepdims=True)
    lane = lax.broadcasted_iota(jnp.int32, (tokens, 3 * tokens), 1)
    token = lax.broadcasted_iota(jnp.int32, (tokens, 3 * tokens), 0)
    row = jnp.zeros((tokens, 3 * tokens), jnp.float32)
    for place, value in enumerate((top, total, chosen)):
        row = jnp.where(lane == token + place * tokens, value, row)
    row = jnp.sum(row, axis=0, keepdims=True)
    for peer in range(out_ref.shape[0]):
        out_ref[peer] = row


def body(gate_pre, up_pre, down_weight, residual, norm_gain, head_weight, targets):
    vocab_count = lax.axis_size("vocab")
    rows, half_units = gate_pre.shape
    block = down_weight.shape[0]
    tokens = rows * vocab_count
    half_tokens = targets.shape[0]
    half_width, columns_here = head_weight.shape
    shaped = jax.ShapeDtypeStruct
    step = block_of(half_units, 512)
    extra = residual.shape[0] * block // rows
    chunk = shaped((vocab_count, rows, half_units + extra), jnp.bfloat16)
    operands = (gate_pre, up_pre, residual)
    places = [VECTOR(one.shape, one.dtype) for one in operands]
    chunks = swapped(call(gated_kernel, chunk, operands, [FAR] * 3, places + [DMA((3,))]))
    part = shaped((half_tokens, block), jnp.float32)
    kept, given = call(
        down_kernel,
        (part, part),
        (chunks, down_weight),
        [NEAR, FAR],
        [
            VECTOR(down_weight.shape, jnp.bfloat16),
            VECTOR((tokens, half_units), jnp.bfloat16),
            VECTOR((tokens, block), jnp.float32),
            DMA((half_units // step,)),
        ],
        grant=24 << 20,
    )
    chunk = shaped((vocab_count, half_tokens, block), jnp.bfloat16)
    gain = norm_gain.astype(jnp.float32).reshape(vocab_count, block)
    arrived, gain = fence((partner(given), gain))
    stream = swapped(call(stream_kernel, chunk, (kept, arrived), [NEAR] * 2))
    part = shaped((half_tokens, half_width), jnp.bfloat16)
    own, other = call(norm_kernel, (part, part), (stream, gain), [NEAR] * 2)
    step = block_of(half_width, 512)
    mine = call(
        head_kernel,
        shaped((tokens, columns_here + 1), jnp.float32),
        (own, partner(other), targets, head_weight.T),
        [NEAR, NEAR, NEAR, FAR],
        [
            VECTOR((columns_here, half_width), jnp.bfloat16),
            VECTOR((tokens, half_width), jnp.bfloat16),
            DMA((half_width // step,)),
        ],
        grant=12 << 20,
    )
    row = shaped((vocab_count, 1, 3 * tokens), jnp.float32)
    stats = call(stats_kernel, row, (mine, partner(mine)), [NEAR] * 2)
    model_count = lax.axis_size("mp")
    mixed = [
        [peer * model_count + (peer + core) % model_count for peer in range(vocab_count)]
        for core in range(model_count)
    ]
    stats, is_low = fence((stats, lax.axis_index("mp") == 0))
    stats = fence(
        lax.all_to_all(stats, ("vocab", "mp"), 0, 0, tiled=True, axis_index_groups=mixed)
    )
    tops, totals, chosen = jnp.split(stats[:, 0], 3, axis=1)
    top = jnp.max(tops, axis=0)
    total = jnp.sum(totals * jnp.exp(tops - top[None]), axis=0)
    chosen = jnp.sum(chosen, axis=0)
    low, high = (
        tuple(one[side] for one in (top, total, chosen))
        for side in (slice(None, half_tokens), slice(half_tokens, None))
    )
    top, total, chosen = (jnp.where(is_low, here, there) for here, there in zip(low, high))
    return chosen - top - jnp.log(total)


def solution(mesh):
    return jax.shard_map(
        body,
        mesh=mesh,
        in_specs=(
            P(("groups", "vocab"), "mp"),
            P(("groups", "vocab"), "mp"),
            P("vocab", "mp"),
            P(("groups", "vocab", "mp"), None),
            P(),
            P("mp", "vocab"),
            P(("groups", "mp")),
        ),
        out_specs=P(("groups", "mp")),
        check_vma=False,
    )
```

time: 50.1 us -> 49.1 us (0.980)
  waiting for transfers between devices: 2.01 us -> 3.46 us
  Pallas kernels: 11 us -> 9.55 us
  blocking collectives: 35.3 us -> 34.7 us
    all_to_all x3 -> x2, blocking collectives: 35.3 us -> 26.4 us  [swapped(): return fence(lax.all_to_all(fence(value), 'vocab', 0, 0, tiled=True))]
    all_to_all x0 -> x1, blocking collectives: none -> 8.28 us  [body(): lax.all_to_all(stats, ('vocab', 'mp'), 0, 0, tiled=True, axis_index_group...]
    pallas_call x7 -> x6, Pallas kernels: 11 us -> 9.55 us  [call(): pl.pallas_call(kernel, out_shape=out_shape, in_specs=places, out_specs=ja...]
    ppermute x3, waiting for transfers between devices: 2.01 us -> 3.46 us  [partner(): return lax.ppermute(value, 'mp', [(0, 1), (1, 0)])]
  transfers between devices with their start and end apart: 3 -> 3, of which waited for: 2 -> 3; matrix products, arithmetic and copies ran while one was open for 0% -> 0% of each run, Pallas kernels for 3% -> 0%
where the time goes in v6:
time: 49.1 us; the launch traced here: 48.8 us
  blocking collectives  34.7 us (71%)
  Pallas kernels  9.55 us (19%)
  waiting for transfers between devices  3.46 us (7%)
  other arithmetic  0.7 us (1%)
    all_to_all x2, blocking collectives, swapped(): return fence(lax.all_to_all(fence(value), 'vocab', 0, 0, tiled=True))  26.4 us
    pallas_call x6, Pallas kernels, call(): pl.pallas_call(kernel, out_shape=out_shape, in_specs=places, out_specs=ja...  9.55 us
    all_to_all x1, blocking collectives, body(): lax.all_to_all(stats, ('vocab', 'mp'), 0, 0, tiled=True, axis_index_group...  8.28 us
    ppermute x3, waiting for transfers between devices, partner(): return lax.ppermute(value, 'mp', [(0, 1), (1, 0)])  3.46 us
  transfers between devices with their start and end apart: 3, of which 3 were waited for; matrix products, arithmetic and copies ran while one was open for 0% of the time, Pallas kernels for 0%

profile of v6, /device:TPU:0, one launch (start us, length us, event | category | flops | bytes accessed | tf_op | source)
XLA Modules:
  0.0 48.8 jit_solution(10534746168476014537)
XLA Ops:
  0.0 0.0 copy-start.1
  0.0 0.0 copy-start
  0.0 0.9 %shard_map.73 = bf16[8,2,7680]{2,1,0:T(2,128)(2,1)S(1)} custom-call(bf16[2,7168]{1,0:T(2,128)(2,1)} %gate_hbm.1, bf16[2,7168]{1,0:T(2,128)(2,1)} %up_hbm.1, bf16[1,8192]{1,0:T(2,128)(2,1)} %residual_hbm.1), custom_call_target="tpu_custom_call" | custom-call | tf_op jit(solution)/shard_map/pallas_call | solution.py:31
  0.9 15.8 %all_to_all.15.chunks_ref = bf16[8,2,7680]{2,1,0:T(2,128)(2,1)S(1)} all-to-all(bf16[8,2,7680]{2,1,0:T(2,128)(2,1)S(1)} %shard_map.73), channel_id=1, replica_groups=mesh['groups'=2,'vocab'=8,'mp'=2] {'vocab'}, dimensions={0} | all-to-all | bytes 491520 | tf_op jit(solution)/shard_map/all_to_all | solution.py:23
  16.7 5.8 %shard_map.74 = (f32[8,1024]{1,0:T(8,128)S(1)}, f32[8,1024]{1,0:T(8,128)S(1)}) custom-call(bf16[8,2,7680]{2,1,0:T(2,128)(2,1)S(1)} %all_to_all.15.chunks_ref, bf16[1024,7168]{1,0:T(8,128)(2,1)} %weight_hbm.1), custom_call_target="tpu_custom_call" | custom-call | tf_op jit(solution)/shard_map/pallas_call | solution.py:31
  22.5 0.1 collective-permute-start
  22.6 0.0 copy-done.1
  22.6 1.2 %collective-permute-done.arrived_ref = f32[8,1024]{1,0:T(8,128)S(1)} collective-permute-done((f32[8,1024]{1,0:T(8,128)S(1)}, f32[8,1024]{1,0:T(8,128)S(1)}, u32[]{:S(2)}, u32[]{:S(2)}) %collective-permute-start) | collective-permute-done | bytes 32800 | tf_op jit(solution)/shard_map/ppermute | solution.py:19
  23.8 10.6 %all_to_all.16.stream_ref = bf16[8,8,1024]{2,1,0:T(8,128)(2,1)S(1)} all-to-all(bf16[8,8,1024]{2,1,0:T(8,128)(2,1)S(1)} %shard_map.75), channel_id=1, replica_groups=mesh['groups'=2,'vocab'=8,'mp'=2] {'vocab'}, dimensions={0} | all-to-all | bytes 262144 | tf_op jit(solution)/shard_map/all_to_all | solution.py:23
  34.4 0.1 shard_map.76
  34.5 0.1 collective-permute-start.1
  34.6 1.2 %collective-permute-done.1.other_ref = bf16[8,4096]{1,0:T(8,128)(2,1)S(1)} collective-permute-done((bf16[8,4096]{1,0:T(8,128)(2,1)S(1)}, bf16[8,4096]{1,0:T(8,128)(2,1)S(1)}, u32[]{:S(2)}, u32[]{:S(2)}) %collective-permute-start.1) | collective-permute-done | bytes 65568 | tf_op jit(solution)/shard_map/ppermute | solution.py:19
  35.9 0.0 copy-done
  35.9 2.5 %shard_map.77.mine_ref = f32[16,505]{1,0:T(8,128)S(1)} custom-call(bf16[8,4096]{1,0:T(8,128)(2,1)S(1)} %get-tuple-element.17.own_ref, bf16[8,4096]{1,0:T(8,128)(2,1)S(1)} %collective-permute-done.1.other_ref, s32[8]{0:T(128)S(1)} %copy-done, bf16[504,4096]{1,0:T(8,128)(2,1)} %bitcast.2), custom_call_target="tpu_custom_call" | custom-call | tf_op jit(solution)/shard_map/pallas_call | solution.py:31
  38.4 0.2 collective-permute-start.2
  38.6 1.1 %collective-permute-done.2.arrived_ref = f32[16,505]{1,0:T(8,128)S(1)} collective-permute-done((f32[16,505]{1,0:T(8,128)S(1)}, f32[16,505]{1,0:T(8,128)S(1)}, u32[]{:S(2)}, u32[]{:S(2)}) %collective-permute-start.2) | collective-permute-done | bytes 32352 | tf_op jit(solution)/shard_map/ppermute | solution.py:19
  39.6 0.2 shard_map.78
  39.8 8.3 %all_to_all.17 = f32[8,1,48]{2,1,0:T(1,128)S(1)} all-to-all(f32[8,1,48]{2,1,0:T(1,128)S(1)} %shard_map.78), channel_id=1, replica_groups={{0,3,4,7,8,11,12,15},{1,2,5,6,9,10,13,14},{16,19,20,23,24,27,28,31},{17..., dimensions={0} | all-to-all | bytes 3072 | tf_op jit(solution)/shard_map/all_to_all | solution.py:239
  48.1 0.1 slice_reduce_fusion
  48.2 0.6 %fusion.1 = f32[8]{0:T(128)} fusion(pred[]{:T(512)S(6)} %eq.3, f32[16]{0:T(128)S(1)} %get-tuple-element.22, f32[16]{0:T(128)S(1)} %slice_reduce_fusion.1, f32[16]{0:T(128)S(1)} %get-tuple-element.21), kind=kLoop, calls=%fused_computation.7 | loop fusion | flops 40 | bytes 225 | tf_op jit(solution)/shard_map/sub | solution.py:250
  (3 shorter events, 0.0 us)
Async XLA Ops:
  0.0 22.6 %copy-start.1 = (bf16[8192]{0:T(1024)(128)(2,1)S(1)}, bf16[8192]{0:T(1024)(128)(2,1)}, u32[]{:S(2)}) copy-start(bf16[8192]{0:T(1024)(128)(2,1)} %param.11) | copy-start | bytes 49156
  0.0 35.9 %copy-start = (s32[8]{0:T(128)S(1)}, s32[8]{0:T(128)}, u32[]{:S(2)}) copy-start(s32[8]{0:T(128)} %targets_ref.1) | copy-start | bytes 100
  22.5 1.3 %collective-permute-start = (f32[8,1024]{1,0:T(8,128)S(1)}, f32[8,1024]{1,0:T(8,128)S(1)}, u32[]{:S(2)}, u32[]{:S(2)}) collective-permute-start(f32[8,1024]{1,0:T(8,128)S(1)} %get-tuple-element.14), channel_id=1, source_target_pairs={{0,1},{1,0},{2,3},{3,2},{4,5},{5,4},{6,7},{7,6},{8,9},{9,8},{10,11... | collective-permute-start | bytes 98312 | tf_op jit(solution)/shard_map/ppermute | solution.py:19
  34.5 1.3 %collective-permute-start.1 = (bf16[8,4096]{1,0:T(8,128)(2,1)S(1)}, bf16[8,4096]{1,0:T(8,128)(2,1)S(1)}, u32[]{:S(2)}, u32[]{:S(2)}) collective-permute-start(bf16[8,4096]{1,0:T(8,128)(2,1)S(1)} %get-tuple-element.18), channel_id=1, source_target_pairs={{0,1},{1,0},{2,3},{3,2},{4,5},{5,4},{6,7},{7,6},{8,9},{9,8},{10,11... | collective-permute-start | bytes 196616 | tf_op jit(solution)/shard_map/ppermute | solution.py:19
  38.4 1.3 %collective-permute-start.2 = (f32[16,505]{1,0:T(8,128)S(1)}, f32[16,505]{1,0:T(8,128)S(1)}, u32[]{:S(2)}, u32[]{:S(2)}) collective-permute-start(f32[16,505]{1,0:T(8,128)S(1)} %shard_map.77.mine_ref), channel_id=1, source_target_pairs={{0,1},{1,0},{2,3},{3,2},{4,5},{5,4},{6,7},{7,6},{8,9},{9,8},{10,11... | collective-permute-start | bytes 96968 | tf_op jit(solution)/shard_map/ppermute | solution.py:19

commit v7 on v6

--- a/solution.py
+++ b/solution.py
@@ -8,6 +8,7 @@
 EPSILON = 1e-05
 ROWS_BY_ROWS = (((1,), (1,)), ((), ()))
 SMALL = 2 << 20
+HEAD_STEP = 1024
 fence = lax.optimization_barrier
 NEAR = pl.BlockSpec(memory_space=pltpu.VMEM)
 FAR = pl.BlockSpec(memory_space=pltpu.HBM)
@@ -21,6 +22,24 @@
 
 def swapped(value):
     return fence(lax.all_to_all(fence(value), "vocab", 0, 0, tiled=True))
+
+
+def fetched(weight, first, size):
+    def kernel(weight_hbm, out_ref, done):
+        load = pltpu.make_async_copy(weight_hbm.at[:, pl.ds(first, size)], out_ref, done)
+        load.start()
+        load.wait()
+
+    rows = weight.shape[0]
+    return pl.pallas_call(
+        kernel,
+        out_shape=pltpu.VMEM((rows, size), weight.dtype),
+        in_specs=[FAR],
+        out_specs=pl.BlockSpec(memory_space=pl.ANY),
+        scratch_shapes=[DMA],
+        cost_estimate=pl.CostEstimate(flops=0, bytes_accessed=4 * rows * size, transcendentals=0),
+        compiler_params=pltpu.CompilerParams(vmem_limit_bytes=SMALL),
+    )(pltpu.with_memory_space_constraint(weight, pltpu.HBM))
 
 
 def call(kernel, out_shape, operands, places, scratch=(), grant=SMALL):
@@ -67,27 +86,40 @@
 
 def weight_loads(weight_hbm, weight_ref, done):
     depth = weight_ref.shape[1] // done.shape[0]
+    first = weight_hbm.shape[1] - weight_ref.shape[1]
     loads = []
     for part in range(done.shape[0]):
-        here = (slice(None), pl.ds(part * depth, depth))
         loads.append(
-            pltpu.make_async_copy(weight_hbm.at[here], weight_ref.at[here], done.at[part])
+            pltpu.make_async_copy(
+                weight_hbm.at[:, pl.ds(first + part * depth, depth)],
+                weight_ref.at[:, pl.ds(part * depth, depth)],
+                done.at[part],
+            )
         )
         loads[-1].start()
     return loads
 
 
-def product(terms, left_ref, weight_ref, loads):
+def product(terms, left_ref, early, weight_ref, loads):
     depth = weight_ref.shape[1] // len(loads)
-    for part, load in enumerate(loads):
-        load.wait()
-        here = slice(part * depth, (part + 1) * depth)
+    at = 0
+    for here in early:
         terms += lax.dot_general(
-            left_ref[:, here],
-            weight_ref[:, here],
+            left_ref[:, at : at + here.shape[1]],
+            here[...],
             ROWS_BY_ROWS,
             preferred_element_type=jnp.float32,
         )
+        at += here.shape[1]
+    for part, load in enumerate(loads):
+        load.wait()
+        terms += lax.dot_general(
+            left_ref[:, at : at + depth],
+            weight_ref[:, part * depth : (part + 1) * depth],
+            ROWS_BY_ROWS,
+            preferred_element_type=jnp.float32,
+        )
+        at += depth
     return terms
 
 
@@ -103,7 +135,7 @@
         pieces = [chunks_ref[peer, row : row + 1, units:].astype(jnp.float32) for row in range(rows)]
         residual = jnp.broadcast_to(jnp.concatenate(pieces, axis=1), (rows, block))
         own_ref[peer * rows : (peer + 1) * rows, :] = jnp.where(token == index, residual, 0.0)
-    terms = product(own_ref[...], units_ref, weight_ref, loads)
+    terms = product(own_ref[...], units_ref, (), weight_ref, loads)
     low, high = terms[:half], terms[half:]
     kept_ref[...] = jnp.where(index == 0, low, high)
     given_ref[...] = jnp.where(index == 0, high, low)
@@ -143,7 +175,8 @@
     return jnp.sum(jnp.where(diagonal, spread, 0.0), axis=1, keepdims=True)
 
 
-def head_kernel(own_ref, other_ref, targets_ref, weight_hbm, out_ref, weight_ref, halves_ref, done):
+def head_kernel(own_ref, other_ref, targets_ref, *refs):
+    *early, weight_hbm, out_ref, weight_ref, halves_ref, done = refs
     loads = weight_loads(weight_hbm, weight_ref, done)
     tokens = own_ref.shape[0]
     columns = weight_ref.shape[0]
@@ -151,7 +184,7 @@
     out_ref[:tokens, columns:] = column_of(targets_ref)
     out_ref[tokens:, columns:] = jnp.zeros((tokens, 1), jnp.float32)
     terms = jnp.zeros((2 * tokens, columns), jnp.float32)
-    out_ref[:, :columns] = product(terms, halves_ref, weight_ref, loads)
+    out_ref[:, :columns] = product(terms, halves_ref, early, weight_ref, loads)
 
 
 def stats_kernel(mine_ref, arrived_ref, out_ref):
@@ -208,22 +241,27 @@
         ],
         grant=24 << 20,
     )
+    step = block_of(half_width, HEAD_STEP)
+    given, head_rows = fence((given, head_weight.T))
+    first = fetched(head_rows, 0, step)
     chunk = shaped((vocab_count, half_tokens, block), jnp.bfloat16)
     gain = norm_gain.astype(jnp.float32).reshape(vocab_count, block)
-    arrived, gain = fence((partner(given), gain))
+    arrived, gain, first = fence((partner(given), gain, first))
     stream = swapped(call(stream_kernel, chunk, (kept, arrived), [NEAR] * 2))
     part = shaped((half_tokens, half_width), jnp.bfloat16)
     own, other = call(norm_kernel, (part, part), (stream, gain), [NEAR] * 2)
-    step = block_of(half_width, 512)
+    other, head_rows = fence((other, head_rows))
+    early = (first, fetched(head_rows, step, step))
+    rest = half_width - 2 * step
     mine = call(
         head_kernel,
         shaped((tokens, columns_here + 1), jnp.float32),
-        (own, partner(other), targets, head_weight.T),
-        [NEAR, NEAR, NEAR, FAR],
+        (own, partner(other), targets, *early, head_rows),
+        [NEAR] * 5 + [FAR],
         [
-            VECTOR((columns_here, half_width), jnp.bfloat16),
+            VECTOR((columns_here, rest), jnp.bfloat16),
             VECTOR((tokens, half_width), jnp.bfloat16),
-            DMA((half_width // step,)),
+            DMA((rest // block_of(rest, 512),)),
         ],
         grant=12 << 20,
     )

time: 49.1 us -> 49.5 us (level)
  waiting for transfers between devices: 3.46 us -> 0.87 us
  Pallas kernels: 9.55 us -> 11.7 us
    ppermute x3, waiting for transfers between devices: 3.46 us -> 0.87 us  [partner(): return lax.ppermute(value, 'mp', [(0, 1), (1, 0)])]
    pallas_call x0 -> x2, Pallas kernels: none -> 2.46 us  [fetched(): pl.pallas_call(kernel, out_shape=pltpu.VMEM((rows, size), weight.dtype),...]
  transfers between devices with their start and end apart: 3 -> 3, of which waited for: 3 -> 1; matrix products, arithmetic and copies ran while one was open for 0% -> 0% of each run, Pallas kernels for 0% -> 5%
where the time goes in v7:
time: 49.5 us; the launch traced here: 49.1 us
  blocking collectives  35 us (71%)
  Pallas kernels  11.7 us (24%)
  waiting for transfers between devices  0.87 us (2%)
  starting transfers between devices  0.7 us (1%)
  other arithmetic  0.7 us (1%)
    all_to_all x2, blocking collectives, swapped(): return fence(lax.all_to_all(fence(value), 'vocab', 0, 0, tiled=True))  26.7 us
    pallas_call x6, Pallas kernels, call(): pl.pallas_call(kernel, out_shape=out_shape, in_specs=places, out_specs=ja...  9.22 us
    all_to_all x1, blocking collectives, body(): lax.all_to_all(stats, ('vocab', 'mp'), 0, 0, tiled=True, axis_index_group...  8.38 us
    pallas_call x2, Pallas kernels, fetched(): pl.pallas_call(kernel, out_shape=pltpu.VMEM((rows, size), weight.dtype),...  2.46 us
  transfers between devices with their start and end apart: 3, of which 1 were waited for; matrix products, arithmetic and copies ran while one was open for 0% of the time, Pallas kernels for 5%

profile of v7, /device:TPU:0, one launch (start us, length us, event | category | flops | bytes accessed | tf_op | source)
XLA Modules:
  0.0 49.1 jit_solution(9497271161295365036)
XLA Ops:
  0.0 0.0 copy-start.1
  0.0 0.0 copy-start
  0.0 0.9 %shard_map.73 = bf16[8,2,7680]{2,1,0:T(2,128)(2,1)S(1)} custom-call(bf16[2,7168]{1,0:T(2,128)(2,1)} %gate_hbm.1, bf16[2,7168]{1,0:T(2,128)(2,1)} %up_hbm.1, bf16[1,8192]{1,0:T(2,128)(2,1)} %residual_hbm.1), custom_call_target="tpu_custom_call" | custom-call | tf_op jit(solution)/shard_map/pallas_call | solution.py:50
  0.9 15.8 %all_to_all.15.chunks_ref = bf16[8,2,7680]{2,1,0:T(2,128)(2,1)S(1)} all-to-all(bf16[8,2,7680]{2,1,0:T(2,128)(2,1)S(1)} %shard_map.73), channel_id=1, replica_groups=mesh['groups'=2,'vocab'=8,'mp'=2] {'vocab'}, dimensions={0} | all-to-all | bytes 491520 | tf_op jit(solution)/shard_map/all_to_all | solution.py:24
  16.7 5.8 %shard_map.74 = (f32[8,1024]{1,0:T(8,128)S(1)}, f32[8,1024]{1,0:T(8,128)S(1)}) custom-call(bf16[8,2,7680]{2,1,0:T(2,128)(2,1)S(1)} %all_to_all.15.chunks_ref, bf16[1024,7168]{1,0:T(8,128)(2,1)} %weight_hbm.1), custom_call_target="tpu_custom_call" | custom-call | tf_op jit(solution)/shard_map/pallas_call | solution.py:50
  22.5 0.1 collective-permute-start
  22.6 0.0 copy-done.1
  22.6 1.2 %shard_map.75.refs_0_ = bf16[504,1024]{1,0:T(8,128)(2,1)S(1)} custom-call(bf16[504,4096]{1,0:T(8,128)(2,1)} %bitcast.2), custom_call_target="tpu_custom_call" | custom-call | bytes 2064384 | tf_op jit(solution)/shard_map/pallas_call | solution.py:34
  23.8 0.0 collective-permute-done.arrived_ref
  23.9 10.9 %all_to_all.16.stream_ref = bf16[8,8,1024]{2,1,0:T(8,128)(2,1)S(1)} all-to-all(bf16[8,8,1024]{2,1,0:T(8,128)(2,1)S(1)} %shard_map.76), channel_id=1, replica_groups=mesh['groups'=2,'vocab'=8,'mp'=2] {'vocab'}, dimensions={0} | all-to-all | bytes 262144 | tf_op jit(solution)/shard_map/all_to_all | solution.py:24
  34.8 0.1 shard_map.77
  34.9 0.1 collective-permute-start.1
  35.0 1.2 %shard_map.78.refs_1_ = bf16[504,1024]{1,0:T(8,128)(2,1)S(1)} custom-call(bf16[504,4096]{1,0:T(8,128)(2,1)} %bitcast.3), custom_call_target="tpu_custom_call" | custom-call | bytes 2064384 | tf_op jit(solution)/shard_map/pallas_call | solution.py:34
  36.2 0.0 collective-permute-done.1.other_ref
  36.3 0.0 copy-done
  36.3 2.2 %shard_map.79.mine_ref = f32[16,505]{1,0:T(8,128)S(1)} custom-call(bf16[8,4096]{1,0:T(8,128)(2,1)S(1)} %get-tuple-element.24.own_ref, bf16[8,4096]{1,0:T(8,128)(2,1)S(1)} %collective-permute-done.1.other_ref, s32[8]{0:T(128)S(1)} %copy-done, bf16[504,1024]{1,0:T(8,128)(2,1)S(1)} %shard_map.75.refs_0_, bf16[504,1024]{1,0:T(8,128)(2,1)S(1)} %shard_map.78.refs_1_, ...), custom_call_target="tpu_custom_call" | custom-call | tf_op jit(solution)/shard_map/pallas_call | solution.py:50
  38.4 0.6 %collective-permute-start.2 = (f32[16,505]{1,0:T(8,128)S(1)}, f32[16,505]{1,0:T(8,128)S(1)}, u32[]{:S(2)}, u32[]{:S(2)}) collective-permute-start(f32[16,505]{1,0:T(8,128)S(1)} %shard_map.79.mine_ref), channel_id=1, source_target_pairs={{0,1},{1,0},{2,3},{3,2},{4,5},{5,4},{6,7},{7,6},{8,9},{9,8},{10,11... | collective-permute-start | bytes 96968 | tf_op jit(solution)/shard_map/ppermute | solution.py:20
  39.0 0.9 %collective-permute-done.2.arrived_ref = f32[16,505]{1,0:T(8,128)S(1)} collective-permute-done((f32[16,505]{1,0:T(8,128)S(1)}, f32[16,505]{1,0:T(8,128)S(1)}, u32[]{:S(2)}, u32[]{:S(2)}) %collective-permute-start.2) | collective-permute-done | bytes 32352 | tf_op jit(solution)/shard_map/ppermute | solution.py:20
  39.9 0.2 shard_map.80
  40.0 8.4 %all_to_all.17 = f32[8,1,48]{2,1,0:T(1,128)S(1)} all-to-all(f32[8,1,48]{2,1,0:T(1,128)S(1)} %shard_map.80), channel_id=1, replica_groups={{0,3,4,7,8,11,12,15},{1,2,5,6,9,10,13,14},{16,19,20,23,24,27,28,31},{17..., dimensions={0} | all-to-all | bytes 3072 | tf_op jit(solution)/shard_map/all_to_all | solution.py:277
  48.5 0.1 slice_reduce_fusion
  48.5 0.6 %fusion.1 = f32[8]{0:T(128)} fusion(pred[]{:T(512)S(6)} %eq.3, f32[16]{0:T(128)S(1)} %get-tuple-element.32, f32[16]{0:T(128)S(1)} %slice_reduce_fusion.1, f32[16]{0:T(128)S(1)} %get-tuple-element.31), kind=kLoop, calls=%fused_computation.7 | loop fusion | flops 40 | bytes 225 | tf_op jit(solution)/shard_map/sub | solution.py:288
  (3 shorter events, 0.0 us)
Async XLA Ops:
  0.0 22.6 %copy-start.1 = (bf16[8192]{0:T(1024)(128)(2,1)S(1)}, bf16[8192]{0:T(1024)(128)(2,1)}, u32[]{:S(2)}) copy-start(bf16[8192]{0:T(1024)(128)(2,1)} %param.11) | copy-start | bytes 49156
  0.0 36.3 %copy-start = (s32[8]{0:T(128)S(1)}, s32[8]{0:T(128)}, u32[]{:S(2)}) copy-start(s32[8]{0:T(128)} %targets_ref.1) | copy-start | bytes 100
  22.5 1.3 %collective-permute-start = (f32[8,1024]{1,0:T(8,128)S(1)}, f32[8,1024]{1,0:T(8,128)S(1)}, u32[]{:S(2)}, u32[]{:S(2)}) collective-permute-start(f32[8,1024]{1,0:T(8,128)S(1)} %get-tuple-element.20), channel_id=1, source_target_pairs={{0,1},{1,0},{2,3},{3,2},{4,5},{5,4},{6,7},{7,6},{8,9},{9,8},{10,11... | collective-permute-start | bytes 98312 | tf_op jit(solution)/shard_map/ppermute | solution.py:20
  34.9 1.3 %collective-permute-start.1 = (bf16[8,4096]{1,0:T(8,128)(2,1)S(1)}, bf16[8,4096]{1,0:T(8,128)(2,1)S(1)}, u32[]{:S(2)}, u32[]{:S(2)}) collective-permute-start(bf16[8,4096]{1,0:T(8,128)(2,1)S(1)} %get-tuple-element.26), channel_id=1, source_target_pairs={{0,1},{1,0},{2,3},{3,2},{4,5},{5,4},{6,7},{7,6},{8,9},{9,8},{10,11... | collective-permute-start | bytes 196616 | tf_op jit(solution)/shard_map/ppermute | solution.py:20
  38.4 1.4 %collective-permute-start.2 = (f32[16,505]{1,0:T(8,128)S(1)}, f32[16,505]{1,0:T(8,128)S(1)}, u32[]{:S(2)}, u32[]{:S(2)}) collective-permute-start(f32[16,505]{1,0:T(8,128)S(1)} %shard_map.79.mine_ref), channel_id=1, source_target_pairs={{0,1},{1,0},{2,3},{3,2},{4,5},{5,4},{6,7},{7,6},{8,9},{9,8},{10,11... | collective-permute-start | bytes 96968 | tf_op jit(solution)/shard_map/ppermute | solution.py:20

commit v8 on v7

--- a/solution.py
+++ b/solution.py
@@ -8,7 +8,7 @@
 EPSILON = 1e-05
 ROWS_BY_ROWS = (((1,), (1,)), ((), ()))
 SMALL = 2 << 20
-HEAD_STEP = 1024
+EARLY = 3
 fence = lax.optimization_barrier
 NEAR = pl.BlockSpec(memory_space=pltpu.VMEM)
 FAR = pl.BlockSpec(memory_space=pltpu.HBM)
@@ -123,7 +123,9 @@
     return terms
 
 
-def down_kernel(chunks_ref, weight_hbm, kept_ref, given_ref, weight_ref, units_ref, own_ref, done):
+def down_kernel(
+    chunks_ref, early_ref, weight_hbm, kept_ref, given_ref, weight_ref, units_ref, own_ref, done
+):
     loads = weight_loads(weight_hbm, weight_ref, done)
     units = weight_hbm.shape[1]
     count, rows, width = chunks_ref.shape
@@ -135,7 +137,7 @@
         pieces = [chunks_ref[peer, row : row + 1, units:].astype(jnp.float32) for row in range(rows)]
         residual = jnp.broadcast_to(jnp.concatenate(pieces, axis=1), (rows, block))
         own_ref[peer * rows : (peer + 1) * rows, :] = jnp.where(token == index, residual, 0.0)
-    terms = product(own_ref[...], units_ref, (), weight_ref, loads)
+    terms = product(own_ref[...], units_ref, (early_ref,), weight_ref, loads)
     low, high = terms[:half], terms[half:]
     kept_ref[...] = jnp.where(index == 0, low, high)
     given_ref[...] = jnp.where(index == 0, high, low)
@@ -226,42 +228,41 @@
     chunk = shaped((vocab_count, rows, half_units + extra), jnp.bfloat16)
     operands = (gate_pre, up_pre, residual)
     places = [VECTOR(one.shape, one.dtype) for one in operands]
-    chunks = swapped(call(gated_kernel, chunk, operands, [FAR] * 3, places + [DMA((3,))]))
+    chunks = call(gated_kernel, chunk, operands, [FAR] * 3, places + [DMA((3,))])
+    chunks, down_weight = fence((chunks, down_weight))
+    early = fetched(down_weight, 0, EARLY * step)
+    chunks = lax.all_to_all(chunks, "vocab", 0, 0, tiled=True)
+    chunks, early = fence((chunks, early))
+    rest = half_units - EARLY * step
     part = shaped((half_tokens, block), jnp.float32)
     kept, given = call(
         down_kernel,
         (part, part),
-        (chunks, down_weight),
-        [NEAR, FAR],
+        (chunks, early, down_weight),
+        [NEAR, NEAR, FAR],
         [
-            VECTOR(down_weight.shape, jnp.bfloat16),
+            VECTOR((block, rest), jnp.bfloat16),
             VECTOR((tokens, half_units), jnp.bfloat16),
             VECTOR((tokens, block), jnp.float32),
-            DMA((half_units // step,)),
+            DMA((rest // step,)),
         ],
         grant=24 << 20,
     )
-    step = block_of(half_width, HEAD_STEP)
-    given, head_rows = fence((given, head_weight.T))
-    first = fetched(head_rows, 0, step)
     chunk = shaped((vocab_count, half_tokens, block), jnp.bfloat16)
     gain = norm_gain.astype(jnp.float32).reshape(vocab_count, block)
-    arrived, gain, first = fence((partner(given), gain, first))
+    arrived, gain = fence((partner(given), gain))
     stream = swapped(call(stream_kernel, chunk, (kept, arrived), [NEAR] * 2))
     part = shaped((half_tokens, half_width), jnp.bfloat16)
     own, other = call(norm_kernel, (part, part), (stream, gain), [NEAR] * 2)
-    other, head_rows = fence((other, head_rows))
-    early = (first, fetched(head_rows, step, step))
-    rest = half_width - 2 * step
     mine = call(
         head_kernel,
         shaped((tokens, columns_here + 1), jnp.float32),
-        (own, partner(other), targets, *early, head_rows),
-        [NEAR] * 5 + [FAR],
+        (own, partner(other), targets, head_weight.T),
+        [NEAR] * 3 + [FAR],
         [
-            VECTOR((columns_here, rest), jnp.bfloat16),
+            VECTOR((columns_here, half_width), jnp.bfloat16),
             VECTOR((tokens, half_width), jnp.bfloat16),
-            DMA((rest // block_of(rest, 512),)),
+            DMA((half_width // block_of(half_width, 512),)),
         ],
         grant=12 << 20,
     )

time: 49.5 us -> 49.3 us (level)
  blocking collectives: 35 us -> 18.9 us
  waiting for transfers between devices: 0.87 us -> 10.2 us
  starting transfers between devices: 0.7 us -> 7.66 us
    all_to_all x2 -> x1, blocking collectives: 26.7 us -> 10.6 us  [swapped(): return fence(lax.all_to_all(fence(value), 'vocab', 0, 0, tiled=True))]
    all_to_all x0 -> x1, starting transfers between devices: none -> 7.29 us  [body(): chunks = lax.all_to_all(chunks, 'vocab', 0, 0, tiled=True)]
    all_to_all x0 -> x1, waiting for transfers between devices: none -> 6.75 us  [body(): chunks = lax.all_to_all(chunks, 'vocab', 0, 0, tiled=True)]
    ppermute x3, waiting for transfers between devices: 0.87 us -> 3.46 us  [partner(): return lax.ppermute(value, 'mp', [(0, 1), (1, 0)])]
    pallas_call x2 -> x1, Pallas kernels: 2.46 us -> 1.9 us  [fetched(): pl.pallas_call(kernel, out_shape=pltpu.VMEM((rows, size), weight.dtype),...]
  transfers between devices with their start and end apart: 3 -> 4, of which waited for: 1 -> 4; matrix products, arithmetic and copies ran while one was open for 0% -> 0% of each run, Pallas kernels for 5% -> 4%
where the time goes in v8:
time: 49.3 us; the launch traced here: 48.9 us
  blocking collectives  18.9 us (38%)
  Pallas kernels  11.3 us (23%)
  waiting for transfers between devices  10.2 us (21%)
  starting transfers between devices  7.66 us (16%)
  other arithmetic  0.7 us (1%)
    all_to_all x1, blocking collectives, swapped(): return fence(lax.all_to_all(fence(value), 'vocab', 0, 0, tiled=True))  10.6 us
    pallas_call x6, Pallas kernels, call(): pl.pallas_call(kernel, out_shape=out_shape, in_specs=places, out_specs=ja...  9.4 us
    all_to_all x1, blocking collectives, body(): lax.all_to_all(stats, ('vocab', 'mp'), 0, 0, tiled=True, axis_index_group...  8.28 us
    all_to_all x1, starting transfers between devices, body(): chunks = lax.all_to_all(chunks, 'vocab', 0, 0, tiled=True)  7.29 us
    all_to_all x1, waiting for transfers between devices, body(): chunks = lax.all_to_all(chunks, 'vocab', 0, 0, tiled=True)  6.75 us
    ppermute x3, waiting for transfers between devices, partner(): return lax.ppermute(value, 'mp', [(0, 1), (1, 0)])  3.46 us
    pallas_call x1, Pallas kernels, fetched(): pl.pallas_call(kernel, out_shape=pltpu.VMEM((rows, size), weight.dtype),...  1.9 us
  transfers between devices with their start and end apart: 4, of which 4 were waited for; matrix products, arithmetic and copies ran while one was open for 0% of the time, Pallas kernels for 4%

profile of v8, /device:TPU:0, one launch (start us, length us, event | category | flops | bytes accessed | tf_op | source)
XLA Modules:
  0.0 48.9 jit_solution(2584919555268588098)
XLA Ops:
  0.0 1.6 %shard_map.73 = bf16[8,2,7680]{2,1,0:T(2,128)(2,1)} custom-call(bf16[2,7168]{1,0:T(2,128)(2,1)} %gate_hbm.1, bf16[2,7168]{1,0:T(2,128)(2,1)} %up_hbm.1, bf16[1,8192]{1,0:T(2,128)(2,1)} %residual_hbm.1), custom_call_target="tpu_custom_call" | custom-call | tf_op jit(solution)/shard_map/pallas_call | solution.py:50
  1.6 7.3 %all-to-all-start = ((bf16[8,2,7680]{2,1,0:T(2,128)(2,1)}), bf16[8,2,7680]{2,1,0:T(2,128)(2,1)S(1)}, u32[]{:S(2)}, u32[]{:S(2)}) async-start(bf16[8,2,7680]{2,1,0:T(2,128)(2,1)} %shard_map.73), calls=%async_computation | async-start | bytes 491520 | tf_op jit(solution)/shard_map/all_to_all | solution.py:234
  8.9 1.9 %shard_map.74.early_ref = bf16[1024,1536]{1,0:T(8,128)(2,1)S(1)} custom-call(bf16[1024,7168]{1,0:T(8,128)(2,1)} %weight_hbm.1), custom_call_target="tpu_custom_call" | custom-call | bytes 6291456 | tf_op jit(solution)/shard_map/pallas_call | solution.py:34
  10.8 0.0 copy-start.1
  10.8 0.0 copy-start
  10.8 6.7 %all-to-all-done.chunks_ref = bf16[8,2,7680]{2,1,0:T(2,128)(2,1)S(1)} async-done(((bf16[8,2,7680]{2,1,0:T(2,128)(2,1)}), bf16[8,2,7680]{2,1,0:T(2,128)(2,1)S(1)}, u32[]{:S(2)}, u32[]{:S(2)}) %all-to-all-start) | async-done | bytes 245792 | tf_op jit(solution)/shard_map/all_to_all | solution.py:234
  17.5 5.0 %shard_map.75 = (f32[8,1024]{1,0:T(8,128)S(1)}, f32[8,1024]{1,0:T(8,128)S(1)}) custom-call(bf16[8,2,7680]{2,1,0:T(2,128)(2,1)S(1)} %all-to-all-done.chunks_ref, bf16[1024,1536]{1,0:T(8,128)(2,1)S(1)} %shard_map.74.early_ref, bf16[1024,7168]{1,0:T(8,128)(2,1)} %weight_hbm.1), custom_call_target="tpu_custom_call" | custom-call | tf_op jit(solution)/shard_map/pallas_call | solution.py:50
  22.6 0.1 collective-permute-start
  22.6 0.0 copy-done.1
  22.7 1.2 %collective-permute-done.arrived_ref = f32[8,1024]{1,0:T(8,128)S(1)} collective-permute-done((f32[8,1024]{1,0:T(8,128)S(1)}, f32[8,1024]{1,0:T(8,128)S(1)}, u32[]{:S(2)}, u32[]{:S(2)}) %collective-permute-start) | collective-permute-done | bytes 32800 | tf_op jit(solution)/shard_map/ppermute | solution.py:20
  23.8 10.6 %all_to_all.15.stream_ref = bf16[8,8,1024]{2,1,0:T(8,128)(2,1)S(1)} all-to-all(bf16[8,8,1024]{2,1,0:T(8,128)(2,1)S(1)} %shard_map.76), channel_id=1, replica_groups=mesh['groups'=2,'vocab'=8,'mp'=2] {'vocab'}, dimensions={0} | all-to-all | bytes 262144 | tf_op jit(solution)/shard_map/all_to_all | solution.py:24
  34.5 0.1 shard_map.77
  34.6 0.1 collective-permute-start.1
  34.7 1.2 %collective-permute-done.1.other_ref = bf16[8,4096]{1,0:T(8,128)(2,1)S(1)} collective-permute-done((bf16[8,4096]{1,0:T(8,128)(2,1)S(1)}, bf16[8,4096]{1,0:T(8,128)(2,1)S(1)}, u32[]{:S(2)}, u32[]{:S(2)}) %collective-permute-start.1) | collective-permute-done | bytes 65568 | tf_op jit(solution)/shard_map/ppermute | solution.py:20
  35.9 0.0 copy-done
  35.9 2.5 %shard_map.78.mine_ref = f32[16,505]{1,0:T(8,128)S(1)} custom-call(bf16[8,4096]{1,0:T(8,128)(2,1)S(1)} %get-tuple-element.25.own_ref, bf16[8,4096]{1,0:T(8,128)(2,1)S(1)} %collective-permute-done.1.other_ref, s32[8]{0:T(128)S(1)} %copy-done, bf16[504,4096]{1,0:T(8,128)(2,1)} %bitcast.2), custom_call_target="tpu_custom_call" | custom-call | tf_op jit(solution)/shard_map/pallas_call | solution.py:50
  38.4 0.2 collective-permute-start.2
  38.7 1.1 %collective-permute-done.2.arrived_ref = f32[16,505]{1,0:T(8,128)S(1)} collective-permute-done((f32[16,505]{1,0:T(8,128)S(1)}, f32[16,505]{1,0:T(8,128)S(1)}, u32[]{:S(2)}, u32[]{:S(2)}) %collective-permute-start.2) | collective-permute-done | bytes 32352 | tf_op jit(solution)/shard_map/ppermute | solution.py:20
  39.7 0.2 shard_map.79
  39.9 8.3 %all_to_all.16 = f32[8,1,48]{2,1,0:T(1,128)S(1)} all-to-all(f32[8,1,48]{2,1,0:T(1,128)S(1)} %shard_map.79), channel_id=1, replica_groups={{0,3,4,7,8,11,12,15},{1,2,5,6,9,10,13,14},{16,19,20,23,24,27,28,31},{17..., dimensions={0} | all-to-all | bytes 3072 | tf_op jit(solution)/shard_map/all_to_all | solution.py:278
  48.2 0.1 slice_reduce_fusion
  48.3 0.6 %fusion.1 = f32[8]{0:T(128)} fusion(pred[]{:T(512)S(6)} %eq.3, f32[16]{0:T(128)S(1)} %get-tuple-element.30, f32[16]{0:T(128)S(1)} %slice_reduce_fusion.1, f32[16]{0:T(128)S(1)} %get-tuple-element.29), kind=kLoop, calls=%fused_computation.7 | loop fusion | flops 40 | bytes 225 | tf_op jit(solution)/shard_map/sub | solution.py:289
  (3 shorter events, 0.0 us)
Async XLA Ops:
  1.6 16.0 %all-to-all-start = ((bf16[8,2,7680]{2,1,0:T(2,128)(2,1)}), bf16[8,2,7680]{2,1,0:T(2,128)(2,1)S(1)}, u32[]{:S(2)}, u32[]{:S(2)}) async-start(bf16[8,2,7680]{2,1,0:T(2,128)(2,1)} %shard_map.73), calls=%async_computation | async-start | bytes 491520 | tf_op jit(solution)/shard_map/all_to_all | solution.py:234
  10.8 11.9 %copy-start.1 = (bf16[8192]{0:T(1024)(128)(2,1)S(1)}, bf16[8192]{0:T(1024)(128)(2,1)}, u32[]{:S(2)}) copy-start(bf16[8192]{0:T(1024)(128)(2,1)} %param.11) | copy-start | bytes 49156
  10.8 25.2 %copy-start = (s32[8]{0:T(128)S(1)}, s32[8]{0:T(128)}, u32[]{:S(2)}) copy-start(s32[8]{0:T(128)} %targets_ref.1) | copy-start | bytes 100
  22.6 1.3 %collective-permute-start = (f32[8,1024]{1,0:T(8,128)S(1)}, f32[8,1024]{1,0:T(8,128)S(1)}, u32[]{:S(2)}, u32[]{:S(2)}) collective-permute-start(f32[8,1024]{1,0:T(8,128)S(1)} %get-tuple-element.22), channel_id=1, source_target_pairs={{0,1},{1,0},{2,3},{3,2},{4,5},{5,4},{6,7},{7,6},{8,9},{9,8},{10,11... | collective-permute-start | bytes 98312 | tf_op jit(solution)/shard_map/ppermute | solution.py:20
  34.6 1.3 %collective-permute-start.1 = (bf16[8,4096]{1,0:T(8,128)(2,1)S(1)}, bf16[8,4096]{1,0:T(8,128)(2,1)S(1)}, u32[]{:S(2)}, u32[]{:S(2)}) collective-permute-start(bf16[8,4096]{1,0:T(8,128)(2,1)S(1)} %get-tuple-element.26), channel_id=1, source_target_pairs={{0,1},{1,0},{2,3},{3,2},{4,5},{5,4},{6,7},{7,6},{8,9},{9,8},{10,11... | collective-permute-start | bytes 196616 | tf_op jit(solution)/shard_map/ppermute | solution.py:20
  38.4 1.3 %collective-permute-start.2 = (f32[16,505]{1,0:T(8,128)S(1)}, f32[16,505]{1,0:T(8,128)S(1)}, u32[]{:S(2)}, u32[]{:S(2)}) collective-permute-start(f32[16,505]{1,0:T(8,128)S(1)} %shard_map.78.mine_ref), channel_id=1, source_target_pairs={{0,1},{1,0},{2,3},{3,2},{4,5},{5,4},{6,7},{7,6},{8,9},{9,8},{10,11... | collective-permute-start | bytes 96968 | tf_op jit(solution)/shard_map/ppermute | solution.py:20

commit v9 on v8

--- a/solution.py
+++ b/solution.py
@@ -9,9 +9,11 @@
 ROWS_BY_ROWS = (((1,), (1,)), ((), ()))
 SMALL = 2 << 20
 EARLY = 3
+CHUNKS_GRANT = 8 << 20
 fence = lax.optimization_barrier
 NEAR = pl.BlockSpec(memory_space=pltpu.VMEM)
 FAR = pl.BlockSpec(memory_space=pltpu.HBM)
+FREE = pl.BlockSpec(memory_space=pl.ANY)
 VECTOR = pltpu.VMEM
 DMA = pltpu.SemaphoreType.DMA
 
@@ -20,29 +22,35 @@
     return lax.ppermute(value, "mp", [(0, 1), (1, 0)])
 
 
-def swapped(value):
-    return fence(lax.all_to_all(fence(value), "vocab", 0, 0, tiled=True))
-
-
-def fetched(weight, first, size):
-    def kernel(weight_hbm, out_ref, done):
-        load = pltpu.make_async_copy(weight_hbm.at[:, pl.ds(first, size)], out_ref, done)
-        load.start()
-        load.wait()
+def fetched(weight, sizes):
+    def kernel(weight_hbm, *refs):
+        *outs, done = refs
+        loads, first = [], 0
+        for out_ref in outs:
+            here = pl.ds(first, out_ref.shape[1])
+            loads.append(
+                pltpu.make_async_copy(weight_hbm.at[:, here], out_ref, done.at[len(loads)])
+            )
+            loads[-1].start()
+            first += out_ref.shape[1]
+        for load in loads:
+            load.wait()
 
     rows = weight.shape[0]
     return pl.pallas_call(
         kernel,
-        out_shape=pltpu.VMEM((rows, size), weight.dtype),
+        out_shape=tuple(pltpu.VMEM((rows, size), weight.dtype) for size in sizes),
         in_specs=[FAR],
-        out_specs=pl.BlockSpec(memory_space=pl.ANY),
-        scratch_shapes=[DMA],
-        cost_estimate=pl.CostEstimate(flops=0, bytes_accessed=4 * rows * size, transcendentals=0),
+        out_specs=(FREE,) * len(sizes),
+        scratch_shapes=[DMA((len(sizes),))],
+        cost_estimate=pl.CostEstimate(
+            flops=0, bytes_accessed=4 * rows * sum(sizes), transcendentals=0
+        ),
         compiler_params=pltpu.CompilerParams(vmem_limit_bytes=SMALL),
     )(pltpu.with_memory_space_constraint(weight, pltpu.HBM))
 
 
-def call(kernel, out_shape, operands, places, scratch=(), grant=SMALL):
+def call(kernel, out_shape, operands, places, scratch=(), grant=SMALL, results=None):
     operands = tuple(
         pltpu.with_memory_space_constraint(one, pltpu.HBM) if place is FAR else one
         for one, place in zip(operands, places)
@@ -51,7 +59,7 @@
         kernel,
         out_shape=out_shape,
         in_specs=places,
-        out_specs=jax.tree.map(lambda _: NEAR, out_shape),
+        out_specs=results or jax.tree.map(lambda _: NEAR, out_shape),
         scratch_shapes=list(scratch),
         compiler_params=pltpu.CompilerParams(vmem_limit_bytes=grant),
     )(*operands)
@@ -61,7 +69,9 @@
     return max(size for size in range(1, most + 1) if length % size == 0)
 
 
-def gated_kernel(gate_hbm, up_hbm, residual_hbm, out_ref, gate_ref, up_ref, residual_ref, done):
+def gated_kernel(
+    gate_hbm, up_hbm, residual_hbm, out_hbm, gate_ref, up_ref, residual_ref, out_ref, done, sent
+):
     loads = (
         pltpu.make_async_copy(gate_hbm, gate_ref, done.at[0]),
         pltpu.make_async_copy(up_hbm, up_ref, done.at[1]),
@@ -77,11 +87,16 @@
     gate = gate_ref[...].astype(jnp.float32)
     up = up_ref[...].astype(jnp.float32)
     gated = (gate / (1.0 + jnp.exp(-gate)) * up).astype(jnp.bfloat16)
+    stores = []
     for peer in range(count):
         out_ref[peer, :, :units] = gated
         for row in range(rows):
             first = (peer * rows + row) * extra
             out_ref[peer, row : row + 1, units:] = residual_ref[:, first : first + extra]
+        stores.append(pltpu.make_async_copy(out_ref.at[peer], out_hbm.at[peer], sent.at[peer]))
+        stores[-1].start()
+    for store in stores:
+        store.wait()
 
 
 def weight_loads(weight_hbm, weight_ref, done):
@@ -143,10 +158,16 @@
     given_ref[...] = jnp.where(index == 0, high, low)
 
 
-def stream_kernel(kept_ref, arrived_ref, out_ref):
-    stream = (kept_ref[...] + arrived_ref[...]).astype(jnp.bfloat16)
-    for peer in range(out_ref.shape[0]):
-        out_ref[peer] = stream
+def stream_kernel(kept_ref, arrived_ref, out_hbm, stream_ref, sent):
+    stream_ref[...] = (kept_ref[...] + arrived_ref[...]).astype(jnp.bfloat16)
+    stores = [
+        pltpu.make_async_copy(stream_ref, out_hbm.at[peer], sent.at[peer])
+        for peer in range(out_hbm.shape[0])
+    ]
+    for store in stores:
+        store.start()
+    for store in stores:
+        store.wait()
 
 
 def norm_kernel(stream_ref, gain_ref, own_ref, other_ref):
@@ -228,9 +249,12 @@
     chunk = shaped((vocab_count, rows, half_units + extra), jnp.bfloat16)
     operands = (gate_pre, up_pre, residual)
     places = [VECTOR(one.shape, one.dtype) for one in operands]
-    chunks = call(gated_kernel, chunk, operands, [FAR] * 3, places + [DMA((3,))])
+    places += [VECTOR(chunk.shape, chunk.dtype), DMA((3,)), DMA((vocab_count,))]
+    chunks = call(
+        gated_kernel, chunk, operands, [FAR] * 3, places, CHUNKS_GRANT, FREE
+    )
     chunks, down_weight = fence((chunks, down_weight))
-    early = fetched(down_weight, 0, EARLY * step)
+    (early,) = fetched(down_weight, (EARLY * step,))
     chunks = lax.all_to_all(chunks, "vocab", 0, 0, tiled=True)
     chunks, early = fence((chunks, early))
     rest = half_units - EARLY * step
@@ -251,18 +275,32 @@
     chunk = shaped((vocab_count, half_tokens, block), jnp.bfloat16)
     gain = norm_gain.astype(jnp.float32).reshape(vocab_count, block)
     arrived, gain = fence((partner(given), gain))
-    stream = swapped(call(stream_kernel, chunk, (kept, arrived), [NEAR] * 2))
+    stream = call(
+        stream_kernel,
+        chunk,
+        (kept, arrived),
+        [NEAR] * 2,
+        [VECTOR(chunk.shape[1:], chunk.dtype), DMA((vocab_count,))],
+        SMALL,
+        FREE,
+    )
+    stream, head_rows = fence((stream, head_weight.T))
+    early_sizes = (half_width // 2, half_width // 4)
+    early = fetched(head_rows, early_sizes)
+    stream = lax.all_to_all(stream, "vocab", 0, 0, tiled=True)
+    stream, *early = fence((stream, *early))
     part = shaped((half_tokens, half_width), jnp.bfloat16)
     own, other = call(norm_kernel, (part, part), (stream, gain), [NEAR] * 2)
+    rest = half_width - sum(early_sizes)
     mine = call(
         head_kernel,
         shaped((tokens, columns_here + 1), jnp.float32),
-        (own, partner(other), targets, head_weight.T),
-        [NEAR] * 3 + [FAR],
+        (own, partner(other), targets, *early, head_rows),
+        [NEAR] * 5 + [FAR],
         [
-            VECTOR((columns_here, half_width), jnp.bfloat16),
+            VECTOR((columns_here, rest), jnp.bfloat16),
             VECTOR((tokens, half_width), jnp.bfloat16),
-            DMA((half_width // block_of(half_width, 512),)),
+            DMA((rest // block_of(rest, 512),)),
         ],
         grant=12 << 20,
     )

time: 49.3 us -> 50 us (1.014)
  blocking collectives: 18.9 us -> 8.28 us
  waiting for transfers between devices: 10.2 us -> 15.8 us
  starting transfers between devices: 7.66 us -> 11.1 us
  Pallas kernels: 11.3 us -> 13.4 us
    all_to_all x1 -> x0, blocking collectives: 10.6 us -> none  [swapped(): return fence(lax.all_to_all(fence(value), 'vocab', 0, 0, tiled=True))]
    all_to_all x0 -> x1, waiting for transfers between devices: none -> 5.56 us  [body(): stream = lax.all_to_all(stream, 'vocab', 0, 0, tiled=True)]
    all_to_all x0 -> x1, starting transfers between devices: none -> 3.49 us  [body(): stream = lax.all_to_all(stream, 'vocab', 0, 0, tiled=True)]
    pallas_call x7 -> x8, Pallas kernels: 11.3 us -> 13.4 us  [the longest x6 9.65 us: call(): pl.pallas_call(kernel, out_shape=out_shape, in_specs=places, out_specs=re...]
  transfers between devices with their start and end apart: 4 -> 5, of which waited for: 4 -> 5; matrix products, arithmetic and copies ran while one was open for 0% -> 0% of each run, Pallas kernels for 4% -> 8%
where the time goes in v9:
time: 50 us; the launch traced here: 49.5 us
  waiting for transfers between devices  15.8 us (32%)
  Pallas kernels  13.4 us (27%)
  starting transfers between devices  11.1 us (22%)
  blocking collectives  8.28 us (17%)
  other arithmetic  0.7 us (1%)
    pallas_call x6, Pallas kernels, call(): pl.pallas_call(kernel, out_shape=out_shape, in_specs=places, out_specs=re...  9.65 us
    all_to_all x1, blocking collectives, body(): lax.all_to_all(stats, ('vocab', 'mp'), 0, 0, tiled=True, axis_index_group...  8.28 us
    all_to_all x1, starting transfers between devices, body(): chunks = lax.all_to_all(chunks, 'vocab', 0, 0, tiled=True)  7.29 us
    all_to_all x1, waiting for transfers between devices, body(): chunks = lax.all_to_all(chunks, 'vocab', 0, 0, tiled=True)  6.76 us
    all_to_all x1, waiting for transfers between devices, body(): stream = lax.all_to_all(stream, 'vocab', 0, 0, tiled=True)  5.56 us
    pallas_call x2, Pallas kernels, fetched(): pl.pallas_call(kernel, out_shape=tuple((pltpu.VMEM((rows, size), weight.d...  3.75 us
    all_to_all x1, starting transfers between devices, body(): stream = lax.all_to_all(stream, 'vocab', 0, 0, tiled=True)  3.49 us
    ppermute x3, waiting for transfers between devices, partner(): return lax.ppermute(value, 'mp', [(0, 1), (1, 0)])  3.46 us
  transfers between devices with their start and end apart: 5, of which 5 were waited for; matrix products, arithmetic and copies ran while one was open for 0% of the time, Pallas kernels for 8%

profile of v9, /device:TPU:0, one launch (start us, length us, event | category | flops | bytes accessed | tf_op | source)
XLA Modules:
  0.0 49.5 jit_solution(9780184508192754818)
XLA Ops:
  0.0 1.6 %shard_map.73 = bf16[8,2,7680]{2,1,0:T(2,128)(2,1)} custom-call(bf16[2,7168]{1,0:T(2,128)(2,1)} %gate_hbm.1, bf16[2,7168]{1,0:T(2,128)(2,1)} %up_hbm.1, bf16[1,8192]{1,0:T(2,128)(2,1)} %residual_hbm.1), custom_call_target="tpu_custom_call" | custom-call | tf_op jit(solution)/shard_map/pallas_call | solution.py:58
  1.6 7.3 %all-to-all-start = ((bf16[8,2,7680]{2,1,0:T(2,128)(2,1)}), bf16[8,2,7680]{2,1,0:T(2,128)(2,1)S(1)}, u32[]{:S(2)}, u32[]{:S(2)}) async-start(bf16[8,2,7680]{2,1,0:T(2,128)(2,1)} %shard_map.73), calls=%async_computation | async-start | bytes 491520 | tf_op jit(solution)/shard_map/all_to_all | solution.py:258
  8.9 1.9 %shard_map.74.early_ref = bf16[1024,1536]{1,0:T(8,128)(2,1)S(1)} custom-call(bf16[1024,7168]{1,0:T(8,128)(2,1)} %weight_hbm.1), custom_call_target="tpu_custom_call" | custom-call | bytes 6291456 | tf_op jit(solution)/shard_map/pallas_call | solution.py:40
  10.8 0.0 copy-start.1
  10.8 6.8 %all-to-all-done.chunks_ref = bf16[8,2,7680]{2,1,0:T(2,128)(2,1)S(1)} async-done(((bf16[8,2,7680]{2,1,0:T(2,128)(2,1)}), bf16[8,2,7680]{2,1,0:T(2,128)(2,1)S(1)}, u32[]{:S(2)}, u32[]{:S(2)}) %all-to-all-start) | async-done | bytes 245792 | tf_op jit(solution)/shard_map/all_to_all | solution.py:258
  17.6 5.0 %shard_map.75 = (f32[8,1024]{1,0:T(8,128)S(1)}, f32[8,1024]{1,0:T(8,128)S(1)}) custom-call(bf16[8,2,7680]{2,1,0:T(2,128)(2,1)S(1)} %all-to-all-done.chunks_ref, bf16[1024,1536]{1,0:T(8,128)(2,1)S(1)} %shard_map.74.early_ref, bf16[1024,7168]{1,0:T(8,128)(2,1)} %weight_hbm.1), custom_call_target="tpu_custom_call" | custom-call | tf_op jit(solution)/shard_map/pallas_call | solution.py:58
  22.6 0.0 copy-start
  22.6 0.1 collective-permute-start
  22.7 1.2 %collective-permute-done.arrived_ref = f32[8,1024]{1,0:T(8,128)S(1)} collective-permute-done((f32[8,1024]{1,0:T(8,128)S(1)}, f32[8,1024]{1,0:T(8,128)S(1)}, u32[]{:S(2)}, u32[]{:S(2)}) %collective-permute-start) | collective-permute-done | bytes 32800 | tf_op jit(solution)/shard_map/ppermute | solution.py:22
  23.9 0.7 %shard_map.76 = bf16[8,8,1024]{2,1,0:T(8,128)(2,1)} custom-call(f32[8,1024]{1,0:T(8,128)S(1)} %get-tuple-element.28.kept_ref, f32[8,1024]{1,0:T(8,128)S(1)} %collective-permute-done.arrived_ref), custom_call_target="tpu_custom_call" | custom-call | tf_op jit(solution)/shard_map/pallas_call | solution.py:58
  24.6 3.5 %all-to-all-start.1 = ((bf16[8,8,1024]{2,1,0:T(8,128)(2,1)}), bf16[8,8,1024]{2,1,0:T(8,128)(2,1)S(1)}, u32[]{:S(2)}, u32[]{:S(2)}) async-start(bf16[8,8,1024]{2,1,0:T(8,128)(2,1)} %shard_map.76), calls=%async_computation.1 | async-start | bytes 262144 | tf_op jit(solution)/shard_map/all_to_all | solution.py:290
  28.1 1.9 %shard_map.77 = (bf16[504,2048]{1,0:T(8,128)(2,1)S(1)}, bf16[504,1024]{1,0:T(8,128)(2,1)S(1)}) custom-call(bf16[504,4096]{1,0:T(8,128)(2,1)} %bitcast.2), custom_call_target="tpu_custom_call" | custom-call | bytes 6193152 | tf_op jit(solution)/shard_map/pallas_call | solution.py:40
  30.0 5.6 %all-to-all-done.1.stream_ref = bf16[8,8,1024]{2,1,0:T(8,128)(2,1)S(1)} async-done(((bf16[8,8,1024]{2,1,0:T(8,128)(2,1)}), bf16[8,8,1024]{2,1,0:T(8,128)(2,1)S(1)}, u32[]{:S(2)}, u32[]{:S(2)}) %all-to-all-start.1) | async-done | bytes 131104 | tf_op jit(solution)/shard_map/all_to_all | solution.py:290
  35.6 0.1 shard_map.78
  35.7 0.1 collective-permute-start.1
  35.8 1.2 %collective-permute-done.1.other_ref = bf16[8,4096]{1,0:T(8,128)(2,1)S(1)} collective-permute-done((bf16[8,4096]{1,0:T(8,128)(2,1)S(1)}, bf16[8,4096]{1,0:T(8,128)(2,1)S(1)}, u32[]{:S(2)}, u32[]{:S(2)}) %collective-permute-start.1) | collective-permute-done | bytes 65568 | tf_op jit(solution)/shard_map/ppermute | solution.py:22
  37.0 0.0 copy-done
  37.0 2.0 %shard_map.79.mine_ref = f32[16,505]{1,0:T(8,128)S(1)} custom-call(bf16[8,4096]{1,0:T(8,128)(2,1)S(1)} %get-tuple-element.37.own_ref, bf16[8,4096]{1,0:T(8,128)(2,1)S(1)} %collective-permute-done.1.other_ref, s32[8]{0:T(128)S(1)} %copy-done, bf16[504,2048]{1,0:T(8,128)(2,1)S(1)} %get-tuple-element.39.refs_0_, ...), custom_call_target="tpu_custom_call" | custom-call | tf_op jit(solution)/shard_map/pallas_call | solution.py:58
  39.0 0.2 collective-permute-start.2
  39.2 1.1 %collective-permute-done.2.arrived_ref = f32[16,505]{1,0:T(8,128)S(1)} collective-permute-done((f32[16,505]{1,0:T(8,128)S(1)}, f32[16,505]{1,0:T(8,128)S(1)}, u32[]{:S(2)}, u32[]{:S(2)}) %collective-permute-start.2) | collective-permute-done | bytes 32352 | tf_op jit(solution)/shard_map/ppermute | solution.py:22
  40.3 0.2 shard_map.80
  40.5 8.3 %all_to_all.15 = f32[8,1,48]{2,1,0:T(1,128)S(1)} all-to-all(f32[8,1,48]{2,1,0:T(1,128)S(1)} %shard_map.80), channel_id=1, replica_groups={{0,3,4,7,8,11,12,15},{1,2,5,6,9,10,13,14},{16,19,20,23,24,27,28,31},{17..., dimensions={0} | all-to-all | bytes 3072 | tf_op jit(solution)/shard_map/all_to_all | solution.py:316
  48.8 0.1 slice_reduce_fusion
  48.9 0.6 %fusion.1 = f32[8]{0:T(128)} fusion(pred[]{:T(512)S(6)} %eq.3, f32[16]{0:T(128)S(1)} %get-tuple-element.44, f32[16]{0:T(128)S(1)} %slice_reduce_fusion.1, f32[16]{0:T(128)S(1)} %get-tuple-element.43), kind=kLoop, calls=%fused_computation.7 | loop fusion | flops 40 | bytes 225 | tf_op jit(solution)/shard_map/sub | solution.py:327
  (3 shorter events, 0.0 us)
Async XLA Ops:
  1.6 16.0 %all-to-all-start = ((bf16[8,2,7680]{2,1,0:T(2,128)(2,1)}), bf16[8,2,7680]{2,1,0:T(2,128)(2,1)S(1)}, u32[]{:S(2)}, u32[]{:S(2)}) async-start(bf16[8,2,7680]{2,1,0:T(2,128)(2,1)} %shard_map.73), calls=%async_computation | async-start | bytes 491520 | tf_op jit(solution)/shard_map/all_to_all | solution.py:258
  10.8 11.9 %copy-start.1 = (bf16[8192]{0:T(1024)(128)(2,1)S(1)}, bf16[8192]{0:T(1024)(128)(2,1)}, u32[]{:S(2)}) copy-start(bf16[8192]{0:T(1024)(128)(2,1)} %param.11) | copy-start | bytes 49156
  22.6 14.4 %copy-start = (s32[8]{0:T(128)S(1)}, s32[8]{0:T(128)}, u32[]{:S(2)}) copy-start(s32[8]{0:T(128)} %targets_ref.1) | copy-start | bytes 100
  22.6 1.3 %collective-permute-start = (f32[8,1024]{1,0:T(8,128)S(1)}, f32[8,1024]{1,0:T(8,128)S(1)}, u32[]{:S(2)}, u32[]{:S(2)}) collective-permute-start(f32[8,1024]{1,0:T(8,128)S(1)} %get-tuple-element.29), channel_id=1, source_target_pairs={{0,1},{1,0},{2,3},{3,2},{4,5},{5,4},{6,7},{7,6},{8,9},{9,8},{10,11... | collective-permute-start | bytes 98312 | tf_op jit(solution)/shard_map/ppermute | solution.py:22
  24.6 10.9 %all-to-all-start.1 = ((bf16[8,8,1024]{2,1,0:T(8,128)(2,1)}), bf16[8,8,1024]{2,1,0:T(8,128)(2,1)S(1)}, u32[]{:S(2)}, u32[]{:S(2)}) async-start(bf16[8,8,1024]{2,1,0:T(8,128)(2,1)} %shard_map.76), calls=%async_computation.1 | async-start | bytes 262144 | tf_op jit(solution)/shard_map/all_to_all | solution.py:290
  35.7 1.3 %collective-permute-start.1 = (bf16[8,4096]{1,0:T(8,128)(2,1)S(1)}, bf16[8,4096]{1,0:T(8,128)(2,1)S(1)}, u32[]{:S(2)}, u32[]{:S(2)}) collective-permute-start(bf16[8,4096]{1,0:T(8,128)(2,1)S(1)} %get-tuple-element.38), channel_id=1, source_target_pairs={{0,1},{1,0},{2,3},{3,2},{4,5},{5,4},{6,7},{7,6},{8,9},{9,8},{10,11... | collective-permute-start | bytes 196616 | tf_op jit(solution)/shard_map/ppermute | solution.py:22
  39.0 1.3 %collective-permute-start.2 = (f32[16,505]{1,0:T(8,128)S(1)}, f32[16,505]{1,0:T(8,128)S(1)}, u32[]{:S(2)}, u32[]{:S(2)}) collective-permute-start(f32[16,505]{1,0:T(8,128)S(1)} %shard_map.79.mine_ref), channel_id=1, source_target_pairs={{0,1},{1,0},{2,3},{3,2},{4,5},{5,4},{6,7},{7,6},{8,9},{9,8},{10,11... | collective-permute-start | bytes 96968 | tf_op jit(solution)/shard_map/ppermute | solution.py:22

commit v10 on v6

--- a/solution.py
+++ b/solution.py
@@ -8,6 +8,7 @@
 EPSILON = 1e-05
 ROWS_BY_ROWS = (((1,), (1,)), ((), ()))
 SMALL = 2 << 20
+HEAD_PARTS = 2
 fence = lax.optimization_barrier
 NEAR = pl.BlockSpec(memory_space=pltpu.VMEM)
 FAR = pl.BlockSpec(memory_space=pltpu.HBM)
@@ -125,7 +126,7 @@
     mean_square = jnp.sum(squares, axis=1, keepdims=True) / (count * block)
     scale = lax.rsqrt(mean_square + EPSILON)
     index = lax.axis_index("mp")
-    for out_ref, side in ((own_ref, index), (other_ref, 1 - index)):
+    for out_ref, side in ((own_ref, 1 - index), (other_ref, index)):
         for part in range(half):
             at = side * half + part
             gain = gain_ref[pl.ds(at, 1), :]
@@ -143,15 +144,23 @@
     return jnp.sum(jnp.where(diagonal, spread, 0.0), axis=1, keepdims=True)
 
 
-def head_kernel(own_ref, other_ref, targets_ref, weight_hbm, out_ref, weight_ref, halves_ref, done):
-    loads = weight_loads(weight_hbm, weight_ref, done)
+def head_kernel(own_ref, other_ref, targets_ref, weight_ref, out_ref, halves_ref):
     tokens = own_ref.shape[0]
-    columns = weight_ref.shape[0]
+    columns, width = weight_ref.shape
     halves_ref[...] = jnp.concatenate([own_ref[...], other_ref[...]], axis=0)
     out_ref[:tokens, columns:] = column_of(targets_ref)
     out_ref[tokens:, columns:] = jnp.zeros((tokens, 1), jnp.float32)
     terms = jnp.zeros((2 * tokens, columns), jnp.float32)
-    out_ref[:, :columns] = product(terms, halves_ref, weight_ref, loads)
+    depth = width // HEAD_PARTS
+    for part in range(HEAD_PARTS):
+        here = slice(part * depth, (part + 1) * depth)
+        terms += lax.dot_general(
+            halves_ref[:, here],
+            weight_ref[:, here],
+            ROWS_BY_ROWS,
+            preferred_element_type=jnp.float32,
+        )
+    out_ref[:, :columns] = terms
 
 
 def stats_kernel(mine_ref, arrived_ref, out_ref):
@@ -210,22 +219,19 @@
     )
     chunk = shaped((vocab_count, half_tokens, block), jnp.bfloat16)
     gain = norm_gain.astype(jnp.float32).reshape(vocab_count, block)
-    arrived, gain = fence((partner(given), gain))
+    arrived, gain, head_rows = fence((partner(given), gain, head_weight.T))
+    head_rows = partner(head_rows)
     stream = swapped(call(stream_kernel, chunk, (kept, arrived), [NEAR] * 2))
+    stream, head_rows = fence((stream, head_rows))
     part = shaped((half_tokens, half_width), jnp.bfloat16)
     own, other = call(norm_kernel, (part, part), (stream, gain), [NEAR] * 2)
-    step = block_of(half_width, 512)
     mine = call(
         head_kernel,
         shaped((tokens, columns_here + 1), jnp.float32),
-        (own, partner(other), targets, head_weight.T),
-        [NEAR, NEAR, NEAR, FAR],
-        [
-            VECTOR((columns_here, half_width), jnp.bfloat16),
-            VECTOR((tokens, half_width), jnp.bfloat16),
-            DMA((half_width // step,)),
-        ],
-        grant=12 << 20,
+        (own, partner(other), targets, head_rows),
+        [NEAR] * 4,
+        [VECTOR((tokens, half_width), jnp.bfloat16)],
+        grant=8 << 20,
     )
     row = shaped((vocab_count, 1, 3 * tokens), jnp.float32)
     stats = call(stats_kernel, row, (mine, partner(mine)), [NEAR] * 2)

time: 49.1 us -> 48.1 us (0.980)
  Pallas kernels: 9.55 us -> 8.23 us
    pallas_call x6, Pallas kernels: 9.55 us -> 8.23 us  [call(): pl.pallas_call(kernel, out_shape=out_shape, in_specs=places, out_specs=ja...]
    ppermute x3 -> x4, waiting for transfers between devices: 3.46 us -> 3.46 us  [partner(): return lax.ppermute(value, 'mp', [(0, 1), (1, 0)])]
  transfers between devices with their start and end apart: 3 -> 4, of which waited for: 3 -> 3; matrix products, arithmetic and copies ran while one was open for 0% -> 0% of each run, Pallas kernels for 0% -> 0%
where the time goes in v10:
time: 48.1 us; the launch traced here: 47.8 us
  blocking collectives  34.8 us (72%)
  Pallas kernels  8.23 us (17%)
  waiting for transfers between devices  3.46 us (7%)
  other arithmetic  0.7 us (1%)
    all_to_all x2, blocking collectives, swapped(): return fence(lax.all_to_all(fence(value), 'vocab', 0, 0, tiled=True))  26.5 us
    all_to_all x1, blocking collectives, body(): lax.all_to_all(stats, ('vocab', 'mp'), 0, 0, tiled=True, axis_index_group...  8.28 us
    pallas_call x6, Pallas kernels, call(): pl.pallas_call(kernel, out_shape=out_shape, in_specs=places, out_specs=ja...  8.23 us
    ppermute x4, waiting for transfers between devices, partner(): return lax.ppermute(value, 'mp', [(0, 1), (1, 0)])  3.46 us
  transfers between devices with their start and end apart: 4, of which 3 were waited for; matrix products, arithmetic and copies ran while one was open for 0% of the time, Pallas kernels for 0%

profile of v10, /device:TPU:0, one launch (start us, length us, event | category | flops | bytes accessed | tf_op | source)
XLA Modules:
  0.0 47.8 jit_solution(14484814297071128240)
XLA Ops:
  0.0 0.9 %shard_map.73 = bf16[8,2,7680]{2,1,0:T(2,128)(2,1)S(1)} custom-call(bf16[2,7168]{1,0:T(2,128)(2,1)} %gate_hbm.1, bf16[2,7168]{1,0:T(2,128)(2,1)} %up_hbm.1, bf16[1,8192]{1,0:T(2,128)(2,1)} %residual_hbm.1), custom_call_target="tpu_custom_call" | custom-call | tf_op jit(solution)/shard_map/pallas_call | solution.py:32
  0.9 15.8 %all_to_all.15.chunks_ref = bf16[8,2,7680]{2,1,0:T(2,128)(2,1)S(1)} all-to-all(bf16[8,2,7680]{2,1,0:T(2,128)(2,1)S(1)} %shard_map.73), channel_id=1, replica_groups=mesh['groups'=2,'vocab'=8,'mp'=2] {'vocab'}, dimensions={0} | all-to-all | bytes 491520 | tf_op jit(solution)/shard_map/all_to_all | solution.py:24
  16.6 0.0 copy-start.1
  16.6 0.0 copy-start
  16.6 5.8 %shard_map.74 = (f32[8,1024]{1,0:T(8,128)S(1)}, f32[8,1024]{1,0:T(8,128)S(1)}) custom-call(bf16[8,2,7680]{2,1,0:T(2,128)(2,1)S(1)} %all_to_all.15.chunks_ref, bf16[1024,7168]{1,0:T(8,128)(2,1)} %weight_hbm.1), custom_call_target="tpu_custom_call" | custom-call | tf_op jit(solution)/shard_map/pallas_call | solution.py:32
  22.5 0.1 collective-permute-start
  22.6 0.0 copy-done.1
  22.6 1.2 %collective-permute-done.arrived_ref = f32[8,1024]{1,0:T(8,128)S(1)} collective-permute-done((f32[8,1024]{1,0:T(8,128)S(1)}, f32[8,1024]{1,0:T(8,128)S(1)}, u32[]{:S(2)}, u32[]{:S(2)}) %collective-permute-start) | collective-permute-done | bytes 32800 | tf_op jit(solution)/shard_map/ppermute | solution.py:20
  23.8 0.2 collective-permute-start.1
  23.9 10.8 %all_to_all.16.stream_ref = bf16[8,8,1024]{2,1,0:T(8,128)(2,1)S(1)} all-to-all(bf16[8,8,1024]{2,1,0:T(8,128)(2,1)S(1)} %shard_map.75), channel_id=1, replica_groups=mesh['groups'=2,'vocab'=8,'mp'=2] {'vocab'}, dimensions={0} | all-to-all | bytes 262144 | tf_op jit(solution)/shard_map/all_to_all | solution.py:24
  34.7 0.0 collective-permute-done.1.weight_ref
  34.7 0.1 shard_map.76
  34.9 0.1 collective-permute-start.2
  34.9 1.2 %collective-permute-done.2.other_ref = bf16[8,4096]{1,0:T(8,128)(2,1)S(1)} collective-permute-done((bf16[8,4096]{1,0:T(8,128)(2,1)S(1)}, bf16[8,4096]{1,0:T(8,128)(2,1)S(1)}, u32[]{:S(2)}, u32[]{:S(2)}) %collective-permute-start.2) | collective-permute-done | bytes 65568 | tf_op jit(solution)/shard_map/ppermute | solution.py:20
  36.2 0.0 copy-done
  36.2 1.2 %shard_map.77.mine_ref = f32[16,505]{1,0:T(8,128)S(1)} custom-call(bf16[8,4096]{1,0:T(8,128)(2,1)S(1)} %get-tuple-element.22.own_ref, bf16[8,4096]{1,0:T(8,128)(2,1)S(1)} %collective-permute-done.2.other_ref, s32[8]{0:T(128)S(1)} %copy-done, bf16[504,4096]{1,0:T(8,128)(2,1)S(1)} %collective-permute-done.1.weight_ref), custom_call_target="tpu_custom_call" | custom-call | tf_op jit(solution)/shard_map/pallas_call | solution.py:32
  37.4 0.2 collective-permute-start.3
  37.5 1.1 %collective-permute-done.3.arrived_ref = f32[16,505]{1,0:T(8,128)S(1)} collective-permute-done((f32[16,505]{1,0:T(8,128)S(1)}, f32[16,505]{1,0:T(8,128)S(1)}, u32[]{:S(2)}, u32[]{:S(2)}) %collective-permute-start.3) | collective-permute-done | bytes 32352 | tf_op jit(solution)/shard_map/ppermute | solution.py:20
  38.6 0.2 shard_map.78
  38.8 8.3 %all_to_all.17 = f32[8,1,48]{2,1,0:T(1,128)S(1)} all-to-all(f32[8,1,48]{2,1,0:T(1,128)S(1)} %shard_map.78), channel_id=1, replica_groups={{0,3,4,7,8,11,12,15},{1,2,5,6,9,10,13,14},{16,19,20,23,24,27,28,31},{17..., dimensions={0} | all-to-all | bytes 3072 | tf_op jit(solution)/shard_map/all_to_all | solution.py:245
  47.1 0.1 slice_reduce_fusion
  47.2 0.6 %fusion.1 = f32[8]{0:T(128)} fusion(pred[]{:T(512)S(6)} %eq.3, f32[16]{0:T(128)S(1)} %get-tuple-element.28, f32[16]{0:T(128)S(1)} %slice_reduce_fusion.1, f32[16]{0:T(128)S(1)} %get-tuple-element.27), kind=kLoop, calls=%fused_computation.7 | loop fusion | flops 40 | bytes 225 | tf_op jit(solution)/shard_map/sub | solution.py:256
  (3 shorter events, 0.0 us)
Async XLA Ops:
  16.6 5.9 %copy-start.1 = (bf16[8192]{0:T(1024)(128)(2,1)S(1)}, bf16[8192]{0:T(1024)(128)(2,1)}, u32[]{:S(2)}) copy-start(bf16[8192]{0:T(1024)(128)(2,1)} %param.11) | copy-start | bytes 49156
  16.6 19.5 %copy-start = (s32[8]{0:T(128)S(1)}, s32[8]{0:T(128)}, u32[]{:S(2)}) copy-start(s32[8]{0:T(128)} %targets_ref.1) | copy-start | bytes 100
  22.5 1.3 %collective-permute-start = (f32[8,1024]{1,0:T(8,128)S(1)}, f32[8,1024]{1,0:T(8,128)S(1)}, u32[]{:S(2)}, u32[]{:S(2)}) collective-permute-start(f32[8,1024]{1,0:T(8,128)S(1)} %get-tuple-element.17), channel_id=1, source_target_pairs={{0,1},{1,0},{2,3},{3,2},{4,5},{5,4},{6,7},{7,6},{8,9},{9,8},{10,11... | collective-permute-start | bytes 98312 | tf_op jit(solution)/shard_map/ppermute | solution.py:20
  23.8 11.0 %collective-permute-start.1 = (bf16[504,4096]{1,0:T(8,128)(2,1)}, bf16[504,4096]{1,0:T(8,128)(2,1)S(1)}, u32[]{:S(2)}, u32[]{:S(2)}) collective-permute-start(bf16[504,4096]{1,0:T(8,128)(2,1)} %bitcast.4), channel_id=1, source_target_pairs={{0,1},{1,0},{2,3},{3,2},{4,5},{5,4},{6,7},{7,6},{8,9},{9,8},{10,11... | collective-permute-start | bytes 12386312 | tf_op jit(solution)/shard_map/ppermute | solution.py:20
  34.9 1.3 %collective-permute-start.2 = (bf16[8,4096]{1,0:T(8,128)(2,1)S(1)}, bf16[8,4096]{1,0:T(8,128)(2,1)S(1)}, u32[]{:S(2)}, u32[]{:S(2)}) collective-permute-start(bf16[8,4096]{1,0:T(8,128)(2,1)S(1)} %get-tuple-element.23), channel_id=1, source_target_pairs={{0,1},{1,0},{2,3},{3,2},{4,5},{5,4},{6,7},{7,6},{8,9},{9,8},{10,11... | collective-permute-start | bytes 196616 | tf_op jit(solution)/shard_map/ppermute | solution.py:20
  37.4 1.2 %collective-permute-start.3 = (f32[16,505]{1,0:T(8,128)S(1)}, f32[16,505]{1,0:T(8,128)S(1)}, u32[]{:S(2)}, u32[]{:S(2)}) collective-permute-start(f32[16,505]{1,0:T(8,128)S(1)} %shard_map.77.mine_ref), channel_id=1, source_target_pairs={{0,1},{1,0},{2,3},{3,2},{4,5},{5,4},{6,7},{7,6},{8,9},{9,8},{10,11... | collective-permute-start | bytes 96968 | tf_op jit(solution)/shard_map/ppermute | solution.py:20

commit v11 on v10

--- a/solution.py
+++ b/solution.py
@@ -116,65 +116,46 @@
         out_ref[peer] = stream
 
 
-def norm_kernel(stream_ref, gain_ref, own_ref, other_ref):
+def column_of(row_ref):
+    size = row_ref.shape[0]
+    square = (size, size)
+    diagonal = lax.broadcasted_iota(jnp.int32, square, 0) == lax.broadcasted_iota(
+        jnp.int32, square, 1
+    )
+    spread = jnp.broadcast_to(row_ref[...].reshape(1, size), square).astype(jnp.float32)
+    return jnp.sum(jnp.where(diagonal, spread, 0.0), axis=1, keepdims=True)
+
+
+def score_kernel(
+    stream_ref, gain_ref, targets_ref, other_ref, weight_hbm, out_ref, weight_ref, normed_ref, done
+):
+    loads = weight_loads(weight_hbm, weight_ref, done)
     count, tokens, block = stream_ref.shape
-    half = count // 2
+    columns, width = weight_ref.shape
+    blocks = width // block
     squares = jnp.zeros((tokens, block), jnp.float32)
     for part in range(count):
         values = stream_ref[part].astype(jnp.float32)
         squares += values * values
     mean_square = jnp.sum(squares, axis=1, keepdims=True) / (count * block)
     scale = lax.rsqrt(mean_square + EPSILON)
+    for part in range(count):
+        values = stream_ref[part].astype(jnp.float32) * scale * gain_ref[part : part + 1, :]
+        first = part % blocks * block
+        normed_ref[part // blocks, :, first : first + block] = values.astype(jnp.bfloat16)
     index = lax.axis_index("mp")
-    for out_ref, side in ((own_ref, 1 - index), (other_ref, index)):
-        for part in range(half):
-            at = side * half + part
-            gain = gain_ref[pl.ds(at, 1), :]
-            values = stream_ref[at].astype(jnp.float32) * scale * gain
-            out_ref[:, part * block : (part + 1) * block] = values.astype(jnp.bfloat16)
-
-
-def column_of(row_ref):
-    size = row_ref.shape[0]
-    square = (size, size)
-    diagonal = lax.broadcasted_iota(jnp.int32, square, 0) == lax.broadcasted_iota(
-        jnp.int32, square, 1
-    )
-    spread = jnp.broadcast_to(row_ref[...].reshape(1, size), square).astype(jnp.float32)
-    return jnp.sum(jnp.where(diagonal, spread, 0.0), axis=1, keepdims=True)
-
-
-def head_kernel(own_ref, other_ref, targets_ref, weight_ref, out_ref, halves_ref):
-    tokens = own_ref.shape[0]
-    columns, width = weight_ref.shape
-    halves_ref[...] = jnp.concatenate([own_ref[...], other_ref[...]], axis=0)
-    out_ref[:tokens, columns:] = column_of(targets_ref)
-    out_ref[tokens:, columns:] = jnp.zeros((tokens, 1), jnp.float32)
-    terms = jnp.zeros((2 * tokens, columns), jnp.float32)
+    wanted = column_of(targets_ref).astype(jnp.int32) - lax.axis_index("vocab") * columns
+    terms = jnp.zeros((tokens, columns), jnp.float32)
     depth = width // HEAD_PARTS
     for part in range(HEAD_PARTS):
         here = slice(part * depth, (part + 1) * depth)
         terms += lax.dot_general(
-            halves_ref[:, here],
-            weight_ref[:, here],
+            normed_ref[1 - index, :, here],
+            other_ref[:, here],
             ROWS_BY_ROWS,
             preferred_element_type=jnp.float32,
         )
-    out_ref[:, :columns] = terms
-
-
-def stats_kernel(mine_ref, arrived_ref, out_ref):
-    half = mine_ref.shape[0] // 2
-    columns = mine_ref.shape[1] - 1
-    own = mine_ref[:half, :] + arrived_ref[half:, :]
-    other = mine_ref[half:, :] + arrived_ref[:half, :]
-    is_low = lax.axis_index("mp") == 0
-    both = jnp.concatenate(
-        [jnp.where(is_low, own, other), jnp.where(is_low, other, own)], axis=0
-    )
-    logits, wanted = both[:, :columns], both[:, columns:].astype(jnp.int32)
-    tokens = 2 * half
-    wanted -= lax.axis_index("vocab") * columns
+    logits = product(terms, normed_ref.at[index], weight_ref, loads)
     here = lax.broadcasted_iota(jnp.int32, logits.shape, 1) == wanted
     chosen = jnp.sum(jnp.where(here, logits, 0.0), axis=1, keepdims=True)
     top = jnp.max(logits, axis=1, keepdims=True)
@@ -220,40 +201,28 @@
     chunk = shaped((vocab_count, half_tokens, block), jnp.bfloat16)
     gain = norm_gain.astype(jnp.float32).reshape(vocab_count, block)
     arrived, gain, head_rows = fence((partner(given), gain, head_weight.T))
-    head_rows = partner(head_rows)
+    other_rows = partner(head_rows)
     stream = swapped(call(stream_kernel, chunk, (kept, arrived), [NEAR] * 2))
-    stream, head_rows = fence((stream, head_rows))
-    part = shaped((half_tokens, half_width), jnp.bfloat16)
-    own, other = call(norm_kernel, (part, part), (stream, gain), [NEAR] * 2)
-    mine = call(
-        head_kernel,
-        shaped((tokens, columns_here + 1), jnp.float32),
-        (own, partner(other), targets, head_rows),
-        [NEAR] * 4,
-        [VECTOR((tokens, half_width), jnp.bfloat16)],
-        grant=8 << 20,
-    )
-    row = shaped((vocab_count, 1, 3 * tokens), jnp.float32)
-    stats = call(stats_kernel, row, (mine, partner(mine)), [NEAR] * 2)
-    model_count = lax.axis_size("mp")
-    mixed = [
-        [peer * model_count + (peer + core) % model_count for peer in range(vocab_count)]
-        for core in range(model_count)
-    ]
-    stats, is_low = fence((stats, lax.axis_index("mp") == 0))
-    stats = fence(
-        lax.all_to_all(stats, ("vocab", "mp"), 0, 0, tiled=True, axis_index_groups=mixed)
-    )
+    stream, other_rows = fence((stream, other_rows))
+    step = block_of(half_width, 512)
+    row = shaped((vocab_count, 1, 3 * half_tokens), jnp.float32)
+    stats = call(
+        score_kernel,
+        row,
+        (stream, gain, targets, other_rows, head_rows),
+        [NEAR] * 4 + [FAR],
+        [
+            VECTOR((columns_here, half_width), jnp.bfloat16),
+            VECTOR((2, half_tokens, half_width), jnp.bfloat16),
+            DMA((half_width // step,)),
+        ],
+        grant=12 << 20,
+    )
+    stats = swapped(stats)
     tops, totals, chosen = jnp.split(stats[:, 0], 3, axis=1)
     top = jnp.max(tops, axis=0)
     total = jnp.sum(totals * jnp.exp(tops - top[None]), axis=0)
-    chosen = jnp.sum(chosen, axis=0)
-    low, high = (
-        tuple(one[side] for one in (top, total, chosen))
-        for side in (slice(None, half_tokens), slice(half_tokens, None))
-    )
-    top, total, chosen = (jnp.where(is_low, here, there) for here, there in zip(low, high))
-    return chosen - top - jnp.log(total)
+    return jnp.sum(chosen, axis=0) - top - jnp.log(total)
 
 
 def solution(mesh):

time: 48.1 us -> 47.9 us (level)
  waiting for transfers between devices: 3.46 us -> 1.17 us
  Pallas kernels: 8.23 us -> 9.89 us
  blocking collectives: 34.8 us -> 35.5 us
    all_to_all x2 -> x3, blocking collectives: 26.5 us -> 35.5 us  [swapped(): return fence(lax.all_to_all(fence(value), 'vocab', 0, 0, tiled=True))]
    all_to_all x1 -> x0, blocking collectives: 8.28 us -> none  [body(): lax.all_to_all(stats, ('vocab', 'mp'), 0, 0, tiled=True, axis_index_group...]
    ppermute x4 -> x2, waiting for transfers between devices: 3.46 us -> 1.17 us  [partner(): return lax.ppermute(value, 'mp', [(0, 1), (1, 0)])]
    pallas_call x6 -> x4, Pallas kernels: 8.23 us -> 9.89 us  [call(): pl.pallas_call(kernel, out_shape=out_shape, in_specs=places, out_specs=ja...]
  transfers between devices with their start and end apart: 4 -> 2, of which waited for: 3 -> 1; matrix products, arithmetic and copies ran while one was open for 0% -> 0% of each run, Pallas kernels for 0% -> 0%
where the time goes in v11:
time: 47.9 us; the launch traced here: 47.5 us
  blocking collectives  35.5 us (74%)
  Pallas kernels  9.89 us (21%)
  waiting for transfers between devices  1.17 us (2%)
  other arithmetic  0.63 us (1%)
    all_to_all x3, blocking collectives, swapped(): return fence(lax.all_to_all(fence(value), 'vocab', 0, 0, tiled=True))  35.5 us
    pallas_call x4, Pallas kernels, call(): pl.pallas_call(kernel, out_shape=out_shape, in_specs=places, out_specs=ja...  9.89 us
    ppermute x2, waiting for transfers between devices, partner(): return lax.ppermute(value, 'mp', [(0, 1), (1, 0)])  1.17 us
  transfers between devices with their start and end apart: 2, of which 1 were waited for; matrix products, arithmetic and copies ran while one was open for 0% of the time, Pallas kernels for 0%

profile of v11, /device:TPU:0, one launch (start us, length us, event | category | flops | bytes accessed | tf_op | source)
XLA Modules:
  0.0 47.5 jit_solution(11924495633972884189)
XLA Ops:
  0.0 0.9 %shard_map.73 = bf16[8,2,7680]{2,1,0:T(2,128)(2,1)S(1)} custom-call(bf16[2,7168]{1,0:T(2,128)(2,1)} %gate_hbm.1, bf16[2,7168]{1,0:T(2,128)(2,1)} %up_hbm.1, bf16[1,8192]{1,0:T(2,128)(2,1)} %residual_hbm.1), custom_call_target="tpu_custom_call" | custom-call | tf_op jit(solution)/shard_map/pallas_call | solution.py:32
  0.9 15.8 %all_to_all.15.chunks_ref = bf16[8,2,7680]{2,1,0:T(2,128)(2,1)S(1)} all-to-all(bf16[8,2,7680]{2,1,0:T(2,128)(2,1)S(1)} %shard_map.73), channel_id=1, replica_groups=mesh['groups'=2,'vocab'=8,'mp'=2] {'vocab'}, dimensions={0} | all-to-all | bytes 491520 | tf_op jit(solution)/shard_map/all_to_all | solution.py:24
  16.6 0.0 copy-start.1
  16.6 0.0 copy-start
  16.6 5.8 %shard_map.74 = (f32[8,1024]{1,0:T(8,128)S(1)}, f32[8,1024]{1,0:T(8,128)S(1)}) custom-call(bf16[8,2,7680]{2,1,0:T(2,128)(2,1)S(1)} %all_to_all.15.chunks_ref, bf16[1024,7168]{1,0:T(8,128)(2,1)} %weight_hbm.1), custom_call_target="tpu_custom_call" | custom-call | tf_op jit(solution)/shard_map/pallas_call | solution.py:32
  22.5 0.1 collective-permute-start
  22.6 0.0 copy-done.1
  22.6 1.2 %collective-permute-done.arrived_ref = f32[8,1024]{1,0:T(8,128)S(1)} collective-permute-done((f32[8,1024]{1,0:T(8,128)S(1)}, f32[8,1024]{1,0:T(8,128)S(1)}, u32[]{:S(2)}, u32[]{:S(2)}) %collective-permute-start) | collective-permute-done | bytes 32800 | tf_op jit(solution)/shard_map/ppermute | solution.py:20
  23.8 0.2 collective-permute-start.1
  23.9 10.8 %all_to_all.16.stream_ref = bf16[8,8,1024]{2,1,0:T(8,128)(2,1)S(1)} all-to-all(bf16[8,8,1024]{2,1,0:T(8,128)(2,1)S(1)} %shard_map.75), channel_id=1, replica_groups=mesh['groups'=2,'vocab'=8,'mp'=2] {'vocab'}, dimensions={0} | all-to-all | bytes 262144 | tf_op jit(solution)/shard_map/all_to_all | solution.py:24
  34.7 0.0 collective-permute-done.1.other_ref
  34.7 0.0 copy-done
  34.7 3.2 %shard_map.76 = f32[8,1,24]{2,1,0:T(1,128)S(1)} custom-call(bf16[8,8,1024]{2,1,0:T(8,128)(2,1)S(1)} %all_to_all.16.stream_ref, f32[8,1024]{1,0:T(8,128)S(1)} %reshape.10.gain_ref, s32[8]{0:T(128)S(1)} %copy-done, bf16[504,4096]{1,0:T(8,128)(2,1)S(1)} %collective-permute-done.1.other_ref, bf16[504,4096]{1,0:T(8,128)(2,1)} %bitcast.3), custom_call_target="tpu_custom_call" | custom-call | tf_op jit(solution)/shard_map/pallas_call | solution.py:32
  37.9 9.0 %all_to_all.17 = f32[8,1,24]{2,1,0:T(1,128)S(1)} all-to-all(f32[8,1,24]{2,1,0:T(1,128)S(1)} %shard_map.76), channel_id=1, replica_groups=mesh['groups'=2,'vocab'=8,'mp'=2] {'vocab'}, dimensions={0} | all-to-all | bytes 1536 | tf_op jit(solution)/shard_map/all_to_all | solution.py:24
  46.9 0.1 slice_reduce_fusion
  47.0 0.5 %log_subtract_fusion = f32[8]{0:T(128)} fusion(f32[8]{0:T(128)S(1)} %get-tuple-element.20, f32[8]{0:T(128)S(1)} %get-tuple-element.19, f32[8]{0:T(128)S(1)} %slice_reduce_fusion.1), kind=kLoop, calls=%fused_computation.3 | loop fusion | flops 16 | bytes 128 | tf_op jit(solution)/shard_map/sub | solution.py:225
  (3 shorter events, 0.0 us)
Async XLA Ops:
  16.6 5.9 %copy-start.1 = (bf16[8192]{0:T(1024)(128)(2,1)S(1)}, bf16[8192]{0:T(1024)(128)(2,1)}, u32[]{:S(2)}) copy-start(bf16[8192]{0:T(1024)(128)(2,1)} %param.11) | copy-start | bytes 49156
  16.6 18.1 %copy-start = (s32[8]{0:T(128)S(1)}, s32[8]{0:T(128)}, u32[]{:S(2)}) copy-start(s32[8]{0:T(128)} %targets_ref.1) | copy-start | bytes 100
  22.5 1.3 %collective-permute-start = (f32[8,1024]{1,0:T(8,128)S(1)}, f32[8,1024]{1,0:T(8,128)S(1)}, u32[]{:S(2)}, u32[]{:S(2)}) collective-permute-start(f32[8,1024]{1,0:T(8,128)S(1)} %get-tuple-element.13), channel_id=1, source_target_pairs={{0,1},{1,0},{2,3},{3,2},{4,5},{5,4},{6,7},{7,6},{8,9},{9,8},{10,11... | collective-permute-start | bytes 98312 | tf_op jit(solution)/shard_map/ppermute | solution.py:20
  23.8 11.0 %collective-permute-start.1 = (bf16[504,4096]{1,0:T(8,128)(2,1)}, bf16[504,4096]{1,0:T(8,128)(2,1)S(1)}, u32[]{:S(2)}, u32[]{:S(2)}) collective-permute-start(bf16[504,4096]{1,0:T(8,128)(2,1)} %bitcast.2), channel_id=1, source_target_pairs={{0,1},{1,0},{2,3},{3,2},{4,5},{5,4},{6,7},{7,6},{8,9},{9,8},{10,11... | collective-permute-start | bytes 12386312 | tf_op jit(solution)/shard_map/ppermute | solution.py:20

commit v12 on v10

--- a/solution.py
+++ b/solution.py
@@ -14,6 +14,21 @@
 FAR = pl.BlockSpec(memory_space=pltpu.HBM)
 VECTOR = pltpu.VMEM
 DMA = pltpu.SemaphoreType.DMA
+
+
+def mixed_groups():
+    count, cores = lax.axis_size("vocab"), lax.axis_size("mp")
+    return [[peer * cores + (peer + core) % cores for peer in range(count)] for core in range(cores)]
+
+
+def group_index():
+    return lax.rem(lax.axis_index("mp") + lax.axis_index("vocab"), 2)
+
+
+def mixed_swap(value):
+    return lax.all_to_all(
+        value, ("vocab", "mp"), 0, 0, tiled=True, axis_index_groups=mixed_groups()
+    )
 
 
 def partner(value):
@@ -106,8 +121,9 @@
         own_ref[peer * rows : (peer + 1) * rows, :] = jnp.where(token == index, residual, 0.0)
     terms = product(own_ref[...], units_ref, weight_ref, loads)
     low, high = terms[:half], terms[half:]
-    kept_ref[...] = jnp.where(index == 0, low, high)
-    given_ref[...] = jnp.where(index == 0, high, low)
+    is_low = group_index() == 0
+    kept_ref[...] = jnp.where(is_low, low, high)
+    given_ref[...] = jnp.where(is_low, high, low)
 
 
 def stream_kernel(kept_ref, arrived_ref, out_ref):
@@ -148,8 +164,10 @@
     tokens = own_ref.shape[0]
     columns, width = weight_ref.shape
     halves_ref[...] = jnp.concatenate([own_ref[...], other_ref[...]], axis=0)
-    out_ref[:tokens, columns:] = column_of(targets_ref)
-    out_ref[tokens:, columns:] = jnp.zeros((tokens, 1), jnp.float32)
+    wanted = column_of(targets_ref)
+    mine = group_index() == lax.axis_index("mp")
+    out_ref[:tokens, columns:] = jnp.where(mine, wanted, 0.0)
+    out_ref[tokens:, columns:] = jnp.where(mine, 0.0, wanted)
     terms = jnp.zeros((2 * tokens, columns), jnp.float32)
     depth = width // HEAD_PARTS
     for part in range(HEAD_PARTS):
@@ -168,7 +186,7 @@
     columns = mine_ref.shape[1] - 1
     own = mine_ref[:half, :] + arrived_ref[half:, :]
     other = mine_ref[half:, :] + arrived_ref[:half, :]
-    is_low = lax.axis_index("mp") == 0
+    is_low = group_index() == 0
     both = jnp.concatenate(
         [jnp.where(is_low, own, other), jnp.where(is_low, other, own)], axis=0
     )
@@ -221,7 +239,8 @@
     gain = norm_gain.astype(jnp.float32).reshape(vocab_count, block)
     arrived, gain, head_rows = fence((partner(given), gain, head_weight.T))
     head_rows = partner(head_rows)
-    stream = swapped(call(stream_kernel, chunk, (kept, arrived), [NEAR] * 2))
+    stream = fence(call(stream_kernel, chunk, (kept, arrived), [NEAR] * 2))
+    stream = mixed_swap(stream)
     stream, head_rows = fence((stream, head_rows))
     part = shaped((half_tokens, half_width), jnp.bfloat16)
     own, other = call(norm_kernel, (part, part), (stream, gain), [NEAR] * 2)
@@ -235,15 +254,8 @@
     )
     row = shaped((vocab_count, 1, 3 * tokens), jnp.float32)
     stats = call(stats_kernel, row, (mine, partner(mine)), [NEAR] * 2)
-    model_count = lax.axis_size("mp")
-    mixed = [
-        [peer * model_count + (peer + core) % model_count for peer in range(vocab_count)]
-        for core in range(model_count)
-    ]
     stats, is_low = fence((stats, lax.axis_index("mp") == 0))
-    stats = fence(
-        lax.all_to_all(stats, ("vocab", "mp"), 0, 0, tiled=True, axis_index_groups=mixed)
-    )
+    stats = fence(mixed_swap(stats))
     tops, totals, chosen = jnp.split(stats[:, 0], 3, axis=1)
     top = jnp.max(tops, axis=0)
     total = jnp.sum(totals * jnp.exp(tops - top[None]), axis=0)

time: 48.1 us -> 48.2 us (level)
  starting transfers between devices: 0.48 us -> 1 us
  waiting for transfers between devices: 3.46 us -> 2.94 us
    all_to_all x1 -> x2, blocking collectives: 8.28 us -> 19.2 us  [mixed_swap(): lax.all_to_all(value, ('vocab', 'mp'), 0, 0, tiled=True, axis_index_group...]
    all_to_all x2 -> x1, blocking collectives: 26.5 us -> 15.8 us  [swapped(): return fence(lax.all_to_all(fence(value), 'vocab', 0, 0, tiled=True))]
    ppermute x4, starting transfers between devices: 0.48 us -> 1 us  [partner(): return lax.ppermute(value, 'mp', [(0, 1), (1, 0)])]
    ppermute x4, waiting for transfers between devices: 3.46 us -> 2.94 us  [partner(): return lax.ppermute(value, 'mp', [(0, 1), (1, 0)])]
where the time goes in v12:
time: 48.2 us; the launch traced here: 48 us
  blocking collectives  35 us (73%)
  Pallas kernels  8.23 us (17%)
  waiting for transfers between devices  2.94 us (6%)
  starting transfers between devices  1 us (2%)
  other arithmetic  0.7 us (1%)
    all_to_all x2, blocking collectives, mixed_swap(): lax.all_to_all(value, ('vocab', 'mp'), 0, 0, tiled=True, axis_index_group...  19.2 us
    all_to_all x1, blocking collectives, swapped(): return fence(lax.all_to_all(fence(value), 'vocab', 0, 0, tiled=True))  15.8 us
    pallas_call x6, Pallas kernels, call(): pl.pallas_call(kernel, out_shape=out_shape, in_specs=places, out_specs=ja...  8.23 us
    ppermute x4, waiting for transfers between devices, partner(): return lax.ppermute(value, 'mp', [(0, 1), (1, 0)])  2.94 us
    ppermute x4, starting transfers between devices, partner(): return lax.ppermute(value, 'mp', [(0, 1), (1, 0)])  1 us
  transfers between devices with their start and end apart: 4, of which 3 were waited for; matrix products, arithmetic and copies ran while one was open for 0% of the time, Pallas kernels for 0%

profile of v12, /device:TPU:0, one launch (start us, length us, event | category | flops | bytes accessed | tf_op | source)
XLA Modules:
  0.0 48.0 jit_solution(9341457441103029473)
XLA Ops:
  0.0 0.9 %shard_map.73 = bf16[8,2,7680]{2,1,0:T(2,128)(2,1)S(1)} custom-call(bf16[2,7168]{1,0:T(2,128)(2,1)} %gate_hbm.1, bf16[2,7168]{1,0:T(2,128)(2,1)} %up_hbm.1, bf16[1,8192]{1,0:T(2,128)(2,1)} %residual_hbm.1), custom_call_target="tpu_custom_call" | custom-call | tf_op jit(solution)/shard_map/pallas_call | solution.py:47
  0.9 15.8 %all_to_all.15.chunks_ref = bf16[8,2,7680]{2,1,0:T(2,128)(2,1)S(1)} all-to-all(bf16[8,2,7680]{2,1,0:T(2,128)(2,1)S(1)} %shard_map.73), channel_id=1, replica_groups=mesh['groups'=2,'vocab'=8,'mp'=2] {'vocab'}, dimensions={0} | all-to-all | bytes 491520 | tf_op jit(solution)/shard_map/all_to_all | solution.py:39
  16.6 0.0 copy-start.1
  16.6 0.0 copy-start
  16.6 5.8 %shard_map.74 = (f32[8,1024]{1,0:T(8,128)S(1)}, f32[8,1024]{1,0:T(8,128)S(1)}) custom-call(bf16[8,2,7680]{2,1,0:T(2,128)(2,1)S(1)} %all_to_all.15.chunks_ref, bf16[1024,7168]{1,0:T(8,128)(2,1)} %weight_hbm.1), custom_call_target="tpu_custom_call" | custom-call | tf_op jit(solution)/shard_map/pallas_call | solution.py:47
  22.5 0.1 collective-permute-start
  22.6 0.0 copy-done.1
  22.6 1.2 %collective-permute-done.arrived_ref = f32[8,1024]{1,0:T(8,128)S(1)} collective-permute-done((f32[8,1024]{1,0:T(8,128)S(1)}, f32[8,1024]{1,0:T(8,128)S(1)}, u32[]{:S(2)}, u32[]{:S(2)}) %collective-permute-start) | collective-permute-done | bytes 32800 | tf_op jit(solution)/shard_map/ppermute | solution.py:35
  23.8 0.2 collective-permute-start.1
  23.9 10.5 %all_to_all.16.stream_ref = bf16[8,8,1024]{2,1,0:T(8,128)(2,1)S(1)} all-to-all(bf16[8,8,1024]{2,1,0:T(8,128)(2,1)S(1)} %shard_map.75), channel_id=1, replica_groups={{0,3,4,7,8,11,12,15},{1,2,5,6,9,10,13,14},{16,19,20,23,24,27,28,31},{17..., dimensions={0} | all-to-all | bytes 262144 | tf_op jit(solution)/shard_map/all_to_all | solution.py:29
  34.5 0.0 collective-permute-done.1.weight_ref
  34.5 0.1 shard_map.76
  34.6 0.4 collective-permute-start.2
  35.0 0.9 %collective-permute-done.2.other_ref = bf16[8,4096]{1,0:T(8,128)(2,1)S(1)} collective-permute-done((bf16[8,4096]{1,0:T(8,128)(2,1)S(1)}, bf16[8,4096]{1,0:T(8,128)(2,1)S(1)}, u32[]{:S(2)}, u32[]{:S(2)}) %collective-permute-start.2) | collective-permute-done | bytes 65568 | tf_op jit(solution)/shard_map/ppermute | solution.py:35
  35.9 0.0 copy-done
  35.9 1.2 %shard_map.77.mine_ref = f32[16,505]{1,0:T(8,128)S(1)} custom-call(bf16[8,4096]{1,0:T(8,128)(2,1)S(1)} %get-tuple-element.22.own_ref, bf16[8,4096]{1,0:T(8,128)(2,1)S(1)} %collective-permute-done.2.other_ref, s32[8]{0:T(128)S(1)} %copy-done, bf16[504,4096]{1,0:T(8,128)(2,1)S(1)} %collective-permute-done.1.weight_ref), custom_call_target="tpu_custom_call" | custom-call | tf_op jit(solution)/shard_map/pallas_call | solution.py:47
  37.1 0.4 collective-permute-start.3
  37.5 0.9 %collective-permute-done.3.arrived_ref = f32[16,505]{1,0:T(8,128)S(1)} collective-permute-done((f32[16,505]{1,0:T(8,128)S(1)}, f32[16,505]{1,0:T(8,128)S(1)}, u32[]{:S(2)}, u32[]{:S(2)}) %collective-permute-start.3) | collective-permute-done | bytes 32352 | tf_op jit(solution)/shard_map/ppermute | solution.py:35
  38.3 0.2 shard_map.78
  38.5 8.7 %all_to_all.17 = f32[8,1,48]{2,1,0:T(1,128)S(1)} all-to-all(f32[8,1,48]{2,1,0:T(1,128)S(1)} %shard_map.78), channel_id=1, replica_groups={{0,3,4,7,8,11,12,15},{1,2,5,6,9,10,13,14},{16,19,20,23,24,27,28,31},{17..., dimensions={0} | all-to-all | bytes 3072 | tf_op jit(solution)/shard_map/all_to_all | solution.py:29
  47.3 0.1 slice_reduce_fusion
  47.4 0.6 %fusion.1 = f32[8]{0:T(128)} fusion(pred[]{:T(512)S(6)} %eq.3, f32[16]{0:T(128)S(1)} %get-tuple-element.28, f32[16]{0:T(128)S(1)} %slice_reduce_fusion.1, f32[16]{0:T(128)S(1)} %get-tuple-element.27), kind=kLoop, calls=%fused_computation.7 | loop fusion | flops 40 | bytes 225 | tf_op jit(solution)/shard_map/sub | solution.py:268
  (3 shorter events, 0.0 us)
Async XLA Ops:
  16.6 5.9 %copy-start.1 = (bf16[8192]{0:T(1024)(128)(2,1)S(1)}, bf16[8192]{0:T(1024)(128)(2,1)}, u32[]{:S(2)}) copy-start(bf16[8192]{0:T(1024)(128)(2,1)} %param.11) | copy-start | bytes 49156
  16.6 19.3 %copy-start = (s32[8]{0:T(128)S(1)}, s32[8]{0:T(128)}, u32[]{:S(2)}) copy-start(s32[8]{0:T(128)} %targets_ref.1) | copy-start | bytes 100
  22.5 1.3 %collective-permute-start = (f32[8,1024]{1,0:T(8,128)S(1)}, f32[8,1024]{1,0:T(8,128)S(1)}, u32[]{:S(2)}, u32[]{:S(2)}) collective-permute-start(f32[8,1024]{1,0:T(8,128)S(1)} %get-tuple-element.17), channel_id=1, source_target_pairs={{0,1},{1,0},{2,3},{3,2},{4,5},{5,4},{6,7},{7,6},{8,9},{9,8},{10,11... | collective-permute-start | bytes 98312 | tf_op jit(solution)/shard_map/ppermute | solution.py:35
  23.8 10.7 %collective-permute-start.1 = (bf16[504,4096]{1,0:T(8,128)(2,1)}, bf16[504,4096]{1,0:T(8,128)(2,1)S(1)}, u32[]{:S(2)}, u32[]{:S(2)}) collective-permute-start(bf16[504,4096]{1,0:T(8,128)(2,1)} %bitcast.4), channel_id=1, source_target_pairs={{0,1},{1,0},{2,3},{3,2},{4,5},{5,4},{6,7},{7,6},{8,9},{9,8},{10,11... | collective-permute-start | bytes 12386312 | tf_op jit(solution)/shard_map/ppermute | solution.py:35
  34.6 1.3 %collective-permute-start.2 = (bf16[8,4096]{1,0:T(8,128)(2,1)S(1)}, bf16[8,4096]{1,0:T(8,128)(2,1)S(1)}, u32[]{:S(2)}, u32[]{:S(2)}) collective-permute-start(bf16[8,4096]{1,0:T(8,128)(2,1)S(1)} %get-tuple-element.23), channel_id=1, source_target_pairs={{0,1},{1,0},{2,3},{3,2},{4,5},{5,4},{6,7},{7,6},{8,9},{9,8},{10,11... | collective-permute-start | bytes 196616 | tf_op jit(solution)/shard_map/ppermute | solution.py:35
  37.1 1.2 %collective-permute-start.3 = (f32[16,505]{1,0:T(8,128)S(1)}, f32[16,505]{1,0:T(8,128)S(1)}, u32[]{:S(2)}, u32[]{:S(2)}) collective-permute-start(f32[16,505]{1,0:T(8,128)S(1)} %shard_map.77.mine_ref), channel_id=1, source_target_pairs={{0,1},{1,0},{2,3},{3,2},{4,5},{5,4},{6,7},{7,6},{8,9},{9,8},{10,11... | collective-permute-start | bytes 96968 | tf_op jit(solution)/shard_map/ppermute | solution.py:35

commit v13 on v11

--- a/solution.py
+++ b/solution.py
@@ -43,7 +43,9 @@
     return max(size for size in range(1, most + 1) if length % size == 0)
 
 
-def gated_kernel(gate_hbm, up_hbm, residual_hbm, out_ref, gate_ref, up_ref, residual_ref, done):
+def gated_kernel(
+    gate_hbm, up_hbm, residual_hbm, weight_hbm, out_ref, gate_ref, up_ref, residual_ref, done
+):
     loads = (
         pltpu.make_async_copy(gate_hbm, gate_ref, done.at[0]),
         pltpu.make_async_copy(up_hbm, up_ref, done.at[1]),
@@ -92,9 +94,8 @@
     return terms
 
 
-def down_kernel(chunks_ref, weight_hbm, kept_ref, given_ref, weight_ref, units_ref, own_ref, done):
-    loads = weight_loads(weight_hbm, weight_ref, done)
-    units = weight_hbm.shape[1]
+def down_kernel(chunks_ref, weight_ref, kept_ref, given_ref, units_ref, own_ref):
+    units = weight_ref.shape[1]
     count, rows, width = chunks_ref.shape
     half, block = kept_ref.shape
     index = lax.axis_index("mp")
@@ -104,13 +105,21 @@
         pieces = [chunks_ref[peer, row : row + 1, units:].astype(jnp.float32) for row in range(rows)]
         residual = jnp.broadcast_to(jnp.concatenate(pieces, axis=1), (rows, block))
         own_ref[peer * rows : (peer + 1) * rows, :] = jnp.where(token == index, residual, 0.0)
-    terms = product(own_ref[...], units_ref, weight_ref, loads)
+    terms = own_ref[...]
+    depth = block_of(units, 1024)
+    for first in range(0, units, depth):
+        terms += lax.dot_general(
+            units_ref[:, first : first + depth],
+            weight_ref[:, first : first + depth],
+            ROWS_BY_ROWS,
+            preferred_element_type=jnp.float32,
+        )
     low, high = terms[:half], terms[half:]
     kept_ref[...] = jnp.where(index == 0, low, high)
     given_ref[...] = jnp.where(index == 0, high, low)
 
 
-def stream_kernel(kept_ref, arrived_ref, out_ref):
+def stream_kernel(kept_ref, arrived_ref, weight_hbm, out_ref):
     stream = (kept_ref[...] + arrived_ref[...]).astype(jnp.bfloat16)
     for peer in range(out_ref.shape[0]):
         out_ref[peer] = stream
@@ -127,9 +136,8 @@
 
 
 def score_kernel(
-    stream_ref, gain_ref, targets_ref, other_ref, weight_hbm, out_ref, weight_ref, normed_ref, done
+    stream_ref, gain_ref, targets_ref, other_ref, weight_ref, out_ref, normed_ref
 ):
-    loads = weight_loads(weight_hbm, weight_ref, done)
     count, tokens, block = stream_ref.shape
     columns, width = weight_ref.shape
     blocks = width // block
@@ -149,13 +157,14 @@
     depth = width // HEAD_PARTS
     for part in range(HEAD_PARTS):
         here = slice(part * depth, (part + 1) * depth)
-        terms += lax.dot_general(
-            normed_ref[1 - index, :, here],
-            other_ref[:, here],
-            ROWS_BY_ROWS,
-            preferred_element_type=jnp.float32,
-        )
-    logits = product(terms, normed_ref.at[index], weight_ref, loads)
+        for side, half_ref in ((index, weight_ref), (1 - index, other_ref)):
+            terms += lax.dot_general(
+                normed_ref[side, :, here],
+                half_ref[:, here],
+                ROWS_BY_ROWS,
+                preferred_element_type=jnp.float32,
+            )
+    logits = terms
     here = lax.broadcasted_iota(jnp.int32, logits.shape, 1) == wanted
     chosen = jnp.sum(jnp.where(here, logits, 0.0), axis=1, keepdims=True)
     top = jnp.max(logits, axis=1, keepdims=True)
@@ -183,40 +192,41 @@
     chunk = shaped((vocab_count, rows, half_units + extra), jnp.bfloat16)
     operands = (gate_pre, up_pre, residual)
     places = [VECTOR(one.shape, one.dtype) for one in operands]
-    chunks = swapped(call(gated_kernel, chunk, operands, [FAR] * 3, places + [DMA((3,))]))
+    chunks = swapped(
+        call(
+            gated_kernel,
+            chunk,
+            operands + (down_weight,),
+            [FAR] * 4,
+            places + [DMA((3,))],
+        )
+    )
     part = shaped((half_tokens, block), jnp.float32)
     kept, given = call(
         down_kernel,
         (part, part),
         (chunks, down_weight),
-        [NEAR, FAR],
+        [NEAR, NEAR],
         [
-            VECTOR(down_weight.shape, jnp.bfloat16),
             VECTOR((tokens, half_units), jnp.bfloat16),
             VECTOR((tokens, block), jnp.float32),
-            DMA((half_units // step,)),
         ],
-        grant=24 << 20,
+        grant=8 << 20,
     )
     chunk = shaped((vocab_count, half_tokens, block), jnp.bfloat16)
     gain = norm_gain.astype(jnp.float32).reshape(vocab_count, block)
     arrived, gain, head_rows = fence((partner(given), gain, head_weight.T))
     other_rows = partner(head_rows)
-    stream = swapped(call(stream_kernel, chunk, (kept, arrived), [NEAR] * 2))
+    stream = swapped(call(stream_kernel, chunk, (kept, arrived, head_rows), [NEAR] * 2 + [FAR]))
     stream, other_rows = fence((stream, other_rows))
-    step = block_of(half_width, 512)
     row = shaped((vocab_count, 1, 3 * half_tokens), jnp.float32)
     stats = call(
         score_kernel,
         row,
         (stream, gain, targets, other_rows, head_rows),
-        [NEAR] * 4 + [FAR],
-        [
-            VECTOR((columns_here, half_width), jnp.bfloat16),
-            VECTOR((2, half_tokens, half_width), jnp.bfloat16),
-            DMA((half_width // step,)),
-        ],
-        grant=12 << 20,
+        [NEAR] * 5,
+        [VECTOR((2, half_tokens, half_width), jnp.bfloat16)],
+        grant=8 << 20,
     )
     stats = swapped(stats)
     tops, totals, chosen = jnp.split(stats[:, 0], 3, axis=1)

time: 47.9 us -> 45.7 us (0.954)
  Pallas kernels: 9.89 us -> 7.45 us
    pallas_call x4, Pallas kernels: 9.89 us -> 7.45 us  [call(): pl.pallas_call(kernel, out_shape=out_shape, in_specs=places, out_specs=ja...]
where the time goes in v13:
time: 45.7 us; the launch traced here: 45.4 us
  blocking collectives  35.9 us (79%)
  Pallas kernels  7.45 us (16%)
  waiting for transfers between devices  1.16 us (3%)
  other arithmetic  0.63 us (1%)
    all_to_all x3, blocking collectives, swapped(): return fence(lax.all_to_all(fence(value), 'vocab', 0, 0, tiled=True))  35.9 us
    pallas_call x4, Pallas kernels, call(): pl.pallas_call(kernel, out_shape=out_shape, in_specs=places, out_specs=ja...  7.45 us
    ppermute x2, waiting for transfers between devices, partner(): return lax.ppermute(value, 'mp', [(0, 1), (1, 0)])  1.16 us
  transfers between devices with their start and end apart: 2, of which 1 were waited for; matrix products, arithmetic and copies ran while one was open for 0% of the time, Pallas kernels for 0%

profile of v13, /device:TPU:0, one launch (start us, length us, event | category | flops | bytes accessed | tf_op | source)
XLA Modules:
  0.0 45.4 jit_solution(12980267606928000854)
XLA Ops:
  0.0 0.0 copy-start
  0.0 1.0 %shard_map.73 = bf16[8,2,7680]{2,1,0:T(2,128)(2,1)S(1)} custom-call(bf16[2,7168]{1,0:T(2,128)(2,1)} %gate_hbm.1, bf16[2,7168]{1,0:T(2,128)(2,1)} %up_hbm.1, bf16[1,8192]{1,0:T(2,128)(2,1)} %residual_hbm.1, bf16[1024,7168]{1,0:T(8,128)(2,1)} %weight_ref.1), custom_call_target="tpu_custom_call" | custom-call | tf_op jit(solution)/shard_map/pallas_call | solution.py:32
  1.0 16.0 %all_to_all.15.chunks_ref = bf16[8,2,7680]{2,1,0:T(2,128)(2,1)S(1)} all-to-all(bf16[8,2,7680]{2,1,0:T(2,128)(2,1)S(1)} %shard_map.73), channel_id=1, replica_groups=mesh['groups'=2,'vocab'=8,'mp'=2] {'vocab'}, dimensions={0} | all-to-all | bytes 491520 | tf_op jit(solution)/shard_map/all_to_all | solution.py:24
  17.1 0.0 copy-done
  17.1 0.0 copy-start.3
  17.1 3.9 %shard_map.74 = (f32[8,1024]{1,0:T(8,128)S(1)}, f32[8,1024]{1,0:T(8,128)S(1)}) custom-call(bf16[8,2,7680]{2,1,0:T(2,128)(2,1)S(1)} %all_to_all.15.chunks_ref, bf16[1024,7168]{1,0:T(8,128)(2,1)S(1)} %copy-done), custom_call_target="tpu_custom_call" | custom-call | tf_op jit(solution)/shard_map/pallas_call | solution.py:32
  21.0 0.0 copy-start.2
  21.0 0.0 collective-permute-start
  21.0 0.0 copy-done.3
  21.0 0.0 copy-start.1
  21.0 1.2 %collective-permute-done.arrived_ref = f32[8,1024]{1,0:T(8,128)S(1)} collective-permute-done((f32[8,1024]{1,0:T(8,128)S(1)}, f32[8,1024]{1,0:T(8,128)S(1)}, u32[]{:S(2)}, u32[]{:S(2)}) %collective-permute-start) | collective-permute-done | bytes 32800 | tf_op jit(solution)/shard_map/ppermute | solution.py:20
  22.2 0.2 collective-permute-start.1
  22.4 10.9 %all_to_all.16.stream_ref = bf16[8,8,1024]{2,1,0:T(8,128)(2,1)S(1)} all-to-all(bf16[8,8,1024]{2,1,0:T(8,128)(2,1)S(1)} %shard_map.75), channel_id=1, replica_groups=mesh['groups'=2,'vocab'=8,'mp'=2] {'vocab'}, dimensions={0} | all-to-all | bytes 262144 | tf_op jit(solution)/shard_map/all_to_all | solution.py:24
  33.3 0.0 collective-permute-done.1.other_ref
  33.3 0.0 copy-done.2
  33.3 0.0 copy-done.1
  33.3 2.5 %shard_map.76 = f32[8,1,24]{2,1,0:T(1,128)S(1)} custom-call(bf16[8,8,1024]{2,1,0:T(8,128)(2,1)S(1)} %all_to_all.16.stream_ref, f32[8,1024]{1,0:T(8,128)S(1)} %reshape.10.gain_ref, s32[8]{0:T(128)S(1)} %copy-done.2, bf16[504,4096]{1,0:T(8,128)(2,1)S(1)} %collective-permute-done.1.other_ref, bf16[504,4096]{1,0:T(8,128)(2,1)S(1)} %bitcast.4), custom_call_target="tpu_custom_call" | custom-call | tf_op jit(solution)/shard_map/pallas_call | solution.py:32
  35.8 9.0 %all_to_all.17 = f32[8,1,24]{2,1,0:T(1,128)S(1)} all-to-all(f32[8,1,24]{2,1,0:T(1,128)S(1)} %shard_map.76), channel_id=1, replica_groups=mesh['groups'=2,'vocab'=8,'mp'=2] {'vocab'}, dimensions={0} | all-to-all | bytes 1536 | tf_op jit(solution)/shard_map/all_to_all | solution.py:24
  44.8 0.1 slice_reduce_fusion
  44.9 0.5 %log_subtract_fusion = f32[8]{0:T(128)} fusion(f32[8]{0:T(128)S(1)} %get-tuple-element.20, f32[8]{0:T(128)S(1)} %get-tuple-element.19, f32[8]{0:T(128)S(1)} %slice_reduce_fusion.1), kind=kLoop, calls=%fused_computation.3 | loop fusion | flops 16 | bytes 128 | tf_op jit(solution)/shard_map/sub | solution.py:235
  (3 shorter events, 0.0 us)
Async XLA Ops:
  0.0 17.1 %copy-start = (bf16[1024,7168]{1,0:T(8,128)(2,1)S(1)}, bf16[1024,7168]{1,0:T(8,128)(2,1)}, u32[]{:S(2)}) copy-start(bf16[1024,7168]{1,0:T(8,128)(2,1)} %weight_ref.1) | copy-start | bytes 44040196
  17.1 4.0 %copy-start.3 = (bf16[8192]{0:T(1024)(128)(2,1)S(1)}, bf16[8192]{0:T(1024)(128)(2,1)}, u32[]{:S(2)}) copy-start(bf16[8192]{0:T(1024)(128)(2,1)} %param.11) | copy-start | bytes 49156
  21.0 12.3 %copy-start.2 = (s32[8]{0:T(128)S(1)}, s32[8]{0:T(128)}, u32[]{:S(2)}) copy-start(s32[8]{0:T(128)} %targets_ref.1) | copy-start | bytes 100
  21.0 1.2 %collective-permute-start = (f32[8,1024]{1,0:T(8,128)S(1)}, f32[8,1024]{1,0:T(8,128)S(1)}, u32[]{:S(2)}, u32[]{:S(2)}) collective-permute-start(f32[8,1024]{1,0:T(8,128)S(1)} %get-tuple-element.13), channel_id=1, source_target_pairs={{0,1},{1,0},{2,3},{3,2},{4,5},{5,4},{6,7},{7,6},{8,9},{9,8},{10,11... | collective-permute-start | bytes 98312 | tf_op jit(solution)/shard_map/ppermute | solution.py:20
  21.0 12.3 %copy-start.1 = (bf16[4096,504]{0,1:T(8,128)(2,1)S(1)}, bf16[4096,504]{0,1:T(8,128)(2,1)}, u32[]{:S(2)}) copy-start(bf16[4096,504]{0,1:T(8,128)(2,1)} %param.12) | copy-start | bytes 12386308
  22.2 11.1 %collective-permute-start.1 = (bf16[504,4096]{1,0:T(8,128)(2,1)}, bf16[504,4096]{1,0:T(8,128)(2,1)S(1)}, u32[]{:S(2)}, u32[]{:S(2)}) collective-permute-start(bf16[504,4096]{1,0:T(8,128)(2,1)} %bitcast.2), channel_id=1, source_target_pairs={{0,1},{1,0},{2,3},{3,2},{4,5},{5,4},{6,7},{7,6},{8,9},{9,8},{10,11... | collective-permute-start | bytes 12386312 | tf_op jit(solution)/shard_map/ppermute | solution.py:20

commit v14 on v13

--- a/solution.py
+++ b/solution.py
@@ -99,21 +99,24 @@
     count, rows, width = chunks_ref.shape
     half, block = kept_ref.shape
     index = lax.axis_index("mp")
+    terms = jnp.zeros((count * rows, block), jnp.float32)
+    depth = block_of(units, 1024)
+    for first in range(0, units, depth):
+        here = slice(first, first + depth)
+        for peer in range(count):
+            units_ref[peer * rows : (peer + 1) * rows, here] = chunks_ref[peer, :, here]
+        terms += lax.dot_general(
+            units_ref[:, here],
+            weight_ref[:, here],
+            ROWS_BY_ROWS,
+            preferred_element_type=jnp.float32,
+        )
     token = lax.broadcasted_iota(jnp.int32, (rows, block), 0)
     for peer in range(count):
-        units_ref[peer * rows : (peer + 1) * rows, :] = chunks_ref[peer, :, :units]
         pieces = [chunks_ref[peer, row : row + 1, units:].astype(jnp.float32) for row in range(rows)]
         residual = jnp.broadcast_to(jnp.concatenate(pieces, axis=1), (rows, block))
         own_ref[peer * rows : (peer + 1) * rows, :] = jnp.where(token == index, residual, 0.0)
-    terms = own_ref[...]
-    depth = block_of(units, 1024)
-    for first in range(0, units, depth):
-        terms += lax.dot_general(
-            units_ref[:, first : first + depth],
-            weight_ref[:, first : first + depth],
-            ROWS_BY_ROWS,
-            preferred_element_type=jnp.float32,
-        )
+    terms += own_ref[...]
     low, high = terms[:half], terms[half:]
     kept_ref[...] = jnp.where(index == 0, low, high)
     given_ref[...] = jnp.where(index == 0, high, low)

time: 45.7 us -> 45.7 us (level)
  no operation moved by 1% of the time
where the time goes in v14:
time: 45.7 us; the launch traced here: 45.4 us
  blocking collectives  35.9 us (79%)
  Pallas kernels  7.45 us (16%)
  waiting for transfers between devices  1.16 us (3%)
  other arithmetic  0.63 us (1%)
    all_to_all x3, blocking collectives, swapped(): return fence(lax.all_to_all(fence(value), 'vocab', 0, 0, tiled=True))  35.9 us
    pallas_call x4, Pallas kernels, call(): pl.pallas_call(kernel, out_shape=out_shape, in_specs=places, out_specs=ja...  7.45 us
    ppermute x2, waiting for transfers between devices, partner(): return lax.ppermute(value, 'mp', [(0, 1), (1, 0)])  1.16 us
  transfers between devices with their start and end apart: 2, of which 1 were waited for; matrix products, arithmetic and copies ran while one was open for 0% of the time, Pallas kernels for 0%

profile of v14, /device:TPU:0, one launch (start us, length us, event | category | flops | bytes accessed | tf_op | source)
XLA Modules:
  0.0 45.4 jit_solution(3084940068026146103)
XLA Ops:
  0.0 0.0 copy-start
  0.0 1.0 %shard_map.73 = bf16[8,2,7680]{2,1,0:T(2,128)(2,1)S(1)} custom-call(bf16[2,7168]{1,0:T(2,128)(2,1)} %gate_hbm.1, bf16[2,7168]{1,0:T(2,128)(2,1)} %up_hbm.1, bf16[1,8192]{1,0:T(2,128)(2,1)} %residual_hbm.1, bf16[1024,7168]{1,0:T(8,128)(2,1)} %weight_ref.1), custom_call_target="tpu_custom_call" | custom-call | tf_op jit(solution)/shard_map/pallas_call | solution.py:32
  1.0 16.0 %all_to_all.15.chunks_ref = bf16[8,2,7680]{2,1,0:T(2,128)(2,1)S(1)} all-to-all(bf16[8,2,7680]{2,1,0:T(2,128)(2,1)S(1)} %shard_map.73), channel_id=1, replica_groups=mesh['groups'=2,'vocab'=8,'mp'=2] {'vocab'}, dimensions={0} | all-to-all | bytes 491520 | tf_op jit(solution)/shard_map/all_to_all | solution.py:24
  17.1 0.0 copy-done
  17.1 0.0 copy-start.3
  17.1 3.9 %shard_map.74 = (f32[8,1024]{1,0:T(8,128)S(1)}, f32[8,1024]{1,0:T(8,128)S(1)}) custom-call(bf16[8,2,7680]{2,1,0:T(2,128)(2,1)S(1)} %all_to_all.15.chunks_ref, bf16[1024,7168]{1,0:T(8,128)(2,1)S(1)} %copy-done), custom_call_target="tpu_custom_call" | custom-call | tf_op jit(solution)/shard_map/pallas_call | solution.py:32
  21.0 0.0 copy-start.2
  21.0 0.0 collective-permute-start
  21.0 0.0 copy-done.3
  21.0 0.0 copy-start.1
  21.0 1.2 %collective-permute-done.arrived_ref = f32[8,1024]{1,0:T(8,128)S(1)} collective-permute-done((f32[8,1024]{1,0:T(8,128)S(1)}, f32[8,1024]{1,0:T(8,128)S(1)}, u32[]{:S(2)}, u32[]{:S(2)}) %collective-permute-start) | collective-permute-done | bytes 32800 | tf_op jit(solution)/shard_map/ppermute | solution.py:20
  22.2 0.2 collective-permute-start.1
  22.4 10.9 %all_to_all.16.stream_ref = bf16[8,8,1024]{2,1,0:T(8,128)(2,1)S(1)} all-to-all(bf16[8,8,1024]{2,1,0:T(8,128)(2,1)S(1)} %shard_map.75), channel_id=1, replica_groups=mesh['groups'=2,'vocab'=8,'mp'=2] {'vocab'}, dimensions={0} | all-to-all | bytes 262144 | tf_op jit(solution)/shard_map/all_to_all | solution.py:24
  33.3 0.0 collective-permute-done.1.other_ref
  33.3 0.0 copy-done.2
  33.3 0.0 copy-done.1
  33.3 2.5 %shard_map.76 = f32[8,1,24]{2,1,0:T(1,128)S(1)} custom-call(bf16[8,8,1024]{2,1,0:T(8,128)(2,1)S(1)} %all_to_all.16.stream_ref, f32[8,1024]{1,0:T(8,128)S(1)} %reshape.10.gain_ref, s32[8]{0:T(128)S(1)} %copy-done.2, bf16[504,4096]{1,0:T(8,128)(2,1)S(1)} %collective-permute-done.1.other_ref, bf16[504,4096]{1,0:T(8,128)(2,1)S(1)} %bitcast.4), custom_call_target="tpu_custom_call" | custom-call | tf_op jit(solution)/shard_map/pallas_call | solution.py:32
  35.8 9.0 %all_to_all.17 = f32[8,1,24]{2,1,0:T(1,128)S(1)} all-to-all(f32[8,1,24]{2,1,0:T(1,128)S(1)} %shard_map.76), channel_id=1, replica_groups=mesh['groups'=2,'vocab'=8,'mp'=2] {'vocab'}, dimensions={0} | all-to-all | bytes 1536 | tf_op jit(solution)/shard_map/all_to_all | solution.py:24
  44.8 0.1 slice_reduce_fusion
  44.9 0.5 %log_subtract_fusion = f32[8]{0:T(128)} fusion(f32[8]{0:T(128)S(1)} %get-tuple-element.20, f32[8]{0:T(128)S(1)} %get-tuple-element.19, f32[8]{0:T(128)S(1)} %slice_reduce_fusion.1), kind=kLoop, calls=%fused_computation.3 | loop fusion | flops 16 | bytes 128 | tf_op jit(solution)/shard_map/sub | solution.py:238
  (3 shorter events, 0.0 us)
Async XLA Ops:
  0.0 17.1 %copy-start = (bf16[1024,7168]{1,0:T(8,128)(2,1)S(1)}, bf16[1024,7168]{1,0:T(8,128)(2,1)}, u32[]{:S(2)}) copy-start(bf16[1024,7168]{1,0:T(8,128)(2,1)} %weight_ref.1) | copy-start | bytes 44040196
  17.1 4.0 %copy-start.3 = (bf16[8192]{0:T(1024)(128)(2,1)S(1)}, bf16[8192]{0:T(1024)(128)(2,1)}, u32[]{:S(2)}) copy-start(bf16[8192]{0:T(1024)(128)(2,1)} %param.11) | copy-start | bytes 49156
  21.0 12.3 %copy-start.2 = (s32[8]{0:T(128)S(1)}, s32[8]{0:T(128)}, u32[]{:S(2)}) copy-start(s32[8]{0:T(128)} %targets_ref.1) | copy-start | bytes 100
  21.0 1.2 %collective-permute-start = (f32[8,1024]{1,0:T(8,128)S(1)}, f32[8,1024]{1,0:T(8,128)S(1)}, u32[]{:S(2)}, u32[]{:S(2)}) collective-permute-start(f32[8,1024]{1,0:T(8,128)S(1)} %get-tuple-element.13), channel_id=1, source_target_pairs={{0,1},{1,0},{2,3},{3,2},{4,5},{5,4},{6,7},{7,6},{8,9},{9,8},{10,11... | collective-permute-start | bytes 98312 | tf_op jit(solution)/shard_map/ppermute | solution.py:20
  21.0 12.3 %copy-start.1 = (bf16[4096,504]{0,1:T(8,128)(2,1)S(1)}, bf16[4096,504]{0,1:T(8,128)(2,1)}, u32[]{:S(2)}) copy-start(bf16[4096,504]{0,1:T(8,128)(2,1)} %param.12) | copy-start | bytes 12386308
  22.2 11.1 %collective-permute-start.1 = (bf16[504,4096]{1,0:T(8,128)(2,1)}, bf16[504,4096]{1,0:T(8,128)(2,1)S(1)}, u32[]{:S(2)}, u32[]{:S(2)}) collective-permute-start(bf16[504,4096]{1,0:T(8,128)(2,1)} %bitcast.2), channel_id=1, source_target_pairs={{0,1},{1,0},{2,3},{3,2},{4,5},{5,4},{6,7},{7,6},{8,9},{9,8},{10,11... | collective-permute-start | bytes 12386312 | tf_op jit(solution)/shard_map/ppermute | solution.py:20

commit v15 on v13

--- a/solution.py
+++ b/solution.py
@@ -8,7 +8,7 @@
 EPSILON = 1e-05
 ROWS_BY_ROWS = (((1,), (1,)), ((), ()))
 SMALL = 2 << 20
-HEAD_PARTS = 2
+HEAD_PARTS = 4
 fence = lax.optimization_barrier
 NEAR = pl.BlockSpec(memory_space=pltpu.VMEM)
 FAR = pl.BlockSpec(memory_space=pltpu.HBM)
@@ -106,7 +106,7 @@
         residual = jnp.broadcast_to(jnp.concatenate(pieces, axis=1), (rows, block))
         own_ref[peer * rows : (peer + 1) * rows, :] = jnp.where(token == index, residual, 0.0)
     terms = own_ref[...]
-    depth = block_of(units, 1024)
+    depth = block_of(units, 1792)
     for first in range(0, units, depth):
         terms += lax.dot_general(
             units_ref[:, first : first + depth],

time: 45.7 us -> 45.7 us (level)
  no operation moved by 1% of the time
where the time goes in v15:
time: 45.7 us; the launch traced here: 45.4 us
  blocking collectives  35.9 us (79%)
  Pallas kernels  7.44 us (16%)
  waiting for transfers between devices  1.16 us (3%)
  other arithmetic  0.63 us (1%)
    all_to_all x3, blocking collectives, swapped(): return fence(lax.all_to_all(fence(value), 'vocab', 0, 0, tiled=True))  35.9 us
    pallas_call x4, Pallas kernels, call(): pl.pallas_call(kernel, out_shape=out_shape, in_specs=places, out_specs=ja...  7.44 us
    ppermute x2, waiting for transfers between devices, partner(): return lax.ppermute(value, 'mp', [(0, 1), (1, 0)])  1.16 us
  transfers between devices with their start and end apart: 2, of which 1 were waited for; matrix products, arithmetic and copies ran while one was open for 0% of the time, Pallas kernels for 0%

profile of v15, /device:TPU:0, one launch (start us, length us, event | category | flops | bytes accessed | tf_op | source)
XLA Modules:
  0.0 45.4 jit_solution(10460527349525210119)
XLA Ops:
  0.0 0.0 copy-start
  0.0 1.0 %shard_map.73 = bf16[8,2,7680]{2,1,0:T(2,128)(2,1)S(1)} custom-call(bf16[2,7168]{1,0:T(2,128)(2,1)} %gate_hbm.1, bf16[2,7168]{1,0:T(2,128)(2,1)} %up_hbm.1, bf16[1,8192]{1,0:T(2,128)(2,1)} %residual_hbm.1, bf16[1024,7168]{1,0:T(8,128)(2,1)} %weight_ref.1), custom_call_target="tpu_custom_call" | custom-call | tf_op jit(solution)/shard_map/pallas_call | solution.py:32
  1.0 16.0 %all_to_all.15.chunks_ref = bf16[8,2,7680]{2,1,0:T(2,128)(2,1)S(1)} all-to-all(bf16[8,2,7680]{2,1,0:T(2,128)(2,1)S(1)} %shard_map.73), channel_id=1, replica_groups=mesh['groups'=2,'vocab'=8,'mp'=2] {'vocab'}, dimensions={0} | all-to-all | bytes 491520 | tf_op jit(solution)/shard_map/all_to_all | solution.py:24
  17.1 0.0 copy-done
  17.1 0.0 copy-start.3
  17.1 3.9 %shard_map.74 = (f32[8,1024]{1,0:T(8,128)S(1)}, f32[8,1024]{1,0:T(8,128)S(1)}) custom-call(bf16[8,2,7680]{2,1,0:T(2,128)(2,1)S(1)} %all_to_all.15.chunks_ref, bf16[1024,7168]{1,0:T(8,128)(2,1)S(1)} %copy-done), custom_call_target="tpu_custom_call" | custom-call | tf_op jit(solution)/shard_map/pallas_call | solution.py:32
  21.0 0.0 copy-start.2
  21.0 0.0 collective-permute-start
  21.0 0.0 copy-done.3
  21.0 0.0 copy-start.1
  21.0 1.2 %collective-permute-done.arrived_ref = f32[8,1024]{1,0:T(8,128)S(1)} collective-permute-done((f32[8,1024]{1,0:T(8,128)S(1)}, f32[8,1024]{1,0:T(8,128)S(1)}, u32[]{:S(2)}, u32[]{:S(2)}) %collective-permute-start) | collective-permute-done | bytes 32800 | tf_op jit(solution)/shard_map/ppermute | solution.py:20
  22.2 0.2 collective-permute-start.1
  22.4 10.9 %all_to_all.16.stream_ref = bf16[8,8,1024]{2,1,0:T(8,128)(2,1)S(1)} all-to-all(bf16[8,8,1024]{2,1,0:T(8,128)(2,1)S(1)} %shard_map.75), channel_id=1, replica_groups=mesh['groups'=2,'vocab'=8,'mp'=2] {'vocab'}, dimensions={0} | all-to-all | bytes 262144 | tf_op jit(solution)/shard_map/all_to_all | solution.py:24
  33.3 0.0 collective-permute-done.1.other_ref
  33.3 0.0 copy-done.2
  33.3 0.0 copy-done.1
  33.3 2.5 %shard_map.76 = f32[8,1,24]{2,1,0:T(1,128)S(1)} custom-call(bf16[8,8,1024]{2,1,0:T(8,128)(2,1)S(1)} %all_to_all.16.stream_ref, f32[8,1024]{1,0:T(8,128)S(1)} %reshape.10.gain_ref, s32[8]{0:T(128)S(1)} %copy-done.2, bf16[504,4096]{1,0:T(8,128)(2,1)S(1)} %collective-permute-done.1.other_ref, bf16[504,4096]{1,0:T(8,128)(2,1)S(1)} %bitcast.4), custom_call_target="tpu_custom_call" | custom-call | tf_op jit(solution)/shard_map/pallas_call | solution.py:32
  35.8 9.0 %all_to_all.17 = f32[8,1,24]{2,1,0:T(1,128)S(1)} all-to-all(f32[8,1,24]{2,1,0:T(1,128)S(1)} %shard_map.76), channel_id=1, replica_groups=mesh['groups'=2,'vocab'=8,'mp'=2] {'vocab'}, dimensions={0} | all-to-all | bytes 1536 | tf_op jit(solution)/shard_map/all_to_all | solution.py:24
  44.8 0.1 slice_reduce_fusion
  44.9 0.5 %log_subtract_fusion = f32[8]{0:T(128)} fusion(f32[8]{0:T(128)S(1)} %get-tuple-element.20, f32[8]{0:T(128)S(1)} %get-tuple-element.19, f32[8]{0:T(128)S(1)} %slice_reduce_fusion.1), kind=kLoop, calls=%fused_computation.3 | loop fusion | flops 16 | bytes 128 | tf_op jit(solution)/shard_map/sub | solution.py:235
  (3 shorter events, 0.0 us)
Async XLA Ops:
  0.0 17.1 %copy-start = (bf16[1024,7168]{1,0:T(8,128)(2,1)S(1)}, bf16[1024,7168]{1,0:T(8,128)(2,1)}, u32[]{:S(2)}) copy-start(bf16[1024,7168]{1,0:T(8,128)(2,1)} %weight_ref.1) | copy-start | bytes 44040196
  17.1 3.9 %copy-start.3 = (bf16[8192]{0:T(1024)(128)(2,1)S(1)}, bf16[8192]{0:T(1024)(128)(2,1)}, u32[]{:S(2)}) copy-start(bf16[8192]{0:T(1024)(128)(2,1)} %param.11) | copy-start | bytes 49156
  21.0 12.3 %copy-start.2 = (s32[8]{0:T(128)S(1)}, s32[8]{0:T(128)}, u32[]{:S(2)}) copy-start(s32[8]{0:T(128)} %targets_ref.1) | copy-start | bytes 100
  21.0 1.2 %collective-permute-start = (f32[8,1024]{1,0:T(8,128)S(1)}, f32[8,1024]{1,0:T(8,128)S(1)}, u32[]{:S(2)}, u32[]{:S(2)}) collective-permute-start(f32[8,1024]{1,0:T(8,128)S(1)} %get-tuple-element.13), channel_id=1, source_target_pairs={{0,1},{1,0},{2,3},{3,2},{4,5},{5,4},{6,7},{7,6},{8,9},{9,8},{10,11... | collective-permute-start | bytes 98312 | tf_op jit(solution)/shard_map/ppermute | solution.py:20
  21.0 12.3 %copy-start.1 = (bf16[4096,504]{0,1:T(8,128)(2,1)S(1)}, bf16[4096,504]{0,1:T(8,128)(2,1)}, u32[]{:S(2)}) copy-start(bf16[4096,504]{0,1:T(8,128)(2,1)} %param.12) | copy-start | bytes 12386308
  22.2 11.1 %collective-permute-start.1 = (bf16[504,4096]{1,0:T(8,128)(2,1)}, bf16[504,4096]{1,0:T(8,128)(2,1)S(1)}, u32[]{:S(2)}, u32[]{:S(2)}) collective-permute-start(bf16[504,4096]{1,0:T(8,128)(2,1)} %bitcast.2), channel_id=1, source_target_pairs={{0,1},{1,0},{2,3},{3,2},{4,5},{5,4},{6,7},{7,6},{8,9},{9,8},{10,11... | collective-permute-start | bytes 12386312 | tf_op jit(solution)/shard_map/ppermute | solution.py:20

commit v16 on v13

--- a/solution.py
+++ b/solution.py
@@ -148,7 +148,8 @@
     mean_square = jnp.sum(squares, axis=1, keepdims=True) / (count * block)
     scale = lax.rsqrt(mean_square + EPSILON)
     for part in range(count):
-        values = stream_ref[part].astype(jnp.float32) * scale * gain_ref[part : part + 1, :]
+        gain = gain_ref[part * block : (part + 1) * block].astype(jnp.float32).reshape(1, block)
+        values = stream_ref[part].astype(jnp.float32) * scale * gain
         first = part % blocks * block
         normed_ref[part // blocks, :, first : first + block] = values.astype(jnp.bfloat16)
     index = lax.axis_index("mp")
@@ -201,6 +202,8 @@
             places + [DMA((3,))],
         )
     )
+    chunks, head_rows = fence((chunks, head_weight.T))
+    other_rows = partner(head_rows)
     part = shaped((half_tokens, block), jnp.float32)
     kept, given = call(
         down_kernel,
@@ -214,16 +217,14 @@
         grant=8 << 20,
     )
     chunk = shaped((vocab_count, half_tokens, block), jnp.bfloat16)
-    gain = norm_gain.astype(jnp.float32).reshape(vocab_count, block)
-    arrived, gain, head_rows = fence((partner(given), gain, head_weight.T))
-    other_rows = partner(head_rows)
+    arrived = partner(given)
     stream = swapped(call(stream_kernel, chunk, (kept, arrived, head_rows), [NEAR] * 2 + [FAR]))
     stream, other_rows = fence((stream, other_rows))
     row = shaped((vocab_count, 1, 3 * half_tokens), jnp.float32)
     stats = call(
         score_kernel,
         row,
-        (stream, gain, targets, other_rows, head_rows),
+        (stream, norm_gain, targets, other_rows, head_rows),
         [NEAR] * 5,
         [VECTOR((2, half_tokens, half_width), jnp.bfloat16)],
         grant=8 << 20,

time: 45.7 us -> 47.3 us (1.035)
  waiting for transfers between devices: 1.16 us -> 2.79 us
    ppermute x2, waiting for transfers between devices: 1.16 us -> 2.79 us  [partner(): return lax.ppermute(value, 'mp', [(0, 1), (1, 0)])]
  transfers between devices with their start and end apart: 2 -> 2, of which waited for: 1 -> 1; matrix products, arithmetic and copies ran while one was open for 0% -> 0% of each run, Pallas kernels for 0% -> 8%
where the time goes in v16:
time: 47.3 us; the launch traced here: 47.1 us
  blocking collectives  35.6 us (75%)
  Pallas kernels  7.45 us (16%)
  waiting for transfers between devices  2.79 us (6%)
  other arithmetic  0.63 us (1%)
  starting transfers between devices  0.57 us (1%)
    all_to_all x3, blocking collectives, swapped(): return fence(lax.all_to_all(fence(value), 'vocab', 0, 0, tiled=True))  35.6 us
    pallas_call x4, Pallas kernels, call(): pl.pallas_call(kernel, out_shape=out_shape, in_specs=places, out_specs=ja...  7.45 us
    ppermute x2, waiting for transfers between devices, partner(): return lax.ppermute(value, 'mp', [(0, 1), (1, 0)])  2.79 us
  transfers between devices with their start and end apart: 2, of which 1 were waited for; matrix products, arithmetic and copies ran while one was open for 0% of the time, Pallas kernels for 8%

profile of v16, /device:TPU:0, one launch (start us, length us, event | category | flops | bytes accessed | tf_op | source)
XLA Modules:
  0.0 47.1 jit_solution(4062337251752966662)
XLA Ops:
  0.0 0.0 copy-start
  0.0 1.0 %shard_map.73 = bf16[8,2,7680]{2,1,0:T(2,128)(2,1)S(1)} custom-call(bf16[2,7168]{1,0:T(2,128)(2,1)} %gate_hbm.1, bf16[2,7168]{1,0:T(2,128)(2,1)} %up_hbm.1, bf16[1,8192]{1,0:T(2,128)(2,1)} %residual_hbm.1, bf16[1024,7168]{1,0:T(8,128)(2,1)} %weight_ref.1), custom_call_target="tpu_custom_call" | custom-call | tf_op jit(solution)/shard_map/pallas_call | solution.py:32
  1.0 16.0 %all_to_all.15.chunks_ref = bf16[8,2,7680]{2,1,0:T(2,128)(2,1)S(1)} all-to-all(bf16[8,2,7680]{2,1,0:T(2,128)(2,1)S(1)} %shard_map.73), channel_id=1, replica_groups=mesh['groups'=2,'vocab'=8,'mp'=2] {'vocab'}, dimensions={0} | all-to-all | bytes 491520 | tf_op jit(solution)/shard_map/all_to_all | solution.py:24
  17.1 0.0 collective-permute-start.1
  17.1 0.0 copy-done
  17.1 3.9 %shard_map.74 = (f32[8,1024]{1,0:T(8,128)S(1)}, f32[8,1024]{1,0:T(8,128)S(1)}) custom-call(bf16[8,2,7680]{2,1,0:T(2,128)(2,1)S(1)} %all_to_all.15.chunks_ref, bf16[1024,7168]{1,0:T(8,128)(2,1)S(1)} %copy-done), custom_call_target="tpu_custom_call" | custom-call | tf_op jit(solution)/shard_map/pallas_call | solution.py:32
  21.0 0.0 copy-start.1
  21.0 0.0 copy-start.2
  21.0 0.0 copy-start.3
  21.0 0.6 %collective-permute-start = (f32[8,1024]{1,0:T(8,128)S(1)}, f32[8,1024]{1,0:T(8,128)S(1)}, u32[]{:S(2)}, u32[]{:S(2)}) collective-permute-start(f32[8,1024]{1,0:T(8,128)S(1)} %get-tuple-element.13), channel_id=1, source_target_pairs={{0,1},{1,0},{2,3},{3,2},{4,5},{5,4},{6,7},{7,6},{8,9},{9,8},{10,11... | collective-permute-start | bytes 98312 | tf_op jit(solution)/shard_map/ppermute | solution.py:20
  21.6 2.8 %collective-permute-done.arrived_ref = f32[8,1024]{1,0:T(8,128)S(1)} collective-permute-done((f32[8,1024]{1,0:T(8,128)S(1)}, f32[8,1024]{1,0:T(8,128)S(1)}, u32[]{:S(2)}, u32[]{:S(2)}) %collective-permute-start) | collective-permute-done | bytes 32800 | tf_op jit(solution)/shard_map/ppermute | solution.py:20
  24.4 10.6 %all_to_all.16.stream_ref = bf16[8,8,1024]{2,1,0:T(8,128)(2,1)S(1)} all-to-all(bf16[8,8,1024]{2,1,0:T(8,128)(2,1)S(1)} %shard_map.75), channel_id=1, replica_groups=mesh['groups'=2,'vocab'=8,'mp'=2] {'vocab'}, dimensions={0} | all-to-all | bytes 262144 | tf_op jit(solution)/shard_map/all_to_all | solution.py:24
  35.0 0.0 collective-permute-done.1.other_ref
  35.0 0.0 copy-done.1
  35.0 0.0 copy-done.2
  35.0 0.0 copy-done.3
  35.0 2.5 %shard_map.76 = f32[8,1,24]{2,1,0:T(1,128)S(1)} custom-call(bf16[8,8,1024]{2,1,0:T(8,128)(2,1)S(1)} %all_to_all.16.stream_ref, bf16[8192]{0:T(1024)(128)(2,1)S(1)} %copy-done.2, s32[8]{0:T(128)S(1)} %copy-done.3, bf16[504,4096]{1,0:T(8,128)(2,1)S(1)} %collective-permute-done.1.other_ref, bf16[504,4096]{1,0:T(8,128)(2,1)S(1)} %bitcast.4), custom_call_target="tpu_custom_call" | custom-call | tf_op jit(solution)/shard_map/pallas_call | solution.py:32
  37.5 9.0 %all_to_all.17 = f32[8,1,24]{2,1,0:T(1,128)S(1)} all-to-all(f32[8,1,24]{2,1,0:T(1,128)S(1)} %shard_map.76), channel_id=1, replica_groups=mesh['groups'=2,'vocab'=8,'mp'=2] {'vocab'}, dimensions={0} | all-to-all | bytes 1536 | tf_op jit(solution)/shard_map/all_to_all | solution.py:24
  46.5 0.1 slice_reduce_fusion
  46.6 0.5 %log_subtract_fusion = f32[8]{0:T(128)} fusion(f32[8]{0:T(128)S(1)} %get-tuple-element.18, f32[8]{0:T(128)S(1)} %get-tuple-element.17, f32[8]{0:T(128)S(1)} %slice_reduce_fusion.1), kind=kLoop, calls=%fused_computation.3 | loop fusion | flops 16 | bytes 128 | tf_op jit(solution)/shard_map/sub | solution.py:236
  (2 shorter events, 0.0 us)
Async XLA Ops:
  0.0 17.1 %copy-start = (bf16[1024,7168]{1,0:T(8,128)(2,1)S(1)}, bf16[1024,7168]{1,0:T(8,128)(2,1)}, u32[]{:S(2)}) copy-start(bf16[1024,7168]{1,0:T(8,128)(2,1)} %weight_ref.1) | copy-start | bytes 44040196
  17.1 18.0 %collective-permute-start.1 = (bf16[504,4096]{1,0:T(8,128)(2,1)}, bf16[504,4096]{1,0:T(8,128)(2,1)S(1)}, u32[]{:S(2)}, u32[]{:S(2)}) collective-permute-start(bf16[504,4096]{1,0:T(8,128)(2,1)} %bitcast.2), channel_id=1, source_target_pairs={{0,1},{1,0},{2,3},{3,2},{4,5},{5,4},{6,7},{7,6},{8,9},{9,8},{10,11... | collective-permute-start | bytes 12386312 | tf_op jit(solution)/shard_map/ppermute | solution.py:20
  21.0 14.0 %copy-start.1 = (bf16[4096,504]{0,1:T(8,128)(2,1)S(1)}, bf16[4096,504]{0,1:T(8,128)(2,1)}, u32[]{:S(2)}) copy-start(bf16[4096,504]{0,1:T(8,128)(2,1)} %param.12) | copy-start | bytes 12386308
  21.0 14.0 %copy-start.2 = (bf16[8192]{0:T(1024)(128)(2,1)S(1)}, bf16[8192]{0:T(1024)(128)(2,1)}, u32[]{:S(2)}) copy-start(bf16[8192]{0:T(1024)(128)(2,1)} %gain_ref.1) | copy-start | bytes 49156
  21.0 14.0 %copy-start.3 = (s32[8]{0:T(128)S(1)}, s32[8]{0:T(128)}, u32[]{:S(2)}) copy-start(s32[8]{0:T(128)} %targets_ref.1) | copy-start | bytes 100
  21.0 3.4 %collective-permute-start = (f32[8,1024]{1,0:T(8,128)S(1)}, f32[8,1024]{1,0:T(8,128)S(1)}, u32[]{:S(2)}, u32[]{:S(2)}) collective-permute-start(f32[8,1024]{1,0:T(8,128)S(1)} %get-tuple-element.13), channel_id=1, source_target_pairs={{0,1},{1,0},{2,3},{3,2},{4,5},{5,4},{6,7},{7,6},{8,9},{9,8},{10,11... | collective-permute-start | bytes 98312 | tf_op jit(solution)/shard_map/ppermute | solution.py:20
